TPU v7x, 32 devices: a whole 2x2x4 slice. The times are simulated.
32 devices in a mesh: seg: 4 (over y, core), op: 8 (over z, x).
Axes of the slice: x: 2, y: 2, z: 4, core: 2. Of those that a mesh axis runs over, the one named last changes fastest.
Arguments:
- left_ops: float32 [4, 8, 768, 768], P('seg', 'op'), as said below
- right_ops: float32 [4, 8, 768, 768], P('seg', 'op'), as said below
- wavefunction: float32 [4, 768, 768], P('seg', 'op'), as said below
- basis_rotation: float32 [4, 768, 768], P('seg'), may hold values from -0.21875 to 0.21875
- pair_term: int32 [4, 8], P('seg', 'op'), may hold values from 0 to 15
- coupling: float32 [16], replicated, may hold values from 0.1 to 1
- left_charge: int32 [4, 768], P('seg'), may hold values from 0 to 2, as said below
- right_charge: int32 [4, 768], P('seg'), may hold values from 0 to 2, as said below
Outputs:
- chebyshev: float32 [4, 768, 768], P('seg', 'op')
- energy: float32 [4], P('seg')
- handed: float32 [4, 8, 768, 768], P('seg', 'op')
Inputs may be any that keep to these rules, and one draw needn't show every extreme that they name: `left_ops`: each operator is a dominant positive diagonal plus dense full-rank off-diagonal entries. `right_ops`: each operator is a dominant positive diagonal plus dense full-rank off-diagonal entries. `wavefunction`: dense real entries of varying scale. `left_charge`: in each segment exactly 256 left bond states carry each quantum number. `right_charge`: in each segment exactly 256 right bond states carry each quantum number.
All inputs are finite; a program needn't handle non-finite values.
Results may differ from a plain program's by a relative error of at most 0.0003.
Values sent between devices are 32-bit elements; how exact they have to be, the bound alone decides.
No kernel may reach another device: no remote copies, remote signals or barrier semaphores. Data moves between devices by JAX's collectives and lax.ppermute only.
A program may use at most 128 MiB of HBM per device.

v0:
```python
import jax
import jax.numpy as jnp
from jax import lax
from jax.sharding import PartitionSpec as P

NQ = 3


HIGH = lax.Precision.HIGHEST


def passed_along(value, axis, steps):
    count = lax.axis_size(axis)
    first, last = (max(0, -steps), min(count, count - steps))
    return lax.ppermute(value, axis, [(source, source + steps) for source in range(first, last)])


def per_device(
    left_ops,
    right_ops,
    wavefunction,
    basis_rotation,
    pair_term,
    coupling,
    left_charge,
    right_charge,
):
    own_left = left_ops[0]
    own_right = right_ops[0]
    row_count = wavefunction.shape[1]
    full_size = wavefunction.shape[2]
    width = float(full_size * full_size)
    row_start = lax.axis_index("op") * row_count
    sector_mask = (left_charge[0][:, None] == right_charge[0][None, :]).astype(jnp.float32)
    table_hits = (
        pair_term[0][:, None] == jnp.arange(coupling.shape[0], dtype=jnp.int32)[None, :]
    ).astype(jnp.float32)
    coefficient = jnp.sum(table_hits * coupling[None, :], axis=1)
    gathered = lax.all_gather(wavefunction, "op", axis=1, tiled=True)[0]
    block = full_size // NQ
    pair_count = own_left.shape[0]
    left_order = jnp.argsort(left_charge[0], stable=True)
    right_order = jnp.argsort(right_charge[0], stable=True)
    left_place = jnp.argsort(left_order, stable=True)
    right_place = jnp.argsort(right_order, stable=True)
    sorted_left = jnp.take(jnp.take(own_left, left_order, axis=1), left_order, axis=2)
    sorted_right = jnp.take(jnp.take(own_right, right_order, axis=1), right_order, axis=2)
    sorted_wave = jnp.take(jnp.take(gathered, left_order, axis=0), right_order, axis=1)
    packed_wave = jnp.stack(
        [sorted_wave[q * block : (q + 1) * block, q * block : (q + 1) * block] for q in range(NQ)],
        axis=0,
    )
    initial = packed_wave / jnp.sqrt(jnp.sum(packed_wave * packed_wave) / width + 1e-06)
    left_blocks = jnp.reshape(sorted_left, (pair_count, full_size, NQ, block))
    right_blocks = jnp.reshape(sorted_right, (pair_count, full_size, NQ, block))

    def sector_apply(packed):
        first_half = jnp.einsum("kaqb,qbc->kaqc", left_blocks, packed, precision=HIGH)
        first_half = first_half * coefficient[:, None, None, None]
        first_half = jnp.reshape(first_half, (pair_count, NQ, block, full_size))
        partial_value = jnp.einsum("kobc,kcod->obd", first_half, right_blocks, precision=HIGH)
        return lax.psum(partial_value, "op")

    image_one = sector_apply(initial)
    energy = jnp.sum(initial * image_one) / width
    spread = jnp.sqrt(jnp.sum(image_one * image_one) / width + 1e-06)
    first_step = (image_one - energy * initial) / spread
    image_two = sector_apply(first_step)
    packed_result = 2.0 * (image_two - energy * first_step) / spread - initial
    flat_result = jnp.reshape(packed_result, (full_size, block))
    row_places = lax.dynamic_slice_in_dim(left_place, row_start, row_count, 0)
    row_values = jnp.take(flat_result, row_places, axis=0)
    column_index = right_place - right_charge[0] * block
    mask_rows = lax.dynamic_slice_in_dim(sector_mask, row_start, row_count, 0)
    chebyshev = jnp.take(row_values, column_index, axis=1) * mask_rows
    half_turn = jnp.einsum("kab,bj->kaj", own_left, basis_rotation[0], precision=HIGH)
    rotated = jnp.einsum("ai,kaj->kij", basis_rotation[0], half_turn, precision=HIGH)
    shifted = passed_along(rotated, "seg", 1)
    handed = jnp.where(lax.axis_index("seg") == 0, own_left, shifted)
    return (chebyshev[None], jnp.reshape(energy, (1,)), handed[None])


def solution(mesh):
    placed = (
        P("seg", "op", None, None),
        P("seg", "op", None, None),
        P("seg", "op", None),
        P("seg", None, None),
        P("seg", "op"),
        P(),
        P("seg", None),
        P("seg", None),
    )
    return jax.shard_map(
        per_device,
        mesh=mesh,
        in_specs=placed,
        out_specs=(P("seg", "op", None), P("seg"), P("seg", "op", None, None)),
        check_vma=False,
    )
```

profile of v0, /device:TPU:0, one launch (start us, length us, event | category | flops | bytes accessed | tf_op | source)
XLA Modules:
  0.0 296.8 jit_solution(15495876006412584390)
XLA Ops:
  7.2 0.7 all-gather.2.cloned.1.call-update
  8.0 0.9 copy-done
  8.8 7.6 %fusion.2 = f32[768,768]{1,0:T(8,128)S(1)} fusion(f32[1,768,768]{2,1,0:T(8,128)S(1)} %copy-done, f32[1,1,768,768]{3,2,1,0:T(8,128)} %param.12), kind=kOutput, calls=%fused_computation.12 | convolution fusion | flops 5435817984 | bytes 7077888 | tf_op jit(solution)/shard_map/kab,bj->kaj/dot_general | solution.py:76
  16.5 7.7 %fusion.11 = f32[1,768,768]{1,2,0:T(8,128)} fusion(f32[768,768]{1,0:T(8,128)S(1)} %fusion.2, f32[1,768,768]{2,1,0:T(8,128)S(1)} %copy-done), kind=kOutput, calls=%fused_computation.27 | convolution fusion | flops 5435817984 | bytes 7077888 | tf_op jit(solution)/shard_map/ai,kaj->kij/dot_general | solution.py:77
  24.2 3.8 %collective-permute-start = (f32[1,768,768]{1,2,0:T(8,128)}, f32[1,768,768]{1,2,0:T(8,128)}, u32[]{:S(2)}, u32[]{:S(2)}) collective-permute-start(f32[1,768,768]{1,2,0:T(8,128)} %fusion.11), channel_id=1, source_target_pairs={{0,8},{8,16},{16,24},{1,9},{9,17},{17,25},{2,10},{10,18},{18,26},{... | collective-permute-start | bytes 7077896 | tf_op jit(solution)/shard_map/ppermute | solution.py:15
  28.7 4.4 %sort.59 = (s32[768]{0:T(1024)}, s32[768]{0:T(1024)S(1)}) sort(s32[768]{0:T(1024)S(1)} %reduce.2, s32[768]{0:T(1024)S(1)} %iota.18), dimensions={0}, to_apply=%region_0.0 | sort | flops 7680 | bytes 12288 | tf_op jit(solution)/shard_map/jit(argsort)/sort | solution.py:43
  33.1 5.7 %gather_fusion.6 = f32[768,768]{1,0:T(8,128)} fusion(f32[768,768]{1,0:T(8,128)} %bitcast.88, s32[1024]{0:T(1024)S(1)} %pad_clamp_fusion.2), kind=kCustom, calls=%fused_computation.2.clone | custom fusion | bytes 4721664 | tf_op jit(solution)/shard_map/jit(_take)/gather | solution.py:47
  38.9 2.0 fusion.6
  40.9 2.0 copy.33
  42.9 5.9 %gather_fusion.7 = f32[768,768]{1,0:T(8,128)} fusion(f32[768,768]{0,1:T(8,128)} %copy.33, s32[1024]{0:T(1024)S(1)} %pad_clamp_fusion.2), kind=kCustom, calls=%fused_computation.3.clone | custom fusion | bytes 4721664 | tf_op jit(solution)/shard_map/jit(_take)/gather | solution.py:47
  48.8 4.4 %sort.61 = (s32[768]{0:T(1024)}, s32[768]{0:T(1024)S(1)}) sort(s32[768]{0:T(1024)S(1)} %reduce.3, s32[768]{0:T(1024)S(1)} %iota.20), dimensions={0}, to_apply=%region_2.3 | sort | flops 7680 | bytes 12288 | tf_op jit(solution)/shard_map/jit(argsort)/sort | solution.py:42
  53.1 3.5 %gather_fusion.4 = f32[768,768]{1,0:T(8,128)} fusion(f32[768,768]{1,0:T(8,128)S(1)} %bitcast.87, s32[1024]{0:T(1024)S(1)} %pad_clamp_fusion.3), kind=kCustom, calls=%fused_computation.clone | custom fusion | bytes 4721664 | tf_op jit(solution)/shard_map/jit(_take)/gather | solution.py:46
  56.6 3.3 %fusion.9 = f32[768,768]{1,0:T(8,128)} fusion(f32[768,768]{1,0:T(8,128)} %gather_fusion.4, pred[768]{0:T(1024)(128)(4,1)S(1)} %compare_and_fusion), kind=kLoop, calls=%fused_computation.21 | loop fusion | flops 589824 | bytes 4719360 | tf_op jit(solution)/shard_map/jit(_take)/Arg_0.7 | solution.py:46
  59.9 3.2 %copy.30 = f32[768,768]{0,1:T(8,128)} copy(f32[768,768]{1,0:T(8,128)} %fusion.9) | data formatting | bytes 4718592 | tf_op jit(solution)/shard_map/jit(_take)/Arg_0.7 | solution.py:46
  63.1 5.8 %gather_fusion.5 = f32[768,768]{1,0:T(8,128)} fusion(f32[768,768]{0,1:T(8,128)} %copy.30, s32[1024]{0:T(1024)S(1)} %pad_clamp_fusion.3), kind=kCustom, calls=%fused_computation.1.clone | custom fusion | bytes 4721664 | tf_op jit(solution)/shard_map/jit(_take)/gather | solution.py:46
  68.9 0.6 fusion.16
  69.4 3.5 %bitcast_select_fusion = f32[1,768,768]{1,2,0:T(8,128)} fusion(f32[768,768]{1,0:T(8,128)} %gather_fusion.7, pred[768]{0:T(1024)(128)(4,1)S(1)} %compare_and_fusion.1), kind=kLoop, calls=%fused_computation.8 | loop fusion | flops 589824 | bytes 4719360 | tf_op jit(solution)/shard_map/jit(_take)/select_n | solution.py:47
  72.9 1.7 bitcast_select_fusion.1
  74.6 5.8 %gather_fusion = f32[768,768]{1,0:T(8,128)} fusion(f32[768,768]{1,0:T(8,128)} %bitcast.89, s32[1024]{0:T(1024)S(1)} %pad_clamp_fusion.3), kind=kCustom, calls=%fused_computation.4 | custom fusion | bytes 4721664 | tf_op jit(solution)/shard_map/jit(_take)/gather | solution.py:48
  80.3 3.3 %broadcast_select_fusion = f32[768,768]{1,0:T(8,128)} fusion(f32[768,768]{1,0:T(8,128)} %gather_fusion, pred[768]{0:T(1024)(128)(4,1)S(1)} %compare_and_fusion), kind=kLoop, calls=%fused_computation.28 | loop fusion | flops 589824 | bytes 4719360 | tf_op jit(solution)/shard_map/jit(_take)/select_n | solution.py:48
  83.6 3.1 %copy.27 = f32[768,768]{0,1:T(8,128)} copy(f32[768,768]{1,0:T(8,128)} %broadcast_select_fusion) | data formatting | bytes 4718592 | tf_op jit(solution)/shard_map/jit(_take)/select_n | solution.py:48
  86.7 5.8 %gather_fusion.1 = f32[768,768]{1,0:T(8,128)} fusion(f32[768,768]{0,1:T(8,128)} %copy.27, s32[1024]{0:T(1024)S(1)} %pad_clamp_fusion.2), kind=kCustom, calls=%fused_computation.5 | custom fusion | bytes 4721664 | tf_op jit(solution)/shard_map/jit(_take)/gather | solution.py:48
  92.5 1.9 select_bitcast_fusion
  94.5 0.8 multiply_reduce_fusion.2
  96.0 5.7 %multiply_bitcast_fusion.1 = f32[1,768,3,256]{1,3,2,0:T(8,128)} fusion(f32[768,3,256]{0,2,1:T(8,128)} %bitcast.92, f32[]{:T(128)} %fusion.16, f32[1,256,256]{1,2,0:T(8,128)S(1)} %get-tuple-element.26, f32[1,256,256]{1,2,0:T(8,128)S(1)} %get-tuple-element.27, f32[1,256,256]{1,2,0:T(8,128)S(1)} %get-tuple-element.25, f32[]{:T(128)S(6)} %sqrt.6), kind=kOutput, calls=%fused_computation.26 | convolution fusion | flops 1813118976 | bytes 5505032 | tf_op jit(solution)/shard_map/kaqb,qbc->kaqc/dot_general | solution.py:58
  101.7 4.5 %reshape.248 = f32[3,256,768]{1,0,2:T(4,128)} reshape(f32[1,768,3,256]{1,3,2,0:T(8,128)} %multiply_bitcast_fusion.1) | data formatting | bytes 4718592 | tf_op jit(solution)/shard_map/reshape.19
  106.2 6.2 %fusion.7 = f32[3,256,256]{1,2,0:T(8,128)} fusion(f32[768,3,256]{0,2,1:T(8,128)} %bitcast.90, f32[3,256,768]{1,0,2:T(4,128)} %reshape.248), kind=kOutput, calls=%fused_computation.18 | convolution fusion | flops 1811939328 | bytes 5505024 | tf_op jit(solution)/shard_map/kobc,kcod->obd/dot_general | solution.py:61
  112.5 4.4 %sort.62 = (s32[768]{0:T(1024)}, s32[768]{0:T(1024)S(1)}) sort(s32[768]{0:T(1024)S(1)} %get-tuple-element.11, s32[768]{0:T(1024)S(1)} %iota.21), dimensions={0}, to_apply=%region_3.4 | sort | flops 7680 | bytes 12288 | tf_op jit(solution)/shard_map/jit(argsort)/sort | solution.py:44
  116.9 0.1 compare_and_fusion.3
  116.9 72.0 %all-reduce.3.cloned.1.call-done = f32[3,256,256]{1,2,0:T(8,128)} async-done(((f32[3,256,256]{1,2,0:T(8,128)}), f32[3,256,256]{1,2,0:T(8,128)}) %all-reduce.3.cloned.1.call-update) | async-done | bytes 786448 | tf_op jit(solution)/shard_map/psum | solution.py:62
  189.0 1.9 multiply_reduce_fusion.1
  192.2 6.1 %multiply_bitcast_fusion = f32[1,768,3,256]{1,3,2,0:T(8,128)} fusion(f32[768,3,256]{0,2,1:T(8,128)} %bitcast.93, f32[]{:T(128)} %fusion.16, f32[3,256,256]{1,2,0:T(8,128)} %all-reduce.3.cloned.1.call-done, f32[]{:T(128)S(6)} %sqrt.7, f32[]{:T(128)} %div.28, f32[1,256,256]{1,2,0:T(8,128)S(1)} %get-tuple-element.26, ...), kind=kOutput, calls=%fused_computation.25 | convolution fusion | flops 1813708800 | bytes 6291472 | tf_op jit(solution)/shard_map/kaqb,qbc->kaqc/dot_general | solution.py:58
  198.4 4.6 %reshape.249 = f32[3,256,768]{1,0,2:T(4,128)} reshape(f32[1,768,3,256]{1,3,2,0:T(8,128)} %multiply_bitcast_fusion) | data formatting | bytes 4718592 | tf_op jit(solution)/shard_map/reshape.23
  203.0 6.2 %fusion.4 = f32[3,256,256]{1,2,0:T(8,128)} fusion(f32[768,3,256]{0,2,1:T(8,128)} %bitcast.91, f32[3,256,768]{1,0,2:T(4,128)} %reshape.249), kind=kOutput, calls=%fused_computation.14 | convolution fusion | flops 1811939328 | bytes 5505024 | tf_op jit(solution)/shard_map/kobc,kcod->obd/dot_general | solution.py:61
  209.2 0.1 dynamic-slice
  209.3 1.9 copy.28
  211.2 4.4 %sort.60 = (s32[768]{0:T(1024)}, s32[768]{0:T(1024)S(1)}) sort(s32[768]{0:T(1024)S(1)} %get-tuple-element.9, s32[768]{0:T(1024)S(1)} %iota.19), dimensions={0}, to_apply=%region_1.0 | sort | flops 7680 | bytes 12288 | tf_op jit(solution)/shard_map/jit(argsort)/sort | solution.py:45
  215.6 2.0 fusion.10
  217.6 2.0 copy.43
  219.5 64.1 %all-reduce.5.cloned.1.call-done = f32[3,256,256]{1,2,0:T(8,128)} async-done(((f32[3,256,256]{1,2,0:T(8,128)}), f32[3,256,256]{1,2,0:T(8,128)}) %all-reduce.5.cloned.1.call-update) | async-done | bytes 786448 | tf_op jit(solution)/shard_map/psum | solution.py:62
  283.7 1.6 divide_subtract_fusion
  285.3 0.3 copy.40
  285.6 0.7 gather_fusion.2
  286.3 0.1 broadcast_select_fusion.1
  286.4 0.1 copy.41
  286.5 1.6 gather_fusion.3
  288.0 0.3 fusion.15
  288.3 0.9 copy.42
  (36 shorter events, 0.4 us)
Async XLA Ops:
  7.2 1.7 copy-start
  7.2 67.4 %all-gather.2.cloned.1.call-start = ((), (), s32[]{:S(2)}) async-start(), calls=%async_computation | async-start | bytes 2654208 | tf_op jit(solution)/shard_map/all_gather | solution.py:39
  7.9 181.0 %all-reduce.3.cloned.1.call-start = ((), (), s32[]{:S(2)}) async-start(), calls=%async_computation.1 | async-start | bytes 1572864 | tf_op jit(solution)/shard_map/psum | solution.py:62
  16.5 12.2 %copy-start.4 = (s32[1,768]{1,0:T(1,128)S(1)}, s32[1,768]{1,0:T(1,128)}, u32[]{:S(2)}) copy-start(s32[1,768]{1,0:T(1,128)} %param.19) | copy-start | bytes 9220
  16.5 12.2 %copy-start.5 = (s32[1,768]{1,0:T(1,128)S(1)}, s32[1,768]{1,0:T(1,128)}, u32[]{:S(2)}) copy-start(s32[1,768]{1,0:T(1,128)} %param.18) | copy-start | bytes 9220
  24.2 191.4 %collective-permute-start = (f32[1,768,768]{1,2,0:T(8,128)}, f32[1,768,768]{1,2,0:T(8,128)}, u32[]{:S(2)}, u32[]{:S(2)}) collective-permute-start(f32[1,768,768]{1,2,0:T(8,128)} %fusion.11), channel_id=1, source_target_pairs={{0,8},{8,16},{16,24},{1,9},{9,17},{17,25},{2,10},{10,18},{18,26},{... | collective-permute-start | bytes 7077896 | tf_op jit(solution)/shard_map/ppermute | solution.py:15
  42.9 10.3 %copy-start.2 = (f32[1,1,768,768]{3,2,1,0:T(8,128)S(1)}, f32[1,1,768,768]{3,2,1,0:T(8,128)}, u32[]{:S(2)}) copy-start(f32[1,1,768,768]{3,2,1,0:T(8,128)} %param.12) | copy-start | bytes 7077892
  63.1 5.8 %copy-start.6 = (f32[16]{0:T(128)S(1)}, f32[16]{0:T(128)}, u32[]{:S(2)}) copy-start(f32[16]{0:T(128)} %param.17) | copy-start | bytes 196
  69.4 3.5 %copy-start.3 = (f32[768,768]{1,0:T(8,128)S(1)}, f32[768,768]{1,0:T(8,128)}, u32[]{:S(2)}) copy-start(f32[768,768]{1,0:T(8,128)} %gather_fusion.5) | copy-start | bytes 7077892
  112.4 171.2 %all-reduce.5.cloned.1.call-start = ((), (), s32[]{:S(2)}) async-start(), calls=%async_computation.2 | async-start | bytes 1572864 | tf_op jit(solution)/shard_map/psum | solution.py:62
  285.6 3.6 %copy-start.1 = (f32[1,768,768]{2,1,0:T(8,128)S(1)}, f32[1,768,768]{2,1,0:T(8,128)}, u32[]{:S(2)}) copy-start(f32[1,768,768]{2,1,0:T(8,128)} %param.15) | copy-start | bytes 7077892
Sparse Core Ops, SparseCore 0:
  10.2 54.4 all-gather.1
  112.5 76.3 all-reduce.2
  209.3 74.3 all-reduce.4
where the time goes:
time: 298 us; the launch traced here: 297 us
  waiting for transfers between devices  137 us (46%)
  local copies, waits for them, and re-layouts  58.2 us (20%)
  other arithmetic  40.5 us (14%)
  matrix products  39.6 us (13%)
  between operations  17.8 us (6%)
  starting transfers between devices  3.9 us (1%)
    psum x2, waiting for transfers between devices, sector_apply(): return lax.psum(partial_value, 'op')  136 us
    dot_general x2, matrix products, sector_apply(): jnp.einsum('kobc,kcod->obd', first_half, right_blocks, precision=HIGH)  12.3 us
    dot_general x2, matrix products, sector_apply(): jnp.einsum('kaqb,qbc->kaqc', left_blocks, packed, precision=HIGH)  11.9 us
    another operation x2, local copies, waits for them, and re-layouts  9.16 us
    dot_general x1, matrix products, per_device(): jnp.einsum('ai,kaj->kij', basis_rotation[0], half_turn, precision=HIGH)  7.73 us
    dot_general x1, matrix products, per_device(): jnp.einsum('kab,bj->kaj', own_left, basis_rotation[0], precision=HIGH)  7.65 us
  transfers between devices with their start and end apart: 4, of which 2 were waited for; matrix products, arithmetic and copies ran while one was open for 44% of the time, Pallas kernels for 0%

commit v1 on v0

v1 whole, which is shorter than its diff:
```python
import functools

import jax
import jax.numpy as jnp
from jax import lax
from jax.experimental import pallas as pl
from jax.experimental.pallas import tpu as pltpu
from jax.sharding import PartitionSpec as P


NQ = 3
F32 = jnp.float32
BF16 = jnp.bfloat16
LANES = 128


VMEM = pl.BlockSpec(memory_space=pltpu.VMEM)
SMEM = pl.BlockSpec(memory_space=pltpu.SMEM)
HBM = pl.BlockSpec(memory_space=pltpu.HBM)
LIMIT = pltpu.CompilerParams(vmem_limit_bytes=16 << 20)
SMALL = pltpu.CompilerParams(vmem_limit_bytes=4 << 20)


def mm(a, b):
    return lax.dot_general(a, b, (((1,), (0,)), ((), ())), preferred_element_type=F32)


def split(x):
    high = x.astype(BF16)
    return high, (x - high.astype(F32)).astype(BF16)


def mm3(ah, al, bh, bl):
    return mm(ah, bh) + (mm(ah, bl) + mm(al, bh))


def places_of(charge, block):
    size = charge.shape[1]
    own = (lax.broadcasted_iota(jnp.int32, (16, size), 0) == charge).astype(F32)
    earlier = lax.broadcasted_iota(jnp.int32, (LANES, LANES), 0) < lax.broadcasted_iota(jnp.int32, (LANES, LANES), 1)
    earlier = earlier.astype(F32).astype(BF16)
    before = jnp.zeros((16, 1), F32)
    ranks = []
    for c in range(size // LANES):
        part = own[:, c * LANES : (c + 1) * LANES]
        counts = mm(part.astype(BF16), earlier) + before
        ranks.append(jnp.sum(part * counts, axis=0, keepdims=True))
        before = before + jnp.sum(part, axis=1, keepdims=True)
    return jnp.concatenate(ranks, axis=1) + (charge * block).astype(F32)


def chosen(places, positions):
    return jnp.where(places.astype(BF16) == positions, jnp.ones((), BF16), jnp.zeros((), BF16))


def sorter(place_row):
    size = place_row.shape[1]
    step = 2 * LANES
    place = lax.broadcasted_iota(jnp.int32, (step, size), 0).astype(F32).astype(BF16)
    row = jnp.broadcast_to(place_row, (step, size))
    return jnp.concatenate([chosen(row - float(c), place) for c in range(0, size, step)], axis=0)


def column(row):
    return jnp.transpose(jnp.broadcast_to(row, (LANES, row.shape[1])))


def unsorter(place_column, size):
    lane = lax.broadcasted_iota(jnp.int32, place_column.shape, 1).astype(F32).astype(BF16)
    return jnp.concatenate([chosen(place_column - float(c), lane) for c in range(0, size, LANES)], axis=1)


def pack_kernel(
    me_ref, left_hbm, right_hbm, wave_hbm, packed_ref, column_ref, left_ref, right_ref, wave_ref, arrived
):
    rows, size = wave_ref.shape
    block = size // NQ
    copies = [
        pltpu.make_async_copy(source, target, arrived.at[i])
        for i, (source, target) in enumerate(
            ((right_hbm, right_ref), (left_hbm, left_ref), (wave_hbm, wave_ref))
        )
    ]
    for copy in copies:
        copy.start()
    for copy in copies:
        copy.wait()
    back = unsorter(column(places_of(right_ref[...], block)), size)
    column_ref[...] = column(left_ref[...].astype(F32))
    start = pl.multiple_of(me_ref[0] * rows, 8)
    charge = column_ref[pl.ds(start, rows), :][:, :1]
    wave = wave_ref[...]
    first, _ = split(wave)
    second, third = split(wave - first.astype(F32))
    ordered = mm(first, back) + (mm(second, back) + mm(third, back))
    packed = jnp.zeros((rows, block), F32)
    for q in range(NQ):
        packed = packed + jnp.where(charge == float(q), ordered[:, q * block : (q + 1) * block], 0.0)
    packed_ref[...] = packed


def columns_kernel(charge_ref, ops_ref, half_high, half_low, onto, back, column_ref):
    rows, size = ops_ref.shape
    step = pl.program_id(0)

    @pl.when(step == 0)
    def _():
        place = places_of(charge_ref[...], size // NQ)
        column_ref[...] = column(place)
        onto[...] = sorter(place)
        back[...] = unsorter(column_ref[...], size)

    high, low = split(ops_ref[...])
    here = pl.ds(pl.multiple_of(step * rows, rows), rows)
    half_high[here, :] = mm(high, back[...]).astype(BF16)
    half_low[here, :] = mm(low, back[...]).astype(BF16)


def sort_kernel(
    charge_ref,
    left_half_high,
    left_half_low,
    left_onto,
    ops_ref,
    left_high,
    left_low,
    right_high,
    right_low,
    place_ref,
    onto,
    back,
    half_high,
    half_low,
):
    rows, size = ops_ref.shape
    step = pl.program_id(0)

    @pl.when(step == 0)
    def _():
        place = places_of(charge_ref[...], size // NQ)
        place_ref[...] = jnp.broadcast_to(place, place_ref.shape)
        onto[...] = sorter(place)
        back[...] = unsorter(column(place), size)

    here = pl.ds(pl.multiple_of(step * rows, rows), rows)
    left_high[here, :] = mm(left_onto[here, :], left_half_high[...]).astype(BF16)
    left_low[here, :] = mm(left_onto[here, :], left_half_low[...]).astype(BF16)
    high, low = split(ops_ref[...])
    half_high[here, :] = mm(high, back[...]).astype(BF16)
    half_low[here, :] = mm(low, back[...]).astype(BF16)

    @pl.when(step == pl.num_programs(0) - 1)
    def _():
        for q in range(NQ):
            there = slice(q * rows, (q + 1) * rows)
            right_high[there, :] = mm(onto[there, :], half_high[...]).astype(BF16)
            right_low[there, :] = mm(onto[there, :], half_low[...]).astype(BF16)


def sort_columns(charge, ops):
    size = ops.shape[0]
    rows = size // NQ
    return pl.pallas_call(
        columns_kernel,
        grid=(NQ,),
        in_specs=[VMEM, pl.BlockSpec((rows, size), lambda i: (i, 0))],
        out_specs=[VMEM] * 5,
        out_shape=[pltpu.VMEM((size, size), BF16)] * 4 + [pltpu.VMEM((size, LANES), F32)],
        compiler_params=LIMIT,
    )(far(charge), far(ops))


def sort_rest(charge, left_half_high, left_half_low, left_onto, ops):
    size = ops.shape[0]
    rows = size // NQ
    return pl.pallas_call(
        sort_kernel,
        grid=(NQ,),
        in_specs=[VMEM] * 4 + [pl.BlockSpec((rows, size), lambda i: (i, 0))],
        out_specs=[VMEM] * 5,
        out_shape=[pltpu.VMEM((size, size), BF16)] * 4 + [jax.ShapeDtypeStruct((8, size), F32)],
        scratch_shapes=[pltpu.VMEM((size, size), BF16) for _ in range(4)],
        compiler_params=LIMIT,
    )(far(charge), left_half_high, left_half_low, left_onto, far(ops))


def apply_blocks(packed, scale, left_high, left_low, right_high, right_low, half_high, half_low, total):
    block = packed.shape[1]
    for q in range(NQ):
        here = slice(q * block, (q + 1) * block)
        high, low = split(packed[here, :])
        value = mm3(left_high[:, here], left_low[:, here], high, low) * scale
        half_high[:, here], half_low[:, here] = split(value)
    for q in range(NQ):
        here = slice(q * block, (q + 1) * block)
        total[here, :] = mm3(half_high[here, :], half_low[here, :], right_high[:, here], right_low[:, here])


def first_kernel(group, me_ref, term_ref, table_ref, onto_ref, *refs):
    parts = refs[:group]
    left_high, left_low, right_high, right_low = refs[group : group + 4]
    initial_ref, initial_rows_ref = refs[group + 4 : group + 6]
    outs = refs[group + 6 : 2 * group + 6]
    half_high, half_low, total = refs[2 * group + 6 :]
    half = lax.div(me_ref[0], group)
    own = lax.rem(me_ref[0], group)
    pair, block = parts[0].shape
    rows = pair // 2
    size = pair * group
    for s in range(group):
        for h, side in enumerate((half, 1 - half)):
            start = pl.multiple_of((side * group + (own ^ s)) * rows, 8)
            total[pl.ds(start, rows), :] = parts[s][h * rows : (h + 1) * rows, :]
    high, low = split(total[...])
    packed = mm(onto_ref[...], high) + mm(onto_ref[...], low)
    norm = jnp.sqrt(jnp.sum(packed * packed, keepdims=True) / float(size * size) + 1e-06)
    initial_ref[...] = packed / norm
    initial_rows_ref[...] = parts[0][:rows, :] / norm
    scale = table_ref[term_ref[0, 0]]
    apply_blocks(
        initial_ref[...], scale, left_high, left_low, right_high, right_low, half_high, half_low, total
    )
    each = block // group
    for s in range(group):
        for q in range(NQ):
            start = pl.multiple_of(q * block + (own ^ s) * each, 8)
            outs[s][q * each : (q + 1) * each, :] = total[pl.ds(start, each), :]


def second_kernel(group, me_ref, term_ref, table_ref, back_ref, column_ref, *refs):
    parts = refs[:group]
    initial_ref, left_high, left_low, right_high, right_low = refs[group : group + 5]
    energy_ref, spread_ref, step_rows_ref, spot_ref = refs[group + 5 : group + 9]
    outs = refs[group + 9 : 2 * group + 9]
    half_high, half_low, total, step_ref = refs[2 * group + 9 :]
    half = lax.div(me_ref[0], group)
    own = lax.rem(me_ref[0], group)
    pair, block = parts[0].shape
    rows = pair // 2
    size = pair * group
    each = block // group
    for s in range(group):
        for q in range(NQ):
            start = pl.multiple_of(q * block + (own ^ s) * each, 8)
            total[pl.ds(start, each), :] = parts[s][q * each : (q + 1) * each, :]
    width = float(size * size)
    energy = jnp.sum(initial_ref[...] * total[...], keepdims=True) / width
    spread = jnp.sqrt(jnp.sum(total[...] * total[...], keepdims=True) / width + 1e-06)
    step_ref[...] = (total[...] - energy * initial_ref[...]) / spread
    energy_ref[...] = energy
    spread_ref[...] = spread
    scale = table_ref[term_ref[0, 0]]
    apply_blocks(
        step_ref[...], scale, left_high, left_low, right_high, right_low, half_high, half_low, total
    )
    high, low = split(total[...])
    total[...] = mm(back_ref[...], high) + mm(back_ref[...], low)
    start = pl.multiple_of(me_ref[0] * rows, 8)
    spot_ref[...] = column_ref[pl.ds(start, rows), :]
    back = unsorter(spot_ref[...], size)
    high, low = split(step_ref[...])
    step_rows_ref[...] = mm(back, high) + mm(back, low)
    for s in range(group):
        for h, side in enumerate((half, 1 - half)):
            start = pl.multiple_of((side * group + (own ^ s)) * rows, 8)
            outs[s][h * rows : (h + 1) * rows, :] = total[pl.ds(start, rows), :]


def last_kernel(spot_ref, place_ref, energy_ref, spread_ref, initial_ref, step_ref, kept_ref, sent_ref, out_ref):
    image = kept_ref[...] + sent_ref[...]
    packed = 2.0 * (image - energy_ref[...] * step_ref[...]) / spread_ref[...] - initial_ref[...]
    block = packed.shape[1]
    spot = jnp.broadcast_to(spot_ref[...][:, :1], packed.shape)
    held = [(spot >= float(q * block)) & (spot < float((q + 1) * block)) for q in range(NQ)]
    onto = sorter(place_ref[...][:1, :])
    high = packed.astype(BF16).astype(F32)
    out = jnp.zeros(out_ref.shape, F32)
    for piece in (high, packed - high):
        wide = jnp.concatenate([jnp.where(here, piece, 0.0) for here in held], axis=1)
        out = out + mm(wide.astype(BF16), onto)
    out_ref[...] = out


def join_kernel(first_ref, second_ref, out_ref):
    rows = first_ref.shape[0]
    out_ref[:rows, :] = first_ref[...]
    out_ref[rows:, :] = second_ref[...]


def sum_kernel(*refs):
    parts = [ref for ref in refs if ref.shape == refs[0].shape]
    outs = refs[len(parts) :]
    if not outs:
        parts, outs = parts[:-1], parts[-1:]
    start = 0
    for out in outs:
        here = slice(start, start + out.shape[0])
        start += out.shape[0]
        value = parts[0][here, :]
        for part in parts[1:]:
            value = value + part[here, :]
        out[...] = value


def choose_kernel(segment_ref, own_ref, shifted_ref, out_ref, held, arrived, left):
    rows = own_ref.shape[0] // NQ
    parts = [slice(q * rows, (q + 1) * rows) for q in range(NQ)]
    outs = [pltpu.make_async_copy(held.at[p], out_ref.at[p], left.at[q]) for q, p in enumerate(parts)]

    def through(source):
        ins = [pltpu.make_async_copy(source.at[p], held.at[p], arrived.at[q]) for q, p in enumerate(parts)]
        for copy in ins:
            copy.start()
        for come, go in zip(ins, outs):
            come.wait()
            go.start()

    pl.when(segment_ref[0] == 0)(lambda: through(own_ref))
    pl.when(segment_ref[0] != 0)(lambda: through(shifted_ref))
    for copy in outs:
        copy.wait()


def passed_along(value, axis, steps):
    count = lax.axis_size(axis)
    first, last = (max(0, -steps), min(count, count - steps))
    return lax.ppermute(value, axis, [(source, source + steps) for source in range(first, last)])


def near(value):
    return pltpu.with_memory_space_constraint(value, pltpu.VMEM)


def far(value):
    return pltpu.with_memory_space_constraint(value, pltpu.HBM)


def swapped(value, axis, mask):
    count = lax.axis_size(axis)
    return near(lax.ppermute(value, axis, [(source, source ^ mask) for source in range(count)]))


def call(kernel, ins, outs, scratch, *operands, params=SMALL):
    return pl.pallas_call(
        kernel,
        in_specs=ins,
        out_specs=[VMEM] * len(outs),
        out_shape=outs,
        scratch_shapes=scratch,
        compiler_params=params,
    )(*operands)


def summed(heights, *parts):
    outs = [pltpu.VMEM((h,) + parts[0].shape[1:], F32) for h in heights]
    return call(sum_kernel, [VMEM] * len(parts), outs, [], *parts)


def all_steps(
    left_ops,
    right_ops,
    wavefunction,
    basis_rotation,
    pair_term,
    coupling,
    left_charge,
    right_charge,
):
    own_left = left_ops[0, 0]
    own_right = right_ops[0, 0]
    rows, size = wavefunction.shape[1:]
    block = size // NQ
    count = lax.axis_size("op")
    group = count // 2
    me = jnp.reshape(lax.axis_index("op").astype(jnp.int32), (1,))

    (packed,) = call(
        pack_kernel,
        [SMEM, HBM, HBM, HBM],
        [pltpu.VMEM((rows, block), F32)],
        [
            pltpu.VMEM((size, LANES), F32),
            pltpu.VMEM((1, size), jnp.int32),
            pltpu.VMEM((1, size), jnp.int32),
            pltpu.VMEM((rows, size), F32),
            pltpu.SemaphoreType.DMA((3,)),
        ],
        me,
        far(left_charge),
        far(right_charge),
        far(wavefunction[0]),
    )
    (pair,) = call(
        join_kernel, [VMEM] * 2, [pltpu.VMEM((2 * rows, block), F32)], [], packed, swapped(packed, "op", group)
    )
    gathered = [pair] + [swapped(pair, "op", s) for s in range(1, group)]

    left_half_high, left_half_low, onto, back, left_column = sort_columns(left_charge, own_left)
    left_high, left_low, right_high, right_low, right_place = sort_rest(
        right_charge, left_half_high, left_half_low, onto, own_right
    )
    pieces = (left_high, left_low, right_high, right_low)
    halves = [pltpu.VMEM((size, size), BF16), pltpu.VMEM((size, size), BF16), pltpu.VMEM((size, block), F32)]
    pairs = [pltpu.VMEM((2 * rows, block), F32)] * group

    initial, initial_rows, *sent = call(
        functools.partial(first_kernel, group),
        [SMEM, SMEM, SMEM] + [VMEM] * (group + 5),
        [pltpu.VMEM((size, block), F32), pltpu.VMEM((rows, block), F32)] + pairs,
        halves,
        me,
        pair_term,
        coupling,
        onto,
        *gathered,
        *pieces,
        params=LIMIT,
    )
    total = summed([2 * rows], sent[0], *[swapped(sent[s], "op", s) for s in range(group - 1, 0, -1)])[0]
    total = summed([2 * rows], total, swapped(total, "op", group))[0]
    gathered = [total] + [swapped(total, "op", s) for s in range(group - 1, 0, -1)][::-1]

    energy, spread, step_rows, spot, *sent = call(
        functools.partial(second_kernel, group),
        [SMEM, SMEM, SMEM] + [VMEM] * (group + 7),
        [
            pltpu.VMEM((1, 1), F32),
            pltpu.VMEM((1, 1), F32),
            pltpu.VMEM((rows, block), F32),
            pltpu.VMEM((rows, LANES), F32),
        ]
        + pairs,
        halves + [pltpu.VMEM((size, block), F32)],
        me,
        pair_term,
        coupling,
        back,
        near(left_column),
        *gathered,
        initial,
        *pieces,
        params=LIMIT,
    )
    kept, away = summed([rows, rows], near(sent[0]), *[swapped(sent[s], "op", s) for s in range(group - 1, 0, -1)])
    received = swapped(away, "op", group)
    (chebyshev,) = call(
        last_kernel,
        [VMEM] * 8,
        [jax.ShapeDtypeStruct((rows, size), F32)],
        [],
        near(spot),
        right_place,
        near(energy),
        near(spread),
        near(initial_rows),
        near(step_rows),
        near(kept),
        received,
    )

    turned_left, _ = lax.optimization_barrier((own_left, initial))
    half_turn = jnp.dot(turned_left, basis_rotation[0], precision=lax.Precision.HIGH)
    rotated = lax.dot_general(
        basis_rotation[0], half_turn, (((0,), (0,)), ((), ())), precision=lax.Precision.HIGH
    )
    shifted = passed_along(far(rotated), "seg", 1)
    segment = jnp.reshape(lax.axis_index("seg").astype(jnp.int32), (1,))
    handed = pl.pallas_call(
        choose_kernel,
        in_specs=[SMEM, HBM, HBM],
        out_specs=HBM,
        out_shape=jax.ShapeDtypeStruct((size, size), F32),
        scratch_shapes=[pltpu.VMEM((size, size), F32), pltpu.SemaphoreType.DMA((NQ,)), pltpu.SemaphoreType.DMA((NQ,))],
        compiler_params=SMALL,
    )(segment, far(own_left), far(shifted))[None, None]
    return (chebyshev[None], energy[0], handed)


def solution(mesh):
    placed = (
        P("seg", "op", None, None),
        P("seg", "op", None, None),
        P("seg", "op", None),
        P("seg", None, None),
        P("seg", "op"),
        P(),
        P("seg", None),
        P("seg", None),
    )
    return jax.shard_map(
        all_steps,
        mesh=mesh,
        in_specs=placed,
        out_specs=(P("seg", "op", None), P("seg"), P("seg", "op", None, None)),
        check_vma=False,
    )
```

time: 298 us -> 111 us (0.37)
  waiting for transfers between devices: 137 us -> 45.2 us
  local copies, waits for them, and re-layouts: 58.2 us -> 0.02 us
  other arithmetic: 40.5 us -> 0 us
  matrix products: 39.6 us -> 7.81 us
  Pallas kernels: 0 us -> 29.1 us
  starting transfers between devices: 3.9 us -> 26 us
  between operations: 17.8 us -> 2.6 us
    psum x2 -> x0, waiting for transfers between devices: 136 us -> none  [sector_apply(): return lax.psum(partial_value, 'op')]
    ppermute x0 -> x15, waiting for transfers between devices: none -> 45.2 us  [swapped(): lax.ppermute(value, axis, [(source, source ^ mask) for source in range(co...]
    gather x8 -> x0, local copies, waits for them, and re-layouts: 34.7 us -> none  [the longest x1 5.9 us: per_device(): jnp.take(jnp.take(own_right, right_order, axis=1), right_order, axis=2)]
    dot_general x6 -> x2, matrix products: 39.6 us -> 7.81 us  [the longest x1 4.71 us: all_steps(): lax.dot_general(basis_rotation[0], half_turn, (((0,), (0,)), ((), ())), p...]
    pallas_call x0 -> x11, Pallas kernels: none -> 29.1 us  [the longest x8 14 us: call(): pl.pallas_call(kernel, in_specs=ins, out_specs=[VMEM] * len(outs), out_sh...]
    ppermute x0 -> x15, starting transfers between devices: none -> 23.3 us  [swapped(): lax.ppermute(value, axis, [(source, source ^ mask) for source in range(co...]
    sort x4 -> x0, other arithmetic: 17.5 us -> none  [the longest x1 4.37 us: per_device(): right_place = jnp.argsort(right_order, stable=True)]
    another operation x5 -> x0, local copies, waits for them, and re-layouts: 14.3 us -> none
  transfers between devices with their start and end apart: 4 -> 16, of which waited for: 2 -> 9; matrix products, arithmetic and copies ran while one was open for 44% -> 0% of each run, Pallas kernels for 0% -> 18%
where the time goes in v1:
time: 111 us
  waiting for transfers between devices  45.2 us (41%)
  Pallas kernels  29.1 us (26%)
  starting transfers between devices  26 us (23%)
  matrix products  7.81 us (7%)
  between operations  2.6 us (2%)
    ppermute x15, waiting for transfers between devices, swapped(): lax.ppermute(value, axis, [(source, source ^ mask) for source in range(co...  45.2 us
    ppermute x15, starting transfers between devices, swapped(): lax.ppermute(value, axis, [(source, source ^ mask) for source in range(co...  23.3 us
    pallas_call x8, Pallas kernels, call(): pl.pallas_call(kernel, in_specs=ins, out_specs=[VMEM] * len(outs), out_sh...  14 us
    pallas_call x1, Pallas kernels, sort_rest(): pl.pallas_call(sort_kernel, grid=(NQ,), in_specs=[VMEM] * 4 + [pl.BlockSp...  8.04 us
    dot_general x1, matrix products, all_steps(): lax.dot_general(basis_rotation[0], half_turn, (((0,), (0,)), ((), ())), p...  4.71 us
    pallas_call x1, Pallas kernels, sort_columns(): pl.pallas_call(columns_kernel, grid=(NQ,), in_specs=[VMEM, pl.BlockSpec((...  4.45 us
    dot_general x1, matrix products, all_steps(): jnp.dot(turned_left, basis_rotation[0], precision=lax.Precision.HIGH)  3.09 us
    ppermute x1, starting transfers between devices, passed_along(): lax.ppermute(value, axis, [(source, source + steps) for source in range(f...  2.73 us
  transfers between devices with their start and end apart: 16, of which 9 were waited for; matrix products, arithmetic and copies ran while one was open for 0% of the time, Pallas kernels for 18%

profile of v1, /device:TPU:0, one launch (start us, length us, event | category | flops | bytes accessed | tf_op | source)
XLA Modules:
  0.0 110.7 jit_solution(8767250529217147379)
XLA Ops:
  0.6 0.0 copy-start
  0.7 2.1 %shard_map.104.first_ref = f32[96,256]{1,0:T(8,128)S(1)} custom-call(s32[1]{0:T(128)} %bitcast.me_ref, s32[1,768]{1,0:T(1,128)} %left_hbm.1, s32[1,768]{1,0:T(1,128)} %charge_ref.3, f32[96,768]{1,0:T(8,128)} %bitcast.24), custom_call_target="tpu_custom_call" | custom-call | tf_op jit(solution)/shard_map/pallas_call | solution.py:344
  2.7 4.1 %collective-permute-start = (f32[96,256]{1,0:T(8,128)S(1)}, f32[96,256]{1,0:T(8,128)S(1)}, u32[]{:S(2)}, u32[]{:S(2)}) collective-permute-start(f32[96,256]{1,0:T(8,128)S(1)} %shard_map.104.first_ref), channel_id=1, source_target_pairs={{0,4},{1,5},{2,6},{3,7},{4,0},{5,1},{6,2},{7,3},{8,12},{9,13},{10,... | collective-permute-start | bytes 294920 | tf_op jit(solution)/shard_map/ppermute | solution.py:340
  6.9 4.9 %collective-permute-done.second_ref = f32[96,256]{1,0:T(8,128)S(1)} collective-permute-done((f32[96,256]{1,0:T(8,128)S(1)}, f32[96,256]{1,0:T(8,128)S(1)}, u32[]{:S(2)}, u32[]{:S(2)}) %collective-permute-start) | collective-permute-done | bytes 98336 | tf_op jit(solution)/shard_map/ppermute | solution.py:340
  11.8 1.7 %collective-permute-start.3 = (f32[192,256]{1,0:T(8,128)S(1)}, f32[192,256]{1,0:T(8,128)S(1)}, u32[]{:S(2)}, u32[]{:S(2)}) collective-permute-start(f32[192,256]{1,0:T(8,128)S(1)} %shard_map.105.refs_0_), channel_id=1, source_target_pairs={{0,3},{1,2},{2,1},{3,0},{4,7},{5,6},{6,5},{7,4},{8,11},{9,10},{10,... | collective-permute-start | bytes 589832 | tf_op jit(solution)/shard_map/ppermute | solution.py:340
  13.5 1.4 %collective-permute-start.2 = (f32[192,256]{1,0:T(8,128)S(1)}, f32[192,256]{1,0:T(8,128)S(1)}, u32[]{:S(2)}, u32[]{:S(2)}) collective-permute-start(f32[192,256]{1,0:T(8,128)S(1)} %shard_map.105.refs_0_), channel_id=1, source_target_pairs={{0,2},{1,3},{2,0},{3,1},{4,6},{5,7},{6,4},{7,5},{8,10},{9,11},{10,... | collective-permute-start | bytes 589832 | tf_op jit(solution)/shard_map/ppermute | solution.py:340
  14.8 0.5 collective-permute-start.1
  16.0 4.4 %shard_map.103 = (bf16[768,768]{1,0:T(8,128)(2,1)S(1)}, bf16[768,768]{1,0:T(8,128)(2,1)S(1)}, bf16[768,768]{1,0:T(8,128)(2,1)S(1)}, bf16[768,768]{1,0:T(8,128)(2,1)S(1)}, f32[768,128]{1,0:T(8,128)S(1)}) custom-call(s32[1,768]{1,0:T(1,128)} %left_hbm.1, f32[768,768]{1,0:T(8,128)} %bitcast.19), custom_call_target="tpu_custom_call" | custom-call | tf_op jit(solution)/shard_map/pallas_call | solution.py:163
  20.4 0.0 copy-start.1
  20.4 8.0 %shard_map.106 = (bf16[768,768]{1,0:T(8,128)(2,1)S(1)}, bf16[768,768]{1,0:T(8,128)(2,1)S(1)}, bf16[768,768]{1,0:T(8,128)(2,1)S(1)}, bf16[768,768]{1,0:T(8,128)(2,1)S(1)}, f32[8,768]{1,0:T(8,128)S(1)}) custom-call(s32[1,768]{1,0:T(1,128)} %charge_ref.3, bf16[768,768]{1,0:T(8,128)(2,1)S(1)} %get-tuple-element.33.left_half_high, ...), custom_call_target="tpu_custom_call" | custom-call | tf_op jit(solution)/shard_map/pallas_call | solution.py:176
  28.5 0.0 collective-permute-done.3.refs_3_
  28.5 0.0 collective-permute-done.2.refs_2_
  28.5 0.0 collective-permute-done.1.refs_1_
  28.5 0.0 copy-start.2
  28.5 4.9 %shard_map.107 = (f32[768,256]{1,0:T(8,128)S(1)}, f32[96,256]{1,0:T(8,128)S(1)}, f32[192,256]{1,0:T(8,128)S(1)}, f32[192,256]{1,0:T(8,128)S(1)}, f32[192,256]{1,0:T(8,128)S(1)}, /*index=5*/f32[192,256]{1,0:T(8,128)S(1)}) custom-call(s32[1]{0:T(128)} %bitcast.me_ref, s32[1,1]{1,0:T(1,128)S(6)} %copy.14.term_ref, f32[16]{0:T(128)S(1)} %copy-done.1, ...), custom_call_target="tpu_custom_call" | custom-call | tf_op jit(solution)/shard_map/pallas_call | solution.py:344
  33.5 0.0 copy-done
  33.5 0.0 copy-done.2
  33.5 3.1 %fusion.2 = f32[768,768]{1,0:T(8,128)S(1)} fusion(f32[768,768]{1,0:T(8,128)S(1)} %bitcast.21, f32[1,768,768]{2,1,0:T(8,128)S(1)} %copy-done), kind=kOutput, calls=%fused_computation.2 | convolution fusion | flops 2717908992 | bytes 7077888 | tf_op jit(solution)/shard_map/dot_general | solution.py:462
  36.6 4.7 %fusion.4 = f32[768,768]{1,0:T(8,128)} fusion(f32[768,768]{1,0:T(8,128)S(1)} %fusion.2, f32[1,768,768]{2,1,0:T(8,128)S(1)} %copy-done), kind=kOutput, calls=%fused_computation.4 | convolution fusion | flops 2717908992 | bytes 7077888 | tf_op jit(solution)/shard_map/dot_general | solution.py:463
  41.3 2.7 %collective-permute-start.15 = (f32[768,768]{1,0:T(8,128)}, f32[768,768]{1,0:T(8,128)}, u32[]{:S(2)}, u32[]{:S(2)}) collective-permute-start(f32[768,768]{1,0:T(8,128)} %fusion.4), channel_id=1, source_target_pairs={{0,8},{8,16},{16,24},{1,9},{9,17},{17,25},{2,10},{10,18},{18,26},{... | collective-permute-start | bytes 7077896 | tf_op jit(solution)/shard_map/ppermute | solution.py:327
  44.0 1.7 %collective-permute-start.4 = (f32[192,256]{1,0:T(8,128)S(1)}, f32[192,256]{1,0:T(8,128)S(1)}, u32[]{:S(2)}, u32[]{:S(2)}) collective-permute-start(f32[192,256]{1,0:T(8,128)S(1)} %get-tuple-element.40), channel_id=1, source_target_pairs={{0,3},{1,2},{2,1},{3,0},{4,7},{5,6},{6,5},{7,4},{8,11},{9,10},{10,... | collective-permute-start | bytes 589832 | tf_op jit(solution)/shard_map/ppermute | solution.py:340
  45.7 1.3 %collective-permute-start.5 = (f32[192,256]{1,0:T(8,128)S(1)}, f32[192,256]{1,0:T(8,128)S(1)}, u32[]{:S(2)}, u32[]{:S(2)}) collective-permute-start(f32[192,256]{1,0:T(8,128)S(1)} %get-tuple-element.41), channel_id=1, source_target_pairs={{0,2},{1,3},{2,0},{3,1},{4,6},{5,7},{6,4},{7,5},{8,10},{9,11},{10,... | collective-permute-start | bytes 589832 | tf_op jit(solution)/shard_map/ppermute | solution.py:340
  47.0 0.5 collective-permute-start.6
  47.5 5.1 %collective-permute-done.4.refs_1_ = f32[192,256]{1,0:T(8,128)S(1)} collective-permute-done((f32[192,256]{1,0:T(8,128)S(1)}, f32[192,256]{1,0:T(8,128)S(1)}, u32[]{:S(2)}, u32[]{:S(2)}) %collective-permute-start.4) | collective-permute-done | bytes 196640 | tf_op jit(solution)/shard_map/ppermute | solution.py:340
  52.6 4.3 %collective-permute-done.5.refs_2_ = f32[192,256]{1,0:T(8,128)S(1)} collective-permute-done((f32[192,256]{1,0:T(8,128)S(1)}, f32[192,256]{1,0:T(8,128)S(1)}, u32[]{:S(2)}, u32[]{:S(2)}) %collective-permute-start.5) | collective-permute-done | bytes 196640 | tf_op jit(solution)/shard_map/ppermute | solution.py:340
  56.9 0.0 collective-permute-done.6.refs_3_
  56.9 0.1 shard_map.108.refs_0_
  57.0 2.3 %collective-permute-start.7 = (f32[192,256]{1,0:T(8,128)S(1)}, f32[192,256]{1,0:T(8,128)S(1)}, u32[]{:S(2)}, u32[]{:S(2)}) collective-permute-start(f32[192,256]{1,0:T(8,128)S(1)} %shard_map.108.refs_0_), channel_id=1, source_target_pairs={{0,4},{1,5},{2,6},{3,7},{4,0},{5,1},{6,2},{7,3},{8,12},{9,13},{10,... | collective-permute-start | bytes 589832 | tf_op jit(solution)/shard_map/ppermute | solution.py:340
  59.3 9.8 %collective-permute-done.7.refs_1_ = f32[192,256]{1,0:T(8,128)S(1)} collective-permute-done((f32[192,256]{1,0:T(8,128)S(1)}, f32[192,256]{1,0:T(8,128)S(1)}, u32[]{:S(2)}, u32[]{:S(2)}) %collective-permute-start.7) | collective-permute-done | bytes 196640 | tf_op jit(solution)/shard_map/ppermute | solution.py:340
  69.1 1.2 %collective-permute-start.10 = (f32[192,256]{1,0:T(8,128)S(1)}, f32[192,256]{1,0:T(8,128)S(1)}, u32[]{:S(2)}, u32[]{:S(2)}) collective-permute-start(f32[192,256]{1,0:T(8,128)S(1)} %shard_map.109.refs_0_), channel_id=1, source_target_pairs={{0,3},{1,2},{2,1},{3,0},{4,7},{5,6},{6,5},{7,4},{8,11},{9,10},{10,... | collective-permute-start | bytes 589832 | tf_op jit(solution)/shard_map/ppermute | solution.py:340
  70.3 1.8 %collective-permute-start.9 = (f32[192,256]{1,0:T(8,128)S(1)}, f32[192,256]{1,0:T(8,128)S(1)}, u32[]{:S(2)}, u32[]{:S(2)}) collective-permute-start(f32[192,256]{1,0:T(8,128)S(1)} %shard_map.109.refs_0_), channel_id=1, source_target_pairs={{0,2},{1,3},{2,0},{3,1},{4,6},{5,7},{6,4},{7,5},{8,10},{9,11},{10,... | collective-permute-start | bytes 589832 | tf_op jit(solution)/shard_map/ppermute | solution.py:340
  72.1 0.5 collective-permute-start.8
  72.6 5.2 %collective-permute-done.10.refs_3_ = f32[192,256]{1,0:T(8,128)S(1)} collective-permute-done((f32[192,256]{1,0:T(8,128)S(1)}, f32[192,256]{1,0:T(8,128)S(1)}, u32[]{:S(2)}, u32[]{:S(2)}) %collective-permute-start.10) | collective-permute-done | bytes 196640 | tf_op jit(solution)/shard_map/ppermute | solution.py:340
  77.8 2.6 %collective-permute-done.9.refs_2_ = f32[192,256]{1,0:T(8,128)S(1)} collective-permute-done((f32[192,256]{1,0:T(8,128)S(1)}, f32[192,256]{1,0:T(8,128)S(1)}, u32[]{:S(2)}, u32[]{:S(2)}) %collective-permute-start.9) | collective-permute-done | bytes 196640 | tf_op jit(solution)/shard_map/ppermute | solution.py:340
  80.4 0.0 collective-permute-done.8.refs_1_
  80.4 5.0 %shard_map.110 = (f32[1,1]{1,0:T(1,128)S(1)}, f32[1,1]{1,0:T(1,128)}, f32[96,256]{1,0:T(8,128)S(1)}, f32[96,128]{1,0:T(8,128)S(1)}, f32[192,256]{1,0:T(8,128)S(1...) custom-call(s32[1]{0:T(128)} %bitcast.me_ref, s32[1,1]{1,0:T(1,128)S(6)} %copy.14.term_ref, ...), custom_call_target="tpu_custom_call" | custom-call | tf_op jit(solution)/shard_map/pallas_call | solution.py:344
  85.4 1.8 %collective-permute-start.11 = (f32[192,256]{1,0:T(8,128)S(1)}, f32[192,256]{1,0:T(8,128)S(1)}, u32[]{:S(2)}, u32[]{:S(2)}) collective-permute-start(f32[192,256]{1,0:T(8,128)S(1)} %get-tuple-element.51), channel_id=1, source_target_pairs={{0,3},{1,2},{2,1},{3,0},{4,7},{5,6},{6,5},{7,4},{8,11},{9,10},{10,... | collective-permute-start | bytes 589832 | tf_op jit(solution)/shard_map/ppermute | solution.py:340
  87.2 1.1 collective-permute-start.12
  88.3 0.6 collective-permute-start.13
  88.9 5.2 %collective-permute-done.11.refs_1_ = f32[192,256]{1,0:T(8,128)S(1)} collective-permute-done((f32[192,256]{1,0:T(8,128)S(1)}, f32[192,256]{1,0:T(8,128)S(1)}, u32[]{:S(2)}, u32[]{:S(2)}) %collective-permute-start.11) | collective-permute-done | bytes 196640 | tf_op jit(solution)/shard_map/ppermute | solution.py:340
  94.1 3.1 %collective-permute-done.12.refs_2_ = f32[192,256]{1,0:T(8,128)S(1)} collective-permute-done((f32[192,256]{1,0:T(8,128)S(1)}, f32[192,256]{1,0:T(8,128)S(1)}, u32[]{:S(2)}, u32[]{:S(2)}) %collective-permute-start.12) | collective-permute-done | bytes 196640 | tf_op jit(solution)/shard_map/ppermute | solution.py:340
  97.2 0.0 collective-permute-done.13.refs_3_
  97.2 0.1 shard_map.111
  97.3 2.8 %collective-permute-start.14 = (f32[96,256]{1,0:T(8,128)S(1)}, f32[96,256]{1,0:T(8,128)S(1)}, u32[]{:S(2)}, u32[]{:S(2)}) collective-permute-start(f32[96,256]{1,0:T(8,128)S(1)} %get-tuple-element.55), channel_id=1, source_target_pairs={{0,4},{1,5},{2,6},{3,7},{4,0},{5,1},{6,2},{7,3},{8,12},{9,13},{10,... | collective-permute-start | bytes 294920 | tf_op jit(solution)/shard_map/ppermute | solution.py:340
  100.1 5.0 %collective-permute-done.14.sent_ref = f32[96,256]{1,0:T(8,128)S(1)} collective-permute-done((f32[96,256]{1,0:T(8,128)S(1)}, f32[96,256]{1,0:T(8,128)S(1)}, u32[]{:S(2)}, u32[]{:S(2)}) %collective-permute-start.14) | collective-permute-done | bytes 98336 | tf_op jit(solution)/shard_map/ppermute | solution.py:340
  105.1 1.9 %shard_map.112 = f32[96,768]{1,0:T(8,128)} custom-call(f32[96,128]{1,0:T(8,128)S(1)} %get-tuple-element.44.spot_ref, f32[8,768]{1,0:T(8,128)S(1)} %get-tuple-element.45.place_ref, f32[1,1]{1,0:T(1,128)S(1)} %get-tuple-element.46.energy_ref, f32[1,1]{1,0:T(1,128)} %get-tuple-element.47.spread_ref, f32[96,256]{1,0:T(8,128)S(1)} %get-tuple-element.48.initial_ref, ...), custom_call_target="tpu_custom_call" | custom-call | tf_op jit(solution)/shard_map/pallas_call | solution.py:344
  107.0 0.0 collective-permute-done.15.shifted_ref
  107.0 2.6 %shard_map.113 = f32[768,768]{1,0:T(8,128)} custom-call(s32[1]{0:T(128)} %bitcast.6.segment_ref, f32[768,768]{1,0:T(8,128)} %bitcast.20, f32[768,768]{1,0:T(8,128)} %collective-permute-done.15.shifted_ref), custom_call_target="tpu_custom_call" | custom-call | tf_op jit(solution)/shard_map/pallas_call | solution.py:468
  (3 shorter events, 0.0 us)
Async XLA Ops:
  0.6 32.8 %copy-start = (f32[1,768,768]{2,1,0:T(8,128)S(1)}, f32[1,768,768]{2,1,0:T(8,128)}, u32[]{:S(2)}) copy-start(f32[1,768,768]{2,1,0:T(8,128)} %param.11) | copy-start | bytes 7077892
  2.7 9.0 %collective-permute-start = (f32[96,256]{1,0:T(8,128)S(1)}, f32[96,256]{1,0:T(8,128)S(1)}, u32[]{:S(2)}, u32[]{:S(2)}) collective-permute-start(f32[96,256]{1,0:T(8,128)S(1)} %shard_map.104.first_ref), channel_id=1, source_target_pairs={{0,4},{1,5},{2,6},{3,7},{4,0},{5,1},{6,2},{7,3},{8,12},{9,13},{10,... | collective-permute-start | bytes 294920 | tf_op jit(solution)/shard_map/ppermute | solution.py:340
  11.8 16.7 %collective-permute-start.3 = (f32[192,256]{1,0:T(8,128)S(1)}, f32[192,256]{1,0:T(8,128)S(1)}, u32[]{:S(2)}, u32[]{:S(2)}) collective-permute-start(f32[192,256]{1,0:T(8,128)S(1)} %shard_map.105.refs_0_), channel_id=1, source_target_pairs={{0,3},{1,2},{2,1},{3,0},{4,7},{5,6},{6,5},{7,4},{8,11},{9,10},{10,... | collective-permute-start | bytes 589832 | tf_op jit(solution)/shard_map/ppermute | solution.py:340
  13.5 15.0 %collective-permute-start.2 = (f32[192,256]{1,0:T(8,128)S(1)}, f32[192,256]{1,0:T(8,128)S(1)}, u32[]{:S(2)}, u32[]{:S(2)}) collective-permute-start(f32[192,256]{1,0:T(8,128)S(1)} %shard_map.105.refs_0_), channel_id=1, source_target_pairs={{0,2},{1,3},{2,0},{3,1},{4,6},{5,7},{6,4},{7,5},{8,10},{9,11},{10,... | collective-permute-start | bytes 589832 | tf_op jit(solution)/shard_map/ppermute | solution.py:340
  14.8 13.7 %collective-permute-start.1 = (f32[192,256]{1,0:T(8,128)S(1)}, f32[192,256]{1,0:T(8,128)S(1)}, u32[]{:S(2)}, u32[]{:S(2)}) collective-permute-start(f32[192,256]{1,0:T(8,128)S(1)} %shard_map.105.refs_0_), channel_id=1, source_target_pairs={{0,1},{1,0},{2,3},{3,2},{4,5},{5,4},{6,7},{7,6},{8,9},{9,8},{10,11... | collective-permute-start | bytes 589832 | tf_op jit(solution)/shard_map/ppermute | solution.py:340
  20.4 8.1 %copy-start.1 = (f32[16]{0:T(128)S(1)}, f32[16]{0:T(128)}, u32[]{:S(2)}) copy-start(f32[16]{0:T(128)} %table_ref.3) | copy-start | bytes 196
  28.5 4.9 %copy-start.2 = (f32[1,1,768,768]{3,2,1,0:T(8,128)S(1)}, f32[1,1,768,768]{3,2,1,0:T(8,128)}, u32[]{:S(2)}) copy-start(f32[1,1,768,768]{3,2,1,0:T(8,128)} %param.8) | copy-start | bytes 7077892
  41.3 65.7 %collective-permute-start.15 = (f32[768,768]{1,0:T(8,128)}, f32[768,768]{1,0:T(8,128)}, u32[]{:S(2)}, u32[]{:S(2)}) collective-permute-start(f32[768,768]{1,0:T(8,128)} %fusion.4), channel_id=1, source_target_pairs={{0,8},{8,16},{16,24},{1,9},{9,17},{17,25},{2,10},{10,18},{18,26},{... | collective-permute-start | bytes 7077896 | tf_op jit(solution)/shard_map/ppermute | solution.py:327
  44.0 8.6 %collective-permute-start.4 = (f32[192,256]{1,0:T(8,128)S(1)}, f32[192,256]{1,0:T(8,128)S(1)}, u32[]{:S(2)}, u32[]{:S(2)}) collective-permute-start(f32[192,256]{1,0:T(8,128)S(1)} %get-tuple-element.40), channel_id=1, source_target_pairs={{0,3},{1,2},{2,1},{3,0},{4,7},{5,6},{6,5},{7,4},{8,11},{9,10},{10,... | collective-permute-start | bytes 589832 | tf_op jit(solution)/shard_map/ppermute | solution.py:340
  45.7 11.2 %collective-permute-start.5 = (f32[192,256]{1,0:T(8,128)S(1)}, f32[192,256]{1,0:T(8,128)S(1)}, u32[]{:S(2)}, u32[]{:S(2)}) collective-permute-start(f32[192,256]{1,0:T(8,128)S(1)} %get-tuple-element.41), channel_id=1, source_target_pairs={{0,2},{1,3},{2,0},{3,1},{4,6},{5,7},{6,4},{7,5},{8,10},{9,11},{10,... | collective-permute-start | bytes 589832 | tf_op jit(solution)/shard_map/ppermute | solution.py:340
  47.0 9.9 %collective-permute-start.6 = (f32[192,256]{1,0:T(8,128)S(1)}, f32[192,256]{1,0:T(8,128)S(1)}, u32[]{:S(2)}, u32[]{:S(2)}) collective-permute-start(f32[192,256]{1,0:T(8,128)S(1)} %get-tuple-element.42), channel_id=1, source_target_pairs={{0,1},{1,0},{2,3},{3,2},{4,5},{5,4},{6,7},{7,6},{8,9},{9,8},{10,11... | collective-permute-start | bytes 589832 | tf_op jit(solution)/shard_map/ppermute | solution.py:340
  57.0 12.1 %collective-permute-start.7 = (f32[192,256]{1,0:T(8,128)S(1)}, f32[192,256]{1,0:T(8,128)S(1)}, u32[]{:S(2)}, u32[]{:S(2)}) collective-permute-start(f32[192,256]{1,0:T(8,128)S(1)} %shard_map.108.refs_0_), channel_id=1, source_target_pairs={{0,4},{1,5},{2,6},{3,7},{4,0},{5,1},{6,2},{7,3},{8,12},{9,13},{10,... | collective-permute-start | bytes 589832 | tf_op jit(solution)/shard_map/ppermute | solution.py:340
  69.1 8.7 %collective-permute-start.10 = (f32[192,256]{1,0:T(8,128)S(1)}, f32[192,256]{1,0:T(8,128)S(1)}, u32[]{:S(2)}, u32[]{:S(2)}) collective-permute-start(f32[192,256]{1,0:T(8,128)S(1)} %shard_map.109.refs_0_), channel_id=1, source_target_pairs={{0,3},{1,2},{2,1},{3,0},{4,7},{5,6},{6,5},{7,4},{8,11},{9,10},{10,... | collective-permute-start | bytes 589832 | tf_op jit(solution)/shard_map/ppermute | solution.py:340
  70.3 10.1 %collective-permute-start.9 = (f32[192,256]{1,0:T(8,128)S(1)}, f32[192,256]{1,0:T(8,128)S(1)}, u32[]{:S(2)}, u32[]{:S(2)}) collective-permute-start(f32[192,256]{1,0:T(8,128)S(1)} %shard_map.109.refs_0_), channel_id=1, source_target_pairs={{0,2},{1,3},{2,0},{3,1},{4,6},{5,7},{6,4},{7,5},{8,10},{9,11},{10,... | collective-permute-start | bytes 589832 | tf_op jit(solution)/shard_map/ppermute | solution.py:340
  72.1 8.3 %collective-permute-start.8 = (f32[192,256]{1,0:T(8,128)S(1)}, f32[192,256]{1,0:T(8,128)S(1)}, u32[]{:S(2)}, u32[]{:S(2)}) collective-permute-start(f32[192,256]{1,0:T(8,128)S(1)} %shard_map.109.refs_0_), channel_id=1, source_target_pairs={{0,1},{1,0},{2,3},{3,2},{4,5},{5,4},{6,7},{7,6},{8,9},{9,8},{10,11... | collective-permute-start | bytes 589832 | tf_op jit(solution)/shard_map/ppermute | solution.py:340
  85.4 8.7 %collective-permute-start.11 = (f32[192,256]{1,0:T(8,128)S(1)}, f32[192,256]{1,0:T(8,128)S(1)}, u32[]{:S(2)}, u32[]{:S(2)}) collective-permute-start(f32[192,256]{1,0:T(8,128)S(1)} %get-tuple-element.51), channel_id=1, source_target_pairs={{0,3},{1,2},{2,1},{3,0},{4,7},{5,6},{6,5},{7,4},{8,11},{9,10},{10,... | collective-permute-start | bytes 589832 | tf_op jit(solution)/shard_map/ppermute | solution.py:340
  87.2 10.0 %collective-permute-start.12 = (f32[192,256]{1,0:T(8,128)S(1)}, f32[192,256]{1,0:T(8,128)S(1)}, u32[]{:S(2)}, u32[]{:S(2)}) collective-permute-start(f32[192,256]{1,0:T(8,128)S(1)} %get-tuple-element.52), channel_id=1, source_target_pairs={{0,2},{1,3},{2,0},{3,1},{4,6},{5,7},{6,4},{7,5},{8,10},{9,11},{10,... | collective-permute-start | bytes 589832 | tf_op jit(solution)/shard_map/ppermute | solution.py:340
  88.3 8.9 %collective-permute-start.13 = (f32[192,256]{1,0:T(8,128)S(1)}, f32[192,256]{1,0:T(8,128)S(1)}, u32[]{:S(2)}, u32[]{:S(2)}) collective-permute-start(f32[192,256]{1,0:T(8,128)S(1)} %get-tuple-element.53), channel_id=1, source_target_pairs={{0,1},{1,0},{2,3},{3,2},{4,5},{5,4},{6,7},{7,6},{8,9},{9,8},{10,11... | collective-permute-start | bytes 589832 | tf_op jit(solution)/shard_map/ppermute | solution.py:340
  97.3 7.8 %collective-permute-start.14 = (f32[96,256]{1,0:T(8,128)S(1)}, f32[96,256]{1,0:T(8,128)S(1)}, u32[]{:S(2)}, u32[]{:S(2)}) collective-permute-start(f32[96,256]{1,0:T(8,128)S(1)} %get-tuple-element.55), channel_id=1, source_target_pairs={{0,4},{1,5},{2,6},{3,7},{4,0},{5,1},{6,2},{7,3},{8,12},{9,13},{10,... | collective-permute-start | bytes 294920 | tf_op jit(solution)/shard_map/ppermute | solution.py:340

commit v2 on v1

--- a/solution.py
+++ b/solution.py
@@ -83,16 +83,15 @@
     ]
     for copy in copies:
         copy.start()
-    for copy in copies:
-        copy.wait()
+    copies[0].wait()
     back = unsorter(column(places_of(right_ref[...], block)), size)
+    copies[1].wait()
     column_ref[...] = column(left_ref[...].astype(F32))
     start = pl.multiple_of(me_ref[0] * rows, 8)
     charge = column_ref[pl.ds(start, rows), :][:, :1]
-    wave = wave_ref[...]
-    first, _ = split(wave)
-    second, third = split(wave - first.astype(F32))
-    ordered = mm(first, back) + (mm(second, back) + mm(third, back))
+    copies[2].wait()
+    both = mm(jnp.concatenate(split(wave_ref[...]), axis=0), back)
+    ordered = both[:rows, :] + both[rows:, :]
     packed = jnp.zeros((rows, block), F32)
     for q in range(NQ):
         packed = packed + jnp.where(charge == float(q), ordered[:, q * block : (q + 1) * block], 0.0)
@@ -126,7 +125,6 @@
     left_low,
     right_high,
     right_low,
-    place_ref,
     onto,
     back,
     half_high,
@@ -138,7 +136,6 @@
     @pl.when(step == 0)
     def _():
         place = places_of(charge_ref[...], size // NQ)
-        place_ref[...] = jnp.broadcast_to(place, place_ref.shape)
         onto[...] = sorter(place)
         back[...] = unsorter(column(place), size)
 
@@ -177,8 +174,8 @@
         sort_kernel,
         grid=(NQ,),
         in_specs=[VMEM] * 4 + [pl.BlockSpec((rows, size), lambda i: (i, 0))],
-        out_specs=[VMEM] * 5,
-        out_shape=[pltpu.VMEM((size, size), BF16)] * 4 + [jax.ShapeDtypeStruct((8, size), F32)],
+        out_specs=[VMEM] * 4,
+        out_shape=[pltpu.VMEM((size, size), BF16)] * 4,
         scratch_shapes=[pltpu.VMEM((size, size), BF16) for _ in range(4)],
         compiler_params=LIMIT,
     )(far(charge), left_half_high, left_half_low, left_onto, far(ops))
@@ -228,24 +225,28 @@
 
 
 def second_kernel(group, me_ref, term_ref, table_ref, back_ref, column_ref, *refs):
-    parts = refs[:group]
-    initial_ref, left_high, left_low, right_high, right_low = refs[group : group + 5]
-    energy_ref, spread_ref, step_rows_ref, spot_ref = refs[group + 5 : group + 9]
-    outs = refs[group + 9 : 2 * group + 9]
-    half_high, half_low, total, step_ref = refs[2 * group + 9 :]
+    count = 2 * group
+    parts = refs[:count]
+    initial_ref, left_high, left_low, right_high, right_low = refs[count : count + 5]
+    energy_ref, spread_ref, step_rows_ref, spot_ref = refs[count + 5 : count + 9]
+    outs = refs[count + 9 : 2 * count + 9]
+    half_high, half_low, total, step_ref = refs[2 * count + 9 :]
     half = lax.div(me_ref[0], group)
     own = lax.rem(me_ref[0], group)
-    pair, block = parts[0].shape
+    pair, width = parts[0].shape
+    block = 2 * width
+    sides = [slice(c * width, (c + 1) * width) for c in range(2)]
     rows = pair // 2
     size = pair * group
     each = block // group
     for s in range(group):
         for q in range(NQ):
             start = pl.multiple_of(q * block + (own ^ s) * each, 8)
-            total[pl.ds(start, each), :] = parts[s][q * each : (q + 1) * each, :]
-    width = float(size * size)
-    energy = jnp.sum(initial_ref[...] * total[...], keepdims=True) / width
-    spread = jnp.sqrt(jnp.sum(total[...] * total[...], keepdims=True) / width + 1e-06)
+            for c in range(2):
+                total[pl.ds(start, each), sides[c]] = parts[c * group + s][q * each : (q + 1) * each, :]
+    cells = float(size * size)
+    energy = jnp.sum(initial_ref[...] * total[...], keepdims=True) / cells
+    spread = jnp.sqrt(jnp.sum(total[...] * total[...], keepdims=True) / cells + 1e-06)
     step_ref[...] = (total[...] - energy * initial_ref[...]) / spread
     energy_ref[...] = energy
     spread_ref[...] = spread
@@ -263,22 +264,28 @@
     for s in range(group):
         for h, side in enumerate((half, 1 - half)):
             start = pl.multiple_of((side * group + (own ^ s)) * rows, 8)
-            outs[s][h * rows : (h + 1) * rows, :] = total[pl.ds(start, rows), :]
-
-
-def last_kernel(spot_ref, place_ref, energy_ref, spread_ref, initial_ref, step_ref, kept_ref, sent_ref, out_ref):
-    image = kept_ref[...] + sent_ref[...]
+            for c in range(2):
+                outs[c * group + s][h * rows : (h + 1) * rows, :] = total[pl.ds(start, rows), sides[c]]
+
+
+def order_kernel(charge_ref, onto_ref):
+    onto_ref[...] = sorter(places_of(charge_ref[...], charge_ref.shape[1] // NQ))
+
+
+def last_kernel(spot_ref, onto_ref, energy_ref, spread_ref, initial_ref, step_ref, *refs):
+    kept, sent, out_ref = refs[:2], refs[2:4], refs[4]
+    image = jnp.concatenate([a[...] + b[...] for a, b in zip(kept, sent)], axis=1)
     packed = 2.0 * (image - energy_ref[...] * step_ref[...]) / spread_ref[...] - initial_ref[...]
     block = packed.shape[1]
     spot = jnp.broadcast_to(spot_ref[...][:, :1], packed.shape)
     held = [(spot >= float(q * block)) & (spot < float((q + 1) * block)) for q in range(NQ)]
-    onto = sorter(place_ref[...][:1, :])
     high = packed.astype(BF16).astype(F32)
-    out = jnp.zeros(out_ref.shape, F32)
-    for piece in (high, packed - high):
-        wide = jnp.concatenate([jnp.where(here, piece, 0.0) for here in held], axis=1)
-        out = out + mm(wide.astype(BF16), onto)
-    out_ref[...] = out
+    wide = [
+        jnp.concatenate([jnp.where(here, piece, 0.0) for here in held], axis=1) for piece in (high, packed - high)
+    ]
+    both = mm(jnp.concatenate(wide, axis=0).astype(BF16), onto_ref[...])
+    rows = packed.shape[0]
+    out_ref[...] = both[:rows, :] + both[rows:, :]
 
 
 def join_kernel(first_ref, second_ref, out_ref):
@@ -287,24 +294,22 @@
     out_ref[rows:, :] = second_ref[...]
 
 
-def sum_kernel(*refs):
-    parts = [ref for ref in refs if ref.shape == refs[0].shape]
-    outs = refs[len(parts) :]
-    if not outs:
-        parts, outs = parts[:-1], parts[-1:]
-    start = 0
-    for out in outs:
-        here = slice(start, start + out.shape[0])
-        start += out.shape[0]
-        value = parts[0][here, :]
+def sum_kernel(count, *refs):
+    parts, outs = refs[:count], refs[count:]
+    rows, width = outs[0].shape
+    across = parts[0].shape[1] // width
+    for i, out in enumerate(outs):
+        here = (slice((i // across) * rows, (i // across + 1) * rows), slice((i % across) * width, (i % across + 1) * width))
+        value = parts[0][here]
         for part in parts[1:]:
-            value = value + part[here, :]
+            value = value + part[here]
         out[...] = value
 
 
 def choose_kernel(segment_ref, own_ref, shifted_ref, out_ref, held, arrived, left):
-    rows = own_ref.shape[0] // NQ
-    parts = [slice(q * rows, (q + 1) * rows) for q in range(NQ)]
+    steps = arrived.shape[0]
+    rows = own_ref.shape[0] // steps
+    parts = [slice(q * rows, (q + 1) * rows) for q in range(steps)]
     outs = [pltpu.make_async_copy(held.at[p], out_ref.at[p], left.at[q]) for q, p in enumerate(parts)]
 
     def through(source):
@@ -351,9 +356,10 @@
     )(*operands)
 
 
-def summed(heights, *parts):
-    outs = [pltpu.VMEM((h,) + parts[0].shape[1:], F32) for h in heights]
-    return call(sum_kernel, [VMEM] * len(parts), outs, [], *parts)
+def summed(shape, *parts):
+    size = parts[0].shape
+    outs = [pltpu.VMEM(shape, F32)] * ((size[0] // shape[0]) * (size[1] // shape[1]))
+    return call(functools.partial(sum_kernel, len(parts)), [VMEM] * len(parts), outs, [], *parts)
 
 
 def all_steps(
@@ -396,9 +402,7 @@
     gathered = [pair] + [swapped(pair, "op", s) for s in range(1, group)]
 
     left_half_high, left_half_low, onto, back, left_column = sort_columns(left_charge, own_left)
-    left_high, left_low, right_high, right_low, right_place = sort_rest(
-        right_charge, left_half_high, left_half_low, onto, own_right
-    )
+    left_high, left_low, right_high, right_low = sort_rest(right_charge, left_half_high, left_half_low, onto, own_right)
     pieces = (left_high, left_low, right_high, right_low)
     halves = [pltpu.VMEM((size, size), BF16), pltpu.VMEM((size, size), BF16), pltpu.VMEM((size, block), F32)]
     pairs = [pltpu.VMEM((2 * rows, block), F32)] * group
@@ -416,20 +420,25 @@
         *pieces,
         params=LIMIT,
     )
-    total = summed([2 * rows], sent[0], *[swapped(sent[s], "op", s) for s in range(group - 1, 0, -1)])[0]
-    total = summed([2 * rows], total, swapped(total, "op", group))[0]
-    gathered = [total] + [swapped(total, "op", s) for s in range(group - 1, 0, -1)][::-1]
+    inner = range(group - 1, 0, -1)
+    wings = [pltpu.VMEM((2 * rows, block // 2), F32)] * (2 * group)
+    totals = summed((2 * rows, block // 2), sent[0], *[swapped(sent[s], "op", s) for s in inner])
+    across = [swapped(total, "op", group) for total in totals]
+    gathered = []
+    for c in range(2):
+        (total,) = summed((2 * rows, block // 2), totals[c], across[c])
+        gathered += [total] + [swapped(total, "op", s) for s in inner][::-1]
 
     energy, spread, step_rows, spot, *sent = call(
         functools.partial(second_kernel, group),
-        [SMEM, SMEM, SMEM] + [VMEM] * (group + 7),
+        [SMEM, SMEM, SMEM] + [VMEM] * (2 * group + 7),
         [
             pltpu.VMEM((1, 1), F32),
             pltpu.VMEM((1, 1), F32),
             pltpu.VMEM((rows, block), F32),
             pltpu.VMEM((rows, LANES), F32),
         ]
-        + pairs,
+        + wings,
         halves + [pltpu.VMEM((size, block), F32)],
         me,
         pair_term,
@@ -441,21 +450,28 @@
         *pieces,
         params=LIMIT,
     )
-    kept, away = summed([rows, rows], near(sent[0]), *[swapped(sent[s], "op", s) for s in range(group - 1, 0, -1)])
-    received = swapped(away, "op", group)
+    kept, received = [], []
+    for c in range(2):
+        mine = sent[c * group : (c + 1) * group]
+        keep, away = summed((rows, block // 2), near(mine[0]), *[swapped(mine[s], "op", s) for s in inner])
+        kept.append(near(keep))
+        received.append(swapped(away, "op", group))
+    (right_onto,) = call(
+        order_kernel, [VMEM], [pltpu.VMEM((size, size), BF16)], [], far(right_charge)
+    )
     (chebyshev,) = call(
         last_kernel,
-        [VMEM] * 8,
+        [VMEM] * 10,
         [jax.ShapeDtypeStruct((rows, size), F32)],
         [],
         near(spot),
-        right_place,
+        near(right_onto),
         near(energy),
         near(spread),
         near(initial_rows),
         near(step_rows),
-        near(kept),
-        received,
+        *kept,
+        *received,
     )
 
     turned_left, _ = lax.optimization_barrier((own_left, initial))
@@ -470,7 +486,11 @@
         in_specs=[SMEM, HBM, HBM],
         out_specs=HBM,
         out_shape=jax.ShapeDtypeStruct((size, size), F32),
-        scratch_shapes=[pltpu.VMEM((size, size), F32), pltpu.SemaphoreType.DMA((NQ,)), pltpu.SemaphoreType.DMA((NQ,))],
+        scratch_shapes=[
+            pltpu.VMEM((size, size), F32),
+            pltpu.SemaphoreType.DMA((4 * NQ,)),
+            pltpu.SemaphoreType.DMA((4 * NQ,)),
+        ],
         compiler_params=SMALL,
     )(segment, far(own_left), far(shifted))[None, None]
     return (chebyshev[None], energy[0], handed)

time: 111 us -> 114 us (1.027)
  waiting for transfers between devices: 45.2 us -> 30.8 us
  starting transfers between devices: 26 us -> 36.3 us
  local copies, waits for them, and re-layouts: 0.02 us -> 4.83 us
  Pallas kernels: 29.1 us -> 31.5 us
    ppermute x15 -> x23, waiting for transfers between devices: 45.2 us -> 30.8 us  [swapped(): lax.ppermute(value, axis, [(source, source ^ mask) for source in range(co...]
    ppermute x15 -> x23, starting transfers between devices: 23.3 us -> 33.6 us  [swapped(): lax.ppermute(value, axis, [(source, source ^ mask) for source in range(co...]
    unnamed x6 -> x26, local copies, waits for them, and re-layouts: 0.02 us -> 4.83 us
    pallas_call x8 -> x11, Pallas kernels: 14 us -> 16.3 us  [call(): pl.pallas_call(kernel, in_specs=ins, out_specs=[VMEM] * len(outs), out_sh...]
  transfers between devices with their start and end apart: 16 -> 24, of which waited for: 9 -> 14; matrix products, arithmetic and copies ran while one was open for 0% -> 0% of each run, Pallas kernels for 18% -> 19%
where the time goes in v2:
time: 114 us
  starting transfers between devices  36.3 us (32%)
  Pallas kernels  31.5 us (28%)
  waiting for transfers between devices  30.8 us (27%)
  matrix products  7.81 us (7%)
  local copies, waits for them, and re-layouts  4.83 us (4%)
  between operations  2.67 us (2%)
    ppermute x23, starting transfers between devices, swapped(): lax.ppermute(value, axis, [(source, source ^ mask) for source in range(co...  33.6 us
    ppermute x23, waiting for transfers between devices, swapped(): lax.ppermute(value, axis, [(source, source ^ mask) for source in range(co...  30.8 us
    pallas_call x11, Pallas kernels, call(): pl.pallas_call(kernel, in_specs=ins, out_specs=[VMEM] * len(outs), out_sh...  16.3 us
    pallas_call x1, Pallas kernels, sort_rest(): pl.pallas_call(sort_kernel, grid=(NQ,), in_specs=[VMEM] * 4 + [pl.BlockSp...  8.04 us
    unnamed x26, local copies, waits for them, and re-layouts  4.83 us
    dot_general x1, matrix products, all_steps(): lax.dot_general(basis_rotation[0], half_turn, (((0,), (0,)), ((), ())), p...  4.71 us
    pallas_call x1, Pallas kernels, sort_columns(): pl.pallas_call(columns_kernel, grid=(NQ,), in_specs=[VMEM, pl.BlockSpec((...  4.45 us
    dot_general x1, matrix products, all_steps(): jnp.dot(turned_left, basis_rotation[0], precision=lax.Precision.HIGH)  3.1 us
  transfers between devices with their start and end apart: 24, of which 14 were waited for; matrix products, arithmetic and copies ran while one was open for 0% of the time, Pallas kernels for 19%

profile of v2, /device:TPU:0, one launch (start us, length us, event | category | flops | bytes accessed | tf_op | source)
XLA Modules:
  0.0 113.9 jit_solution(6087137940164111015)
XLA Ops:
  0.7 1.8 %shard_map.104.first_ref = f32[96,256]{1,0:T(8,128)S(1)} custom-call(s32[1]{0:T(128)} %bitcast.me_ref, s32[1,768]{1,0:T(1,128)} %left_hbm.1, s32[1,768]{1,0:T(1,128)} %charge_ref.5, f32[96,768]{1,0:T(8,128)} %bitcast.25), custom_call_target="tpu_custom_call" | custom-call | tf_op jit(solution)/shard_map/pallas_call | solution.py:349
  2.5 4.1 %collective-permute-start = (f32[96,256]{1,0:T(8,128)S(1)}, f32[96,256]{1,0:T(8,128)S(1)}, u32[]{:S(2)}, u32[]{:S(2)}) collective-permute-start(f32[96,256]{1,0:T(8,128)S(1)} %shard_map.104.first_ref), channel_id=1, source_target_pairs={{0,4},{1,5},{2,6},{3,7},{4,0},{5,1},{6,2},{7,3},{8,12},{9,13},{10,... | collective-permute-start | bytes 294920 | tf_op jit(solution)/shard_map/ppermute | solution.py:345
  6.6 4.9 %collective-permute-done.second_ref = f32[96,256]{1,0:T(8,128)S(1)} collective-permute-done((f32[96,256]{1,0:T(8,128)S(1)}, f32[96,256]{1,0:T(8,128)S(1)}, u32[]{:S(2)}, u32[]{:S(2)}) %collective-permute-start) | collective-permute-done | bytes 98336 | tf_op jit(solution)/shard_map/ppermute | solution.py:345
  11.5 1.6 %collective-permute-start.1 = (f32[192,256]{1,0:T(8,128)S(1)}, f32[192,256]{1,0:T(8,128)S(1)}, u32[]{:S(2)}, u32[]{:S(2)}) collective-permute-start(f32[192,256]{1,0:T(8,128)S(1)} %shard_map.105.refs_0_), channel_id=1, source_target_pairs={{0,1},{1,0},{2,3},{3,2},{4,5},{5,4},{6,7},{7,6},{8,9},{9,8},{10,11... | collective-permute-start | bytes 589832 | tf_op jit(solution)/shard_map/ppermute | solution.py:345
  13.2 0.7 collective-permute-start.2
  13.8 1.3 %collective-permute-start.3 = (f32[192,256]{1,0:T(8,128)S(1)}, f32[192,256]{1,0:T(8,128)S(1)}, u32[]{:S(2)}, u32[]{:S(2)}) collective-permute-start(f32[192,256]{1,0:T(8,128)S(1)} %shard_map.105.refs_0_), channel_id=1, source_target_pairs={{0,3},{1,2},{2,1},{3,0},{4,7},{5,6},{6,5},{7,4},{8,11},{9,10},{10,... | collective-permute-start | bytes 589832 | tf_op jit(solution)/shard_map/ppermute | solution.py:345
  15.8 4.5 %shard_map.103 = (bf16[768,768]{1,0:T(8,128)(2,1)S(1)}, bf16[768,768]{1,0:T(8,128)(2,1)S(1)}, bf16[768,768]{1,0:T(8,128)(2,1)S(1)}, bf16[768,768]{1,0:T(8,128)(2,1)S(1)}, f32[768,128]{1,0:T(8,128)S(1)}) custom-call(s32[1,768]{1,0:T(1,128)} %left_hbm.1, f32[768,768]{1,0:T(8,128)} %bitcast.19), custom_call_target="tpu_custom_call" | custom-call | tf_op jit(solution)/shard_map/pallas_call | solution.py:160
  20.2 8.0 %shard_map.106 = (bf16[768,768]{1,0:T(8,128)(2,1)S(1)}, bf16[768,768]{1,0:T(8,128)(2,1)S(1)}, bf16[768,768]{1,0:T(8,128)(2,1)S(1)}, bf16[768,768]{1,0:T(8,128)(2,1)S(1)}) custom-call(s32[1,768]{1,0:T(1,128)} %charge_ref.5, bf16[768,768]{1,0:T(8,128)(2,1)S(1)} %get-tuple-element.40.left_half_high, bf16[768,768]{1,0:T(8,128)(2,1)S(1)} %get-tuple-element.41.left_half_low, ...), custom_call_target="tpu_custom_call" | custom-call | tf_op jit(solution)/shard_map/pallas_call | solution.py:173
  28.3 4.9 %shard_map.107 = (f32[768,256]{1,0:T(8,128)S(1)}, f32[96,256]{1,0:T(8,128)S(1)}, f32[192,256]{1,0:T(8,128)S(1)}, f32[192,256]{1,0:T(8,128)S(1)}, f32[192,256]{1,0:T(8,128)S(1)}, /*index=5*/f32[192,256]{1,0:T(8,128)S(1)}) custom-call(s32[1]{0:T(128)} %bitcast.me_ref, s32[1,1]{1,0:T(1,128)S(6)} %copy.14.term_ref, f32[16]{0:T(128)S(1)} %copy-done.11, ...), custom_call_target="tpu_custom_call" | custom-call | tf_op jit(solution)/shard_map/pallas_call | solution.py:349
  33.3 3.1 %fusion.2 = f32[768,768]{1,0:T(8,128)S(1)} fusion(f32[768,768]{1,0:T(8,128)S(1)} %bitcast.21, f32[1,768,768]{2,1,0:T(8,128)S(1)} %copy-done), kind=kOutput, calls=%fused_computation.2 | convolution fusion | flops 2717908992 | bytes 7077888 | tf_op jit(solution)/shard_map/dot_general | solution.py:478
  36.4 4.7 %fusion.4 = f32[768,768]{1,0:T(8,128)} fusion(f32[768,768]{1,0:T(8,128)S(1)} %fusion.2, f32[1,768,768]{2,1,0:T(8,128)S(1)} %copy-done), kind=kOutput, calls=%fused_computation.4 | convolution fusion | flops 2717908992 | bytes 7077888 | tf_op jit(solution)/shard_map/dot_general | solution.py:479
  41.1 2.7 %collective-permute-start.23 = (f32[768,768]{1,0:T(8,128)}, f32[768,768]{1,0:T(8,128)}, u32[]{:S(2)}, u32[]{:S(2)}) collective-permute-start(f32[768,768]{1,0:T(8,128)} %fusion.4), channel_id=1, source_target_pairs={{0,8},{8,16},{16,24},{1,9},{9,17},{17,25},{2,10},{10,18},{18,26},{... | collective-permute-start | bytes 7077896 | tf_op jit(solution)/shard_map/ppermute | solution.py:332
  43.8 1.7 %collective-permute-start.4 = (f32[192,256]{1,0:T(8,128)S(1)}, f32[192,256]{1,0:T(8,128)S(1)}, u32[]{:S(2)}, u32[]{:S(2)}) collective-permute-start(f32[192,256]{1,0:T(8,128)S(1)} %get-tuple-element.47), channel_id=1, source_target_pairs={{0,3},{1,2},{2,1},{3,0},{4,7},{5,6},{6,5},{7,4},{8,11},{9,10},{10,... | collective-permute-start | bytes 589832 | tf_op jit(solution)/shard_map/ppermute | solution.py:345
  45.5 1.3 %collective-permute-start.5 = (f32[192,256]{1,0:T(8,128)S(1)}, f32[192,256]{1,0:T(8,128)S(1)}, u32[]{:S(2)}, u32[]{:S(2)}) collective-permute-start(f32[192,256]{1,0:T(8,128)S(1)} %get-tuple-element.48), channel_id=1, source_target_pairs={{0,2},{1,3},{2,0},{3,1},{4,6},{5,7},{6,4},{7,5},{8,10},{9,11},{10,... | collective-permute-start | bytes 589832 | tf_op jit(solution)/shard_map/ppermute | solution.py:345
  47.3 5.1 %collective-permute-done.4.refs_1_ = f32[192,256]{1,0:T(8,128)S(1)} collective-permute-done((f32[192,256]{1,0:T(8,128)S(1)}, f32[192,256]{1,0:T(8,128)S(1)}, u32[]{:S(2)}, u32[]{:S(2)}) %collective-permute-start.4) | collective-permute-done | bytes 196640 | tf_op jit(solution)/shard_map/ppermute | solution.py:345
  52.4 4.3 %collective-permute-done.5.refs_2_ = f32[192,256]{1,0:T(8,128)S(1)} collective-permute-done((f32[192,256]{1,0:T(8,128)S(1)}, f32[192,256]{1,0:T(8,128)S(1)}, u32[]{:S(2)}, u32[]{:S(2)}) %collective-permute-start.5) | collective-permute-done | bytes 196640 | tf_op jit(solution)/shard_map/ppermute | solution.py:345
  56.8 2.2 %collective-permute-start.7 = (f32[192,128]{1,0:T(8,128)S(1)}, f32[192,128]{1,0:T(8,128)S(1)}, u32[]{:S(2)}, u32[]{:S(2)}) collective-permute-start(f32[192,128]{1,0:T(8,128)S(1)} %get-tuple-element.50.refs_0_), channel_id=1, source_target_pairs={{0,4},{1,5},{2,6},{3,7},{4,0},{5,1},{6,2},{7,3},{8,12},{9,13},{10,... | collective-permute-start | bytes 294920 | tf_op jit(solution)/shard_map/ppermute | solution.py:345
  59.0 0.7 collective-permute-start.11
  59.7 7.9 %collective-permute-done.7.refs_1_ = f32[192,128]{1,0:T(8,128)S(1)} collective-permute-done((f32[192,128]{1,0:T(8,128)S(1)}, f32[192,128]{1,0:T(8,128)S(1)}, u32[]{:S(2)}, u32[]{:S(2)}) %collective-permute-start.7) | collective-permute-done | bytes 98336 | tf_op jit(solution)/shard_map/ppermute | solution.py:345
  67.6 1.6 %collective-permute-start.8 = (f32[192,128]{1,0:T(8,128)S(1)}, f32[192,128]{1,0:T(8,128)S(1)}, u32[]{:S(2)}, u32[]{:S(2)}) collective-permute-start(f32[192,128]{1,0:T(8,128)S(1)} %shard_map.109.refs_0_), channel_id=1, source_target_pairs={{0,1},{1,0},{2,3},{3,2},{4,5},{5,4},{6,7},{7,6},{8,9},{9,8},{10,11... | collective-permute-start | bytes 294920 | tf_op jit(solution)/shard_map/ppermute | solution.py:345
  69.2 2.0 %collective-permute-start.10 = (f32[192,128]{1,0:T(8,128)S(1)}, f32[192,128]{1,0:T(8,128)S(1)}, u32[]{:S(2)}, u32[]{:S(2)}) collective-permute-start(f32[192,128]{1,0:T(8,128)S(1)} %shard_map.109.refs_0_), channel_id=1, source_target_pairs={{0,3},{1,2},{2,1},{3,0},{4,7},{5,6},{6,5},{7,4},{8,11},{9,10},{10,... | collective-permute-start | bytes 294920 | tf_op jit(solution)/shard_map/ppermute | solution.py:345
  71.2 1.6 %collective-permute-start.12 = (f32[192,128]{1,0:T(8,128)S(1)}, f32[192,128]{1,0:T(8,128)S(1)}, u32[]{:S(2)}, u32[]{:S(2)}) collective-permute-start(f32[192,128]{1,0:T(8,128)S(1)} %shard_map.110.refs_4_), channel_id=1, source_target_pairs={{0,1},{1,0},{2,3},{3,2},{4,5},{5,4},{6,7},{7,6},{8,9},{9,8},{10,11... | collective-permute-start | bytes 294920 | tf_op jit(solution)/shard_map/ppermute | solution.py:345
  72.8 1.4 %collective-permute-done.8.refs_1_ = f32[192,128]{1,0:T(8,128)S(1)} collective-permute-done((f32[192,128]{1,0:T(8,128)S(1)}, f32[192,128]{1,0:T(8,128)S(1)}, u32[]{:S(2)}, u32[]{:S(2)}) %collective-permute-start.8) | collective-permute-done | bytes 98336 | tf_op jit(solution)/shard_map/ppermute | solution.py:345
  74.4 2.3 %collective-permute-start.14 = (f32[192,128]{1,0:T(8,128)S(1)}, f32[192,128]{1,0:T(8,128)S(1)}, u32[]{:S(2)}, u32[]{:S(2)}) collective-permute-start(f32[192,128]{1,0:T(8,128)S(1)} %shard_map.110.refs_4_), channel_id=1, source_target_pairs={{0,3},{1,2},{2,1},{3,0},{4,7},{5,6},{6,5},{7,4},{8,11},{9,10},{10,... | collective-permute-start | bytes 294920 | tf_op jit(solution)/shard_map/ppermute | solution.py:345
  77.0 1.0 collective-permute-done.12.refs_5_
  77.9 0.9 collective-permute-done.13.refs_6_
  78.8 1.5 %collective-permute-done.14.refs_7_ = f32[192,128]{1,0:T(8,128)S(1)} collective-permute-done((f32[192,128]{1,0:T(8,128)S(1)}, f32[192,128]{1,0:T(8,128)S(1)}, u32[]{:S(2)}, u32[]{:S(2)}) %collective-permute-start.14) | collective-permute-done | bytes 98336 | tf_op jit(solution)/shard_map/ppermute | solution.py:345
  80.4 4.6 %shard_map.111 = (f32[1,1]{1,0:T(1,128)S(1)}, f32[1,1]{1,0:T(1,128)}, f32[96,256]{1,0:T(8,128)S(1)}, f32[96,128]{1,0:T(8,128)S(1)}, f32[192,128]{1,0:T(8,128)S(1...) custom-call(s32[1]{0:T(128)} %bitcast.me_ref, ...), custom_call_target="tpu_custom_call" | custom-call | tf_op jit(solution)/shard_map/pallas_call | solution.py:349
  85.0 1.9 %collective-permute-start.15 = (f32[192,128]{1,0:T(8,128)S(1)}, f32[192,128]{1,0:T(8,128)S(1)}, u32[]{:S(2)}, u32[]{:S(2)}) collective-permute-start(f32[192,128]{1,0:T(8,128)S(1)} %get-tuple-element.59), channel_id=1, source_target_pairs={{0,3},{1,2},{2,1},{3,0},{4,7},{5,6},{6,5},{7,4},{8,11},{9,10},{10,... | collective-permute-start | bytes 294920 | tf_op jit(solution)/shard_map/ppermute | solution.py:345
  87.5 1.0 collective-permute-start.17
  88.6 1.9 %collective-permute-start.18 = (f32[192,128]{1,0:T(8,128)S(1)}, f32[192,128]{1,0:T(8,128)S(1)}, u32[]{:S(2)}, u32[]{:S(2)}) collective-permute-start(f32[192,128]{1,0:T(8,128)S(1)} %get-tuple-element.64), channel_id=1, source_target_pairs={{0,3},{1,2},{2,1},{3,0},{4,7},{5,6},{6,5},{7,4},{8,11},{9,10},{10,... | collective-permute-start | bytes 294920 | tf_op jit(solution)/shard_map/ppermute | solution.py:345
  90.4 0.7 collective-permute-done.15.refs_1_
  91.1 1.0 collective-permute-start.19
  92.1 1.0 collective-permute-start.20
  93.1 0.6 shard_map.113
  93.8 2.1 %collective-permute-start.21 = (f32[96,128]{1,0:T(8,128)}, f32[96,128]{1,0:T(8,128)}, u32[]{:S(2)}, u32[]{:S(2)}) collective-permute-start(f32[96,128]{1,0:T(8,128)} %get-tuple-element.68), channel_id=1, source_target_pairs={{0,4},{1,5},{2,6},{3,7},{4,0},{5,1},{6,2},{7,3},{8,12},{9,13},{10,... | collective-permute-start | bytes 147464 | tf_op jit(solution)/shard_map/ppermute | solution.py:345
  96.7 0.6 shard_map.114
  97.4 0.6 copy-done.9
  98.0 2.4 %collective-permute-start.22 = (f32[96,128]{1,0:T(8,128)}, f32[96,128]{1,0:T(8,128)}, u32[]{:S(2)}, u32[]{:S(2)}) collective-permute-start(f32[96,128]{1,0:T(8,128)} %get-tuple-element.69), channel_id=1, source_target_pairs={{0,4},{1,5},{2,6},{3,7},{4,0},{5,1},{6,2},{7,3},{8,12},{9,13},{10,... | collective-permute-start | bytes 147464 | tf_op jit(solution)/shard_map/ppermute | solution.py:345
  100.3 1.0 shard_map.112.onto_ref
  101.4 1.9 %collective-permute-done.22.refs_3_ = f32[96,128]{1,0:T(8,128)} collective-permute-done((f32[96,128]{1,0:T(8,128)}, f32[96,128]{1,0:T(8,128)}, u32[]{:S(2)}, u32[]{:S(2)}) %collective-permute-start.22) | collective-permute-done | bytes 49184 | tf_op jit(solution)/shard_map/ppermute | solution.py:345
  103.3 0.9 copy-done.2
  104.2 0.9 copy-done.4
  105.1 0.8 copy-done.6
  105.9 0.8 copy-done.8
  106.7 0.8 copy-done.10
  107.5 2.6 %shard_map.115 = f32[96,768]{1,0:T(8,128)} custom-call(f32[96,128]{1,0:T(8,128)S(1)} %copy-done.6, bf16[768,768]{1,0:T(8,128)(2,1)S(1)} %shard_map.112.onto_ref, f32[1,1]{1,0:T(1,128)S(1)} %get-tuple-element.54.energy_ref, f32[1,1]{1,0:T(1,128)} %get-tuple-element.55.spread_ref, f32[96,256]{1,0:T(8,128)S(1)} %copy-done.2, f32[96,256]{1,0:T(8,128)S(1)} %copy-done.4, ...), custom_call_target="tpu_custom_call" | custom-call | tf_op jit(solution)/shard_map/pallas_call | solution.py:349
  110.1 2.6 %shard_map.116 = f32[768,768]{1,0:T(8,128)} custom-call(s32[1]{0:T(128)} %bitcast.6.segment_ref, f32[768,768]{1,0:T(8,128)} %bitcast.20, f32[768,768]{1,0:T(8,128)} %collective-permute-done.23.shifted_ref), custom_call_target="tpu_custom_call" | custom-call | tf_op jit(solution)/shard_map/pallas_call | solution.py:484
  (42 shorter events, 2.5 us)
Async XLA Ops:
  0.6 32.6 %copy-start = (f32[1,768,768]{2,1,0:T(8,128)S(1)}, f32[1,768,768]{2,1,0:T(8,128)}, u32[]{:S(2)}) copy-start(f32[1,768,768]{2,1,0:T(8,128)} %param.11) | copy-start | bytes 7077892
  2.5 9.0 %collective-permute-start = (f32[96,256]{1,0:T(8,128)S(1)}, f32[96,256]{1,0:T(8,128)S(1)}, u32[]{:S(2)}, u32[]{:S(2)}) collective-permute-start(f32[96,256]{1,0:T(8,128)S(1)} %shard_map.104.first_ref), channel_id=1, source_target_pairs={{0,4},{1,5},{2,6},{3,7},{4,0},{5,1},{6,2},{7,3},{8,12},{9,13},{10,... | collective-permute-start | bytes 294920 | tf_op jit(solution)/shard_map/ppermute | solution.py:345
  11.5 16.7 %collective-permute-start.1 = (f32[192,256]{1,0:T(8,128)S(1)}, f32[192,256]{1,0:T(8,128)S(1)}, u32[]{:S(2)}, u32[]{:S(2)}) collective-permute-start(f32[192,256]{1,0:T(8,128)S(1)} %shard_map.105.refs_0_), channel_id=1, source_target_pairs={{0,1},{1,0},{2,3},{3,2},{4,5},{5,4},{6,7},{7,6},{8,9},{9,8},{10,11... | collective-permute-start | bytes 589832 | tf_op jit(solution)/shard_map/ppermute | solution.py:345
  13.2 15.1 %collective-permute-start.2 = (f32[192,256]{1,0:T(8,128)S(1)}, f32[192,256]{1,0:T(8,128)S(1)}, u32[]{:S(2)}, u32[]{:S(2)}) collective-permute-start(f32[192,256]{1,0:T(8,128)S(1)} %shard_map.105.refs_0_), channel_id=1, source_target_pairs={{0,2},{1,3},{2,0},{3,1},{4,6},{5,7},{6,4},{7,5},{8,10},{9,11},{10,... | collective-permute-start | bytes 589832 | tf_op jit(solution)/shard_map/ppermute | solution.py:345
  13.8 14.5 %collective-permute-start.3 = (f32[192,256]{1,0:T(8,128)S(1)}, f32[192,256]{1,0:T(8,128)S(1)}, u32[]{:S(2)}, u32[]{:S(2)}) collective-permute-start(f32[192,256]{1,0:T(8,128)S(1)} %shard_map.105.refs_0_), channel_id=1, source_target_pairs={{0,3},{1,2},{2,1},{3,0},{4,7},{5,6},{6,5},{7,4},{8,11},{9,10},{10,... | collective-permute-start | bytes 589832 | tf_op jit(solution)/shard_map/ppermute | solution.py:345
  20.2 8.1 %copy-start.11 = (f32[16]{0:T(128)S(1)}, f32[16]{0:T(128)}, u32[]{:S(2)}) copy-start(f32[16]{0:T(128)} %table_ref.3) | copy-start | bytes 196
  28.3 4.9 %copy-start.12 = (f32[1,1,768,768]{3,2,1,0:T(8,128)S(1)}, f32[1,1,768,768]{3,2,1,0:T(8,128)}, u32[]{:S(2)}) copy-start(f32[1,1,768,768]{3,2,1,0:T(8,128)} %param.8) | copy-start | bytes 7077892
  33.2 3.1 %copy-start.1 = (f32[96,256]{1,0:T(8,128)}, f32[96,256]{1,0:T(8,128)S(1)}, u32[]{:S(2)}) copy-start(f32[96,256]{1,0:T(8,128)S(1)} %get-tuple-element.56.initial_ref) | copy-start | bytes 294916
  41.1 69.0 %collective-permute-start.23 = (f32[768,768]{1,0:T(8,128)}, f32[768,768]{1,0:T(8,128)}, u32[]{:S(2)}, u32[]{:S(2)}) collective-permute-start(f32[768,768]{1,0:T(8,128)} %fusion.4), channel_id=1, source_target_pairs={{0,8},{8,16},{16,24},{1,9},{9,17},{17,25},{2,10},{10,18},{18,26},{... | collective-permute-start | bytes 7077896 | tf_op jit(solution)/shard_map/ppermute | solution.py:332
  43.8 8.6 %collective-permute-start.4 = (f32[192,256]{1,0:T(8,128)S(1)}, f32[192,256]{1,0:T(8,128)S(1)}, u32[]{:S(2)}, u32[]{:S(2)}) collective-permute-start(f32[192,256]{1,0:T(8,128)S(1)} %get-tuple-element.47), channel_id=1, source_target_pairs={{0,3},{1,2},{2,1},{3,0},{4,7},{5,6},{6,5},{7,4},{8,11},{9,10},{10,... | collective-permute-start | bytes 589832 | tf_op jit(solution)/shard_map/ppermute | solution.py:345
  45.5 11.2 %collective-permute-start.5 = (f32[192,256]{1,0:T(8,128)S(1)}, f32[192,256]{1,0:T(8,128)S(1)}, u32[]{:S(2)}, u32[]{:S(2)}) collective-permute-start(f32[192,256]{1,0:T(8,128)S(1)} %get-tuple-element.48), channel_id=1, source_target_pairs={{0,2},{1,3},{2,0},{3,1},{4,6},{5,7},{6,4},{7,5},{8,10},{9,11},{10,... | collective-permute-start | bytes 589832 | tf_op jit(solution)/shard_map/ppermute | solution.py:345
  46.8 9.9 %collective-permute-start.6 = (f32[192,256]{1,0:T(8,128)S(1)}, f32[192,256]{1,0:T(8,128)S(1)}, u32[]{:S(2)}, u32[]{:S(2)}) collective-permute-start(f32[192,256]{1,0:T(8,128)S(1)} %get-tuple-element.49), channel_id=1, source_target_pairs={{0,1},{1,0},{2,3},{3,2},{4,5},{5,4},{6,7},{7,6},{8,9},{9,8},{10,11... | collective-permute-start | bytes 589832 | tf_op jit(solution)/shard_map/ppermute | solution.py:345
  56.8 10.8 %collective-permute-start.7 = (f32[192,128]{1,0:T(8,128)S(1)}, f32[192,128]{1,0:T(8,128)S(1)}, u32[]{:S(2)}, u32[]{:S(2)}) collective-permute-start(f32[192,128]{1,0:T(8,128)S(1)} %get-tuple-element.50.refs_0_), channel_id=1, source_target_pairs={{0,4},{1,5},{2,6},{3,7},{4,0},{5,1},{6,2},{7,3},{8,12},{9,13},{10,... | collective-permute-start | bytes 294920 | tf_op jit(solution)/shard_map/ppermute | solution.py:345
  59.0 12.2 %collective-permute-start.11 = (f32[192,128]{1,0:T(8,128)S(1)}, f32[192,128]{1,0:T(8,128)S(1)}, u32[]{:S(2)}, u32[]{:S(2)}) collective-permute-start(f32[192,128]{1,0:T(8,128)S(1)} %get-tuple-element.51.refs_0_), channel_id=1, source_target_pairs={{0,4},{1,5},{2,6},{3,7},{4,0},{5,1},{6,2},{7,3},{8,12},{9,13},{10,... | collective-permute-start | bytes 294920 | tf_op jit(solution)/shard_map/ppermute | solution.py:345
  67.6 6.6 %collective-permute-start.8 = (f32[192,128]{1,0:T(8,128)S(1)}, f32[192,128]{1,0:T(8,128)S(1)}, u32[]{:S(2)}, u32[]{:S(2)}) collective-permute-start(f32[192,128]{1,0:T(8,128)S(1)} %shard_map.109.refs_0_), channel_id=1, source_target_pairs={{0,1},{1,0},{2,3},{3,2},{4,5},{5,4},{6,7},{7,6},{8,9},{9,8},{10,11... | collective-permute-start | bytes 294920 | tf_op jit(solution)/shard_map/ppermute | solution.py:345
  69.2 5.2 %collective-permute-start.9 = (f32[192,128]{1,0:T(8,128)S(1)}, f32[192,128]{1,0:T(8,128)S(1)}, u32[]{:S(2)}, u32[]{:S(2)}) collective-permute-start(f32[192,128]{1,0:T(8,128)S(1)} %shard_map.109.refs_0_), channel_id=1, source_target_pairs={{0,2},{1,3},{2,0},{3,1},{4,6},{5,7},{6,4},{7,5},{8,10},{9,11},{10,... | collective-permute-start | bytes 294920 | tf_op jit(solution)/shard_map/ppermute | solution.py:345
  69.2 7.8 %collective-permute-start.10 = (f32[192,128]{1,0:T(8,128)S(1)}, f32[192,128]{1,0:T(8,128)S(1)}, u32[]{:S(2)}, u32[]{:S(2)}) collective-permute-start(f32[192,128]{1,0:T(8,128)S(1)} %shard_map.109.refs_0_), channel_id=1, source_target_pairs={{0,3},{1,2},{2,1},{3,0},{4,7},{5,6},{6,5},{7,4},{8,11},{9,10},{10,... | collective-permute-start | bytes 294920 | tf_op jit(solution)/shard_map/ppermute | solution.py:345
  71.2 6.7 %collective-permute-start.12 = (f32[192,128]{1,0:T(8,128)S(1)}, f32[192,128]{1,0:T(8,128)S(1)}, u32[]{:S(2)}, u32[]{:S(2)}) collective-permute-start(f32[192,128]{1,0:T(8,128)S(1)} %shard_map.110.refs_4_), channel_id=1, source_target_pairs={{0,1},{1,0},{2,3},{3,2},{4,5},{5,4},{6,7},{7,6},{8,9},{9,8},{10,11... | collective-permute-start | bytes 294920 | tf_op jit(solution)/shard_map/ppermute | solution.py:345
  74.2 4.6 %collective-permute-start.13 = (f32[192,128]{1,0:T(8,128)S(1)}, f32[192,128]{1,0:T(8,128)S(1)}, u32[]{:S(2)}, u32[]{:S(2)}) collective-permute-start(f32[192,128]{1,0:T(8,128)S(1)} %shard_map.110.refs_4_), channel_id=1, source_target_pairs={{0,2},{1,3},{2,0},{3,1},{4,6},{5,7},{6,4},{7,5},{8,10},{9,11},{10,... | collective-permute-start | bytes 294920 | tf_op jit(solution)/shard_map/ppermute | solution.py:345
  74.4 6.0 %collective-permute-start.14 = (f32[192,128]{1,0:T(8,128)S(1)}, f32[192,128]{1,0:T(8,128)S(1)}, u32[]{:S(2)}, u32[]{:S(2)}) collective-permute-start(f32[192,128]{1,0:T(8,128)S(1)} %shard_map.110.refs_4_), channel_id=1, source_target_pairs={{0,3},{1,2},{2,1},{3,0},{4,7},{5,6},{6,5},{7,4},{8,11},{9,10},{10,... | collective-permute-start | bytes 294920 | tf_op jit(solution)/shard_map/ppermute | solution.py:345
  85.0 13.0 %copy-start.3 = (f32[96,256]{1,0:T(8,128)}, f32[96,256]{1,0:T(8,128)S(1)}, u32[]{:S(2)}) copy-start(f32[96,256]{1,0:T(8,128)S(1)} %get-tuple-element.57.step_ref) | copy-start | bytes 294916
  85.0 15.4 %copy-start.5 = (f32[96,128]{1,0:T(8,128)}, f32[96,128]{1,0:T(8,128)S(1)}, u32[]{:S(2)}) copy-start(f32[96,128]{1,0:T(8,128)S(1)} %get-tuple-element.53.spot_ref) | copy-start | bytes 147460
  85.0 6.1 %collective-permute-start.15 = (f32[192,128]{1,0:T(8,128)S(1)}, f32[192,128]{1,0:T(8,128)S(1)}, u32[]{:S(2)}, u32[]{:S(2)}) collective-permute-start(f32[192,128]{1,0:T(8,128)S(1)} %get-tuple-element.59), channel_id=1, source_target_pairs={{0,3},{1,2},{2,1},{3,0},{4,7},{5,6},{6,5},{7,4},{8,11},{9,10},{10,... | collective-permute-start | bytes 294920 | tf_op jit(solution)/shard_map/ppermute | solution.py:345
  86.9 5.2 %collective-permute-start.16 = (f32[192,128]{1,0:T(8,128)S(1)}, f32[192,128]{1,0:T(8,128)S(1)}, u32[]{:S(2)}, u32[]{:S(2)}) collective-permute-start(f32[192,128]{1,0:T(8,128)S(1)} %get-tuple-element.60), channel_id=1, source_target_pairs={{0,2},{1,3},{2,0},{3,1},{4,6},{5,7},{6,4},{7,5},{8,10},{9,11},{10,... | collective-permute-start | bytes 294920 | tf_op jit(solution)/shard_map/ppermute | solution.py:345
  87.5 5.6 %collective-permute-start.17 = (f32[192,128]{1,0:T(8,128)S(1)}, f32[192,128]{1,0:T(8,128)S(1)}, u32[]{:S(2)}, u32[]{:S(2)}) collective-permute-start(f32[192,128]{1,0:T(8,128)S(1)} %get-tuple-element.61), channel_id=1, source_target_pairs={{0,1},{1,0},{2,3},{3,2},{4,5},{5,4},{6,7},{7,6},{8,9},{9,8},{10,11... | collective-permute-start | bytes 294920 | tf_op jit(solution)/shard_map/ppermute | solution.py:345
  88.6 7.4 %collective-permute-start.18 = (f32[192,128]{1,0:T(8,128)S(1)}, f32[192,128]{1,0:T(8,128)S(1)}, u32[]{:S(2)}, u32[]{:S(2)}) collective-permute-start(f32[192,128]{1,0:T(8,128)S(1)} %get-tuple-element.64), channel_id=1, source_target_pairs={{0,3},{1,2},{2,1},{3,0},{4,7},{5,6},{6,5},{7,4},{8,11},{9,10},{10,... | collective-permute-start | bytes 294920 | tf_op jit(solution)/shard_map/ppermute | solution.py:345
  91.1 5.1 %collective-permute-start.19 = (f32[192,128]{1,0:T(8,128)S(1)}, f32[192,128]{1,0:T(8,128)S(1)}, u32[]{:S(2)}, u32[]{:S(2)}) collective-permute-start(f32[192,128]{1,0:T(8,128)S(1)} %get-tuple-element.65), channel_id=1, source_target_pairs={{0,2},{1,3},{2,0},{3,1},{4,6},{5,7},{6,4},{7,5},{8,10},{9,11},{10,... | collective-permute-start | bytes 294920 | tf_op jit(solution)/shard_map/ppermute | solution.py:345
  92.1 4.6 %collective-permute-start.20 = (f32[192,128]{1,0:T(8,128)S(1)}, f32[192,128]{1,0:T(8,128)S(1)}, u32[]{:S(2)}, u32[]{:S(2)}) collective-permute-start(f32[192,128]{1,0:T(8,128)S(1)} %get-tuple-element.66), channel_id=1, source_target_pairs={{0,1},{1,0},{2,3},{3,2},{4,5},{5,4},{6,7},{7,6},{8,9},{9,8},{10,11... | collective-permute-start | bytes 294920 | tf_op jit(solution)/shard_map/ppermute | solution.py:345
  93.8 6.6 %copy-start.7 = (f32[96,128]{1,0:T(8,128)}, f32[96,128]{1,0:T(8,128)S(1)}, u32[]{:S(2)}) copy-start(f32[96,128]{1,0:T(8,128)S(1)} %get-tuple-element.62.refs_0_) | copy-start | bytes 147460
  93.8 7.6 %collective-permute-start.21 = (f32[96,128]{1,0:T(8,128)}, f32[96,128]{1,0:T(8,128)}, u32[]{:S(2)}, u32[]{:S(2)}) collective-permute-start(f32[96,128]{1,0:T(8,128)} %get-tuple-element.68), channel_id=1, source_target_pairs={{0,4},{1,5},{2,6},{3,7},{4,0},{5,1},{6,2},{7,3},{8,12},{9,13},{10,... | collective-permute-start | bytes 147464 | tf_op jit(solution)/shard_map/ppermute | solution.py:345
  97.4 0.6 copy-start.9
  98.0 5.3 %collective-permute-start.22 = (f32[96,128]{1,0:T(8,128)}, f32[96,128]{1,0:T(8,128)}, u32[]{:S(2)}, u32[]{:S(2)}) collective-permute-start(f32[96,128]{1,0:T(8,128)} %get-tuple-element.69), channel_id=1, source_target_pairs={{0,4},{1,5},{2,6},{3,7},{4,0},{5,1},{6,2},{7,3},{8,12},{9,13},{10,... | collective-permute-start | bytes 147464 | tf_op jit(solution)/shard_map/ppermute | solution.py:345
  103.3 0.9 copy-start.2
  104.2 0.9 copy-start.4
  105.1 0.8 copy-start.6
  105.9 0.8 copy-start.8
  106.7 0.8 copy-start.10

commit v3 on v2

--- a/solution.py
+++ b/solution.py
@@ -310,19 +310,23 @@
     steps = arrived.shape[0]
     rows = own_ref.shape[0] // steps
     parts = [slice(q * rows, (q + 1) * rows) for q in range(steps)]
-    outs = [pltpu.make_async_copy(held.at[p], out_ref.at[p], left.at[q]) for q, p in enumerate(parts)]
-
-    def through(source):
-        ins = [pltpu.make_async_copy(source.at[p], held.at[p], arrived.at[q]) for q, p in enumerate(parts)]
+
+    @pl.when(segment_ref[0] == 0)
+    def _():
+        ins = [pltpu.make_async_copy(own_ref.at[p], held.at[p], arrived.at[q]) for q, p in enumerate(parts)]
+        outs = [pltpu.make_async_copy(held.at[p], out_ref.at[p], left.at[q]) for q, p in enumerate(parts)]
         for copy in ins:
             copy.start()
         for come, go in zip(ins, outs):
             come.wait()
             go.start()
-
-    pl.when(segment_ref[0] == 0)(lambda: through(own_ref))
-    pl.when(segment_ref[0] != 0)(lambda: through(shifted_ref))
-    for copy in outs:
+        for copy in outs:
+            copy.wait()
+
+    @pl.when(segment_ref[0] != 0)
+    def _():
+        copy = pltpu.make_async_copy(shifted_ref, out_ref, left.at[0])
+        copy.start()
         copy.wait()
 
 
@@ -379,6 +383,8 @@
     count = lax.axis_size("op")
     group = count // 2
     me = jnp.reshape(lax.axis_index("op").astype(jnp.int32), (1,))
+    segment = jnp.reshape(lax.axis_index("seg").astype(jnp.int32), (1,))
+    me, segment = lax.optimization_barrier((me, segment))
 
     (packed,) = call(
         pack_kernel,
@@ -480,10 +486,9 @@
         basis_rotation[0], half_turn, (((0,), (0,)), ((), ())), precision=lax.Precision.HIGH
     )
     shifted = passed_along(far(rotated), "seg", 1)
-    segment = jnp.reshape(lax.axis_index("seg").astype(jnp.int32), (1,))
     handed = pl.pallas_call(
         choose_kernel,
-        in_specs=[SMEM, HBM, HBM],
+        in_specs=[SMEM, HBM, VMEM],
         out_specs=HBM,
         out_shape=jax.ShapeDtypeStruct((size, size), F32),
         scratch_shapes=[
@@ -492,7 +497,7 @@
             pltpu.SemaphoreType.DMA((4 * NQ,)),
         ],
         compiler_params=SMALL,
-    )(segment, far(own_left), far(shifted))[None, None]
+    )(segment, far(own_left), near(shifted))[None, None]
     return (chebyshev[None], energy[0], handed)
 
 

time: 114 us -> 106 us (0.930)
  local copies, waits for them, and re-layouts: 4.83 us -> 0.02 us
  Pallas kernels: 31.5 us -> 29.5 us
  starting transfers between devices: 36.3 us -> 34.6 us
  matrix products: 7.81 us -> 6.64 us
    unnamed x26 -> x6, local copies, waits for them, and re-layouts: 4.83 us -> 0.02 us
    pallas_call x11, Pallas kernels: 16.3 us -> 14.3 us  [call(): pl.pallas_call(kernel, in_specs=ins, out_specs=[VMEM] * len(outs), out_sh...]
    dot_general x1, matrix products: 4.71 us -> 3.55 us  [all_steps(): lax.dot_general(basis_rotation[0], half_turn, (((0,), (0,)), ((), ())), p...]
where the time goes in v3:
time: 106 us; the launch traced here: 105 us
  starting transfers between devices  34.6 us (33%)
  waiting for transfers between devices  31.8 us (30%)
  Pallas kernels  29.5 us (28%)
  matrix products  6.64 us (6%)
  between operations  2.64 us (2%)
    ppermute x23, starting transfers between devices, swapped(): lax.ppermute(value, axis, [(source, source ^ mask) for source in range(co...  32.9 us
    ppermute x23, waiting for transfers between devices, swapped(): lax.ppermute(value, axis, [(source, source ^ mask) for source in range(co...  31.8 us
    pallas_call x11, Pallas kernels, call(): pl.pallas_call(kernel, in_specs=ins, out_specs=[VMEM] * len(outs), out_sh...  14.3 us
    pallas_call x1, Pallas kernels, sort_rest(): pl.pallas_call(sort_kernel, grid=(NQ,), in_specs=[VMEM] * 4 + [pl.BlockSp...  8.04 us
    pallas_call x1, Pallas kernels, sort_columns(): pl.pallas_call(columns_kernel, grid=(NQ,), in_specs=[VMEM, pl.BlockSpec((...  4.45 us
    dot_general x1, matrix products, all_steps(): lax.dot_general(basis_rotation[0], half_turn, (((0,), (0,)), ((), ())), p...  3.55 us
    dot_general x1, matrix products, all_steps(): jnp.dot(turned_left, basis_rotation[0], precision=lax.Precision.HIGH)  3.09 us
    pallas_call x1, Pallas kernels, all_steps(): pl.pallas_call(choose_kernel, in_specs=[SMEM, HBM, VMEM], out_specs=HBM,...  2.62 us
  transfers between devices with their start and end apart: 24, of which 14 were waited for; matrix products, arithmetic and copies ran while one was open for 0% of the time, Pallas kernels for 19%

profile of v3, /device:TPU:0, one launch (start us, length us, event | category | flops | bytes accessed | tf_op | source)
XLA Modules:
  0.0 105.2 jit_solution(1881117689953846192)
XLA Ops:
  0.6 0.0 copy-start
  0.7 1.8 %shard_map.104.first_ref = f32[96,256]{1,0:T(8,128)S(1)} custom-call(s32[1]{0:T(128)} %bitcast.me_ref, s32[1,768]{1,0:T(1,128)} %left_hbm.1, s32[1,768]{1,0:T(1,128)} %charge_ref.5, f32[96,768]{1,0:T(8,128)} %bitcast.25), custom_call_target="tpu_custom_call" | custom-call | tf_op jit(solution)/shard_map/pallas_call | solution.py:353
  2.5 4.1 %collective-permute-start = (f32[96,256]{1,0:T(8,128)S(1)}, f32[96,256]{1,0:T(8,128)S(1)}, u32[]{:S(2)}, u32[]{:S(2)}) collective-permute-start(f32[96,256]{1,0:T(8,128)S(1)} %shard_map.104.first_ref), channel_id=1, source_target_pairs={{0,4},{1,5},{2,6},{3,7},{4,0},{5,1},{6,2},{7,3},{8,12},{9,13},{10,... | collective-permute-start | bytes 294920 | tf_op jit(solution)/shard_map/ppermute | solution.py:349
  6.6 4.9 %collective-permute-done.second_ref = f32[96,256]{1,0:T(8,128)S(1)} collective-permute-done((f32[96,256]{1,0:T(8,128)S(1)}, f32[96,256]{1,0:T(8,128)S(1)}, u32[]{:S(2)}, u32[]{:S(2)}) %collective-permute-start) | collective-permute-done | bytes 98336 | tf_op jit(solution)/shard_map/ppermute | solution.py:349
  11.5 1.6 %collective-permute-start.1 = (f32[192,256]{1,0:T(8,128)S(1)}, f32[192,256]{1,0:T(8,128)S(1)}, u32[]{:S(2)}, u32[]{:S(2)}) collective-permute-start(f32[192,256]{1,0:T(8,128)S(1)} %shard_map.105.refs_0_), channel_id=1, source_target_pairs={{0,1},{1,0},{2,3},{3,2},{4,5},{5,4},{6,7},{7,6},{8,9},{9,8},{10,11... | collective-permute-start | bytes 589832 | tf_op jit(solution)/shard_map/ppermute | solution.py:349
  13.2 0.7 collective-permute-start.2
  13.8 1.3 %collective-permute-start.3 = (f32[192,256]{1,0:T(8,128)S(1)}, f32[192,256]{1,0:T(8,128)S(1)}, u32[]{:S(2)}, u32[]{:S(2)}) collective-permute-start(f32[192,256]{1,0:T(8,128)S(1)} %shard_map.105.refs_0_), channel_id=1, source_target_pairs={{0,3},{1,2},{2,1},{3,0},{4,7},{5,6},{6,5},{7,4},{8,11},{9,10},{10,... | collective-permute-start | bytes 589832 | tf_op jit(solution)/shard_map/ppermute | solution.py:349
  15.8 4.5 %shard_map.103 = (bf16[768,768]{1,0:T(8,128)(2,1)S(1)}, bf16[768,768]{1,0:T(8,128)(2,1)S(1)}, bf16[768,768]{1,0:T(8,128)(2,1)S(1)}, bf16[768,768]{1,0:T(8,128)(2,1)S(1)}, f32[768,128]{1,0:T(8,128)S(1)}) custom-call(s32[1,768]{1,0:T(1,128)} %left_hbm.1, f32[768,768]{1,0:T(8,128)} %bitcast.19), custom_call_target="tpu_custom_call" | custom-call | tf_op jit(solution)/shard_map/pallas_call | solution.py:160
  20.2 8.0 %shard_map.106 = (bf16[768,768]{1,0:T(8,128)(2,1)S(1)}, bf16[768,768]{1,0:T(8,128)(2,1)S(1)}, bf16[768,768]{1,0:T(8,128)(2,1)S(1)}, bf16[768,768]{1,0:T(8,128)(2,1)S(1)}) custom-call(s32[1,768]{1,0:T(1,128)} %charge_ref.5, bf16[768,768]{1,0:T(8,128)(2,1)S(1)} %get-tuple-element.43.left_half_high, bf16[768,768]{1,0:T(8,128)(2,1)S(1)} %get-tuple-element.44.left_half_low, ...), custom_call_target="tpu_custom_call" | custom-call | tf_op jit(solution)/shard_map/pallas_call | solution.py:173
  28.3 4.9 %shard_map.107 = (f32[768,256]{1,0:T(8,128)S(1)}, f32[96,256]{1,0:T(8,128)S(1)}, f32[192,256]{1,0:T(8,128)S(1)}, f32[192,256]{1,0:T(8,128)S(1)}, f32[192,256]{1,0:T(8,128)S(1)}, /*index=5*/f32[192,256]{1,0:T(8,128)S(1)}) custom-call(s32[1]{0:T(128)} %bitcast.me_ref, s32[1,1]{1,0:T(1,128)S(6)} %copy.14.term_ref, f32[16]{0:T(128)S(1)} %copy-done.1, ...), custom_call_target="tpu_custom_call" | custom-call | tf_op jit(solution)/shard_map/pallas_call | solution.py:353
  33.3 3.1 %fusion.2 = f32[768,768]{1,0:T(8,128)S(1)} fusion(f32[768,768]{1,0:T(8,128)S(1)} %bitcast.21, f32[1,768,768]{2,1,0:T(8,128)S(1)} %copy-done), kind=kOutput, calls=%fused_computation.2 | convolution fusion | flops 2717908992 | bytes 7077888 | tf_op jit(solution)/shard_map/dot_general | solution.py:484
  36.4 3.5 %fusion.4 = f32[768,768]{1,0:T(8,128)S(1)} fusion(f32[768,768]{1,0:T(8,128)S(1)} %fusion.2, f32[1,768,768]{2,1,0:T(8,128)S(1)} %copy-done), kind=kOutput, calls=%fused_computation.4 | convolution fusion | flops 2717908992 | bytes 7077888 | tf_op jit(solution)/shard_map/dot_general | solution.py:485
  39.9 1.7 %collective-permute-start.23 = (f32[768,768]{1,0:T(8,128)S(1)}, f32[768,768]{1,0:T(8,128)S(1)}, u32[]{:S(2)}, u32[]{:S(2)}) collective-permute-start(f32[768,768]{1,0:T(8,128)S(1)} %fusion.4), channel_id=1, source_target_pairs={{0,8},{8,16},{16,24},{1,9},{9,17},{17,25},{2,10},{10,18},{18,26},{... | collective-permute-start | bytes 7077896 | tf_op jit(solution)/shard_map/ppermute | solution.py:336
  41.6 1.7 %collective-permute-start.4 = (f32[192,256]{1,0:T(8,128)S(1)}, f32[192,256]{1,0:T(8,128)S(1)}, u32[]{:S(2)}, u32[]{:S(2)}) collective-permute-start(f32[192,256]{1,0:T(8,128)S(1)} %get-tuple-element.50), channel_id=1, source_target_pairs={{0,3},{1,2},{2,1},{3,0},{4,7},{5,6},{6,5},{7,4},{8,11},{9,10},{10,... | collective-permute-start | bytes 589832 | tf_op jit(solution)/shard_map/ppermute | solution.py:349
  43.3 1.3 %collective-permute-start.5 = (f32[192,256]{1,0:T(8,128)S(1)}, f32[192,256]{1,0:T(8,128)S(1)}, u32[]{:S(2)}, u32[]{:S(2)}) collective-permute-start(f32[192,256]{1,0:T(8,128)S(1)} %get-tuple-element.51), channel_id=1, source_target_pairs={{0,2},{1,3},{2,0},{3,1},{4,6},{5,7},{6,4},{7,5},{8,10},{9,11},{10,... | collective-permute-start | bytes 589832 | tf_op jit(solution)/shard_map/ppermute | solution.py:349
  44.6 0.5 collective-permute-start.6
  45.1 4.1 %collective-permute-done.4.refs_1_ = f32[192,256]{1,0:T(8,128)S(1)} collective-permute-done((f32[192,256]{1,0:T(8,128)S(1)}, f32[192,256]{1,0:T(8,128)S(1)}, u32[]{:S(2)}, u32[]{:S(2)}) %collective-permute-start.4) | collective-permute-done | bytes 196640 | tf_op jit(solution)/shard_map/ppermute | solution.py:349
  49.2 4.3 %collective-permute-done.5.refs_2_ = f32[192,256]{1,0:T(8,128)S(1)} collective-permute-done((f32[192,256]{1,0:T(8,128)S(1)}, f32[192,256]{1,0:T(8,128)S(1)}, u32[]{:S(2)}, u32[]{:S(2)}) %collective-permute-start.5) | collective-permute-done | bytes 196640 | tf_op jit(solution)/shard_map/ppermute | solution.py:349
  53.5 1.0 collective-permute-done.6.refs_3_
  54.5 0.1 shard_map.108
  54.5 2.2 %collective-permute-start.7 = (f32[192,128]{1,0:T(8,128)S(1)}, f32[192,128]{1,0:T(8,128)S(1)}, u32[]{:S(2)}, u32[]{:S(2)}) collective-permute-start(f32[192,128]{1,0:T(8,128)S(1)} %get-tuple-element.53.refs_0_), channel_id=1, source_target_pairs={{0,4},{1,5},{2,6},{3,7},{4,0},{5,1},{6,2},{7,3},{8,12},{9,13},{10,... | collective-permute-start | bytes 294920 | tf_op jit(solution)/shard_map/ppermute | solution.py:349
  56.8 0.8 collective-permute-start.11
  57.5 7.9 %collective-permute-done.7.refs_1_ = f32[192,128]{1,0:T(8,128)S(1)} collective-permute-done((f32[192,128]{1,0:T(8,128)S(1)}, f32[192,128]{1,0:T(8,128)S(1)}, u32[]{:S(2)}, u32[]{:S(2)}) %collective-permute-start.7) | collective-permute-done | bytes 98336 | tf_op jit(solution)/shard_map/ppermute | solution.py:349
  65.4 1.6 %collective-permute-start.8 = (f32[192,128]{1,0:T(8,128)S(1)}, f32[192,128]{1,0:T(8,128)S(1)}, u32[]{:S(2)}, u32[]{:S(2)}) collective-permute-start(f32[192,128]{1,0:T(8,128)S(1)} %shard_map.109.refs_0_), channel_id=1, source_target_pairs={{0,1},{1,0},{2,3},{3,2},{4,5},{5,4},{6,7},{7,6},{8,9},{9,8},{10,11... | collective-permute-start | bytes 294920 | tf_op jit(solution)/shard_map/ppermute | solution.py:349
  67.0 2.0 %collective-permute-start.10 = (f32[192,128]{1,0:T(8,128)S(1)}, f32[192,128]{1,0:T(8,128)S(1)}, u32[]{:S(2)}, u32[]{:S(2)}) collective-permute-start(f32[192,128]{1,0:T(8,128)S(1)} %shard_map.109.refs_0_), channel_id=1, source_target_pairs={{0,3},{1,2},{2,1},{3,0},{4,7},{5,6},{6,5},{7,4},{8,11},{9,10},{10,... | collective-permute-start | bytes 294920 | tf_op jit(solution)/shard_map/ppermute | solution.py:349
  69.0 1.6 %collective-permute-start.12 = (f32[192,128]{1,0:T(8,128)S(1)}, f32[192,128]{1,0:T(8,128)S(1)}, u32[]{:S(2)}, u32[]{:S(2)}) collective-permute-start(f32[192,128]{1,0:T(8,128)S(1)} %shard_map.110.refs_4_), channel_id=1, source_target_pairs={{0,1},{1,0},{2,3},{3,2},{4,5},{5,4},{6,7},{7,6},{8,9},{9,8},{10,11... | collective-permute-start | bytes 294920 | tf_op jit(solution)/shard_map/ppermute | solution.py:349
  70.6 1.4 %collective-permute-done.8.refs_1_ = f32[192,128]{1,0:T(8,128)S(1)} collective-permute-done((f32[192,128]{1,0:T(8,128)S(1)}, f32[192,128]{1,0:T(8,128)S(1)}, u32[]{:S(2)}, u32[]{:S(2)}) %collective-permute-start.8) | collective-permute-done | bytes 98336 | tf_op jit(solution)/shard_map/ppermute | solution.py:349
  72.0 0.6 collective-permute-done.9.refs_2_
  72.7 2.2 %collective-permute-start.14 = (f32[192,128]{1,0:T(8,128)S(1)}, f32[192,128]{1,0:T(8,128)S(1)}, u32[]{:S(2)}, u32[]{:S(2)}) collective-permute-start(f32[192,128]{1,0:T(8,128)S(1)} %shard_map.110.refs_4_), channel_id=1, source_target_pairs={{0,3},{1,2},{2,1},{3,0},{4,7},{5,6},{6,5},{7,4},{8,11},{9,10},{10,... | collective-permute-start | bytes 294920 | tf_op jit(solution)/shard_map/ppermute | solution.py:349
  74.8 0.7 collective-permute-done.12.refs_5_
  75.5 1.1 %collective-permute-done.13.refs_6_ = f32[192,128]{1,0:T(8,128)S(1)} collective-permute-done((f32[192,128]{1,0:T(8,128)S(1)}, f32[192,128]{1,0:T(8,128)S(1)}, u32[]{:S(2)}, u32[]{:S(2)}) %collective-permute-start.13) | collective-permute-done | bytes 98336 | tf_op jit(solution)/shard_map/ppermute | solution.py:349
  76.6 1.9 %collective-permute-done.14.refs_7_ = f32[192,128]{1,0:T(8,128)S(1)} collective-permute-done((f32[192,128]{1,0:T(8,128)S(1)}, f32[192,128]{1,0:T(8,128)S(1)}, u32[]{:S(2)}, u32[]{:S(2)}) %collective-permute-start.14) | collective-permute-done | bytes 98336 | tf_op jit(solution)/shard_map/ppermute | solution.py:349
  78.5 4.6 %shard_map.111 = (f32[1,1]{1,0:T(1,128)S(1)}, f32[1,1]{1,0:T(1,128)}, f32[96,256]{1,0:T(8,128)S(1)}, f32[96,128]{1,0:T(8,128)S(1)}, f32[192,128]{1,0:T(8,128)S(1...) custom-call(s32[1]{0:T(128)} %bitcast.me_ref, ...), custom_call_target="tpu_custom_call" | custom-call | tf_op jit(solution)/shard_map/pallas_call | solution.py:353
  83.1 1.9 %collective-permute-start.15 = (f32[192,128]{1,0:T(8,128)S(1)}, f32[192,128]{1,0:T(8,128)S(1)}, u32[]{:S(2)}, u32[]{:S(2)}) collective-permute-start(f32[192,128]{1,0:T(8,128)S(1)} %get-tuple-element.62), channel_id=1, source_target_pairs={{0,3},{1,2},{2,1},{3,0},{4,7},{5,6},{6,5},{7,4},{8,11},{9,10},{10,... | collective-permute-start | bytes 294920 | tf_op jit(solution)/shard_map/ppermute | solution.py:349
  85.0 0.2 collective-permute-start.16
  85.3 1.4 %collective-permute-start.17 = (f32[192,128]{1,0:T(8,128)S(1)}, f32[192,128]{1,0:T(8,128)S(1)}, u32[]{:S(2)}, u32[]{:S(2)}) collective-permute-start(f32[192,128]{1,0:T(8,128)S(1)} %get-tuple-element.64), channel_id=1, source_target_pairs={{0,1},{1,0},{2,3},{3,2},{4,5},{5,4},{6,7},{7,6},{8,9},{9,8},{10,11... | collective-permute-start | bytes 294920 | tf_op jit(solution)/shard_map/ppermute | solution.py:349
  86.7 1.9 %collective-permute-start.18 = (f32[192,128]{1,0:T(8,128)S(1)}, f32[192,128]{1,0:T(8,128)S(1)}, u32[]{:S(2)}, u32[]{:S(2)}) collective-permute-start(f32[192,128]{1,0:T(8,128)S(1)} %get-tuple-element.67), channel_id=1, source_target_pairs={{0,3},{1,2},{2,1},{3,0},{4,7},{5,6},{6,5},{7,4},{8,11},{9,10},{10,... | collective-permute-start | bytes 294920 | tf_op jit(solution)/shard_map/ppermute | solution.py:349
  88.5 1.0 collective-permute-done.15.refs_1_
  89.5 0.3 collective-permute-start.19
  89.9 1.4 %collective-permute-start.20 = (f32[192,128]{1,0:T(8,128)S(1)}, f32[192,128]{1,0:T(8,128)S(1)}, u32[]{:S(2)}, u32[]{:S(2)}) collective-permute-start(f32[192,128]{1,0:T(8,128)S(1)} %get-tuple-element.69), channel_id=1, source_target_pairs={{0,1},{1,0},{2,3},{3,2},{4,5},{5,4},{6,7},{7,6},{8,9},{9,8},{10,11... | collective-permute-start | bytes 294920 | tf_op jit(solution)/shard_map/ppermute | solution.py:349
  91.3 1.8 %collective-permute-start.21 = (f32[96,128]{1,0:T(8,128)S(1)}, f32[96,128]{1,0:T(8,128)S(1)}, u32[]{:S(2)}, u32[]{:S(2)}) collective-permute-start(f32[96,128]{1,0:T(8,128)S(1)} %get-tuple-element.71), channel_id=1, source_target_pairs={{0,4},{1,5},{2,6},{3,7},{4,0},{5,1},{6,2},{7,3},{8,12},{9,13},{10,... | collective-permute-start | bytes 147464 | tf_op jit(solution)/shard_map/ppermute | solution.py:349
  93.1 1.0 collective-permute-done.19.refs_2_
  94.1 0.3 collective-permute-done.20.refs_3_
  94.5 2.4 %collective-permute-start.22 = (f32[96,128]{1,0:T(8,128)S(1)}, f32[96,128]{1,0:T(8,128)S(1)}, u32[]{:S(2)}, u32[]{:S(2)}) collective-permute-start(f32[96,128]{1,0:T(8,128)S(1)} %get-tuple-element.72), channel_id=1, source_target_pairs={{0,4},{1,5},{2,6},{3,7},{4,0},{5,1},{6,2},{7,3},{8,12},{9,13},{10,... | collective-permute-start | bytes 147464 | tf_op jit(solution)/shard_map/ppermute | solution.py:349
  96.9 1.0 shard_map.112.onto_ref
  98.0 1.6 %collective-permute-done.22.refs_3_ = f32[96,128]{1,0:T(8,128)S(1)} collective-permute-done((f32[96,128]{1,0:T(8,128)S(1)}, f32[96,128]{1,0:T(8,128)S(1)}, u32[]{:S(2)}, u32[]{:S(2)}) %collective-permute-start.22) | collective-permute-done | bytes 49184 | tf_op jit(solution)/shard_map/ppermute | solution.py:349
  99.6 1.9 %shard_map.115 = f32[96,768]{1,0:T(8,128)} custom-call(f32[96,128]{1,0:T(8,128)S(1)} %get-tuple-element.56.spot_ref, bf16[768,768]{1,0:T(8,128)(2,1)S(1)} %shard_map.112.onto_ref, f32[1,1]{1,0:T(1,128)S(1)} %get-tuple-element.57.energy_ref, f32[1,1]{1,0:T(1,128)} %get-tuple-element.58.spread_ref, f32[96,256]{1,0:T(8,128)S(1)} %get-tuple-element.59.initial_ref, ...), custom_call_target="tpu_custom_call" | custom-call | tf_op jit(solution)/shard_map/pallas_call | solution.py:353
  101.4 2.6 %shard_map.116 = f32[768,768]{1,0:T(8,128)} custom-call(s32[1]{0:T(128)} %bitcast.1.segment_ref, f32[768,768]{1,0:T(8,128)} %bitcast.20, f32[768,768]{1,0:T(8,128)S(1)} %collective-permute-done.23.shifted_ref), custom_call_target="tpu_custom_call" | custom-call | tf_op jit(solution)/shard_map/pallas_call | solution.py:489
  (22 shorter events, 0.1 us)
Async XLA Ops:
  0.6 32.6 %copy-start = (f32[1,768,768]{2,1,0:T(8,128)S(1)}, f32[1,768,768]{2,1,0:T(8,128)}, u32[]{:S(2)}) copy-start(f32[1,768,768]{2,1,0:T(8,128)} %param.11) | copy-start | bytes 7077892
  2.5 9.0 %collective-permute-start = (f32[96,256]{1,0:T(8,128)S(1)}, f32[96,256]{1,0:T(8,128)S(1)}, u32[]{:S(2)}, u32[]{:S(2)}) collective-permute-start(f32[96,256]{1,0:T(8,128)S(1)} %shard_map.104.first_ref), channel_id=1, source_target_pairs={{0,4},{1,5},{2,6},{3,7},{4,0},{5,1},{6,2},{7,3},{8,12},{9,13},{10,... | collective-permute-start | bytes 294920 | tf_op jit(solution)/shard_map/ppermute | solution.py:349
  11.5 16.7 %collective-permute-start.1 = (f32[192,256]{1,0:T(8,128)S(1)}, f32[192,256]{1,0:T(8,128)S(1)}, u32[]{:S(2)}, u32[]{:S(2)}) collective-permute-start(f32[192,256]{1,0:T(8,128)S(1)} %shard_map.105.refs_0_), channel_id=1, source_target_pairs={{0,1},{1,0},{2,3},{3,2},{4,5},{5,4},{6,7},{7,6},{8,9},{9,8},{10,11... | collective-permute-start | bytes 589832 | tf_op jit(solution)/shard_map/ppermute | solution.py:349
  13.2 15.1 %collective-permute-start.2 = (f32[192,256]{1,0:T(8,128)S(1)}, f32[192,256]{1,0:T(8,128)S(1)}, u32[]{:S(2)}, u32[]{:S(2)}) collective-permute-start(f32[192,256]{1,0:T(8,128)S(1)} %shard_map.105.refs_0_), channel_id=1, source_target_pairs={{0,2},{1,3},{2,0},{3,1},{4,6},{5,7},{6,4},{7,5},{8,10},{9,11},{10,... | collective-permute-start | bytes 589832 | tf_op jit(solution)/shard_map/ppermute | solution.py:349
  13.8 14.5 %collective-permute-start.3 = (f32[192,256]{1,0:T(8,128)S(1)}, f32[192,256]{1,0:T(8,128)S(1)}, u32[]{:S(2)}, u32[]{:S(2)}) collective-permute-start(f32[192,256]{1,0:T(8,128)S(1)} %shard_map.105.refs_0_), channel_id=1, source_target_pairs={{0,3},{1,2},{2,1},{3,0},{4,7},{5,6},{6,5},{7,4},{8,11},{9,10},{10,... | collective-permute-start | bytes 589832 | tf_op jit(solution)/shard_map/ppermute | solution.py:349
  20.2 8.1 %copy-start.1 = (f32[16]{0:T(128)S(1)}, f32[16]{0:T(128)}, u32[]{:S(2)}) copy-start(f32[16]{0:T(128)} %table_ref.3) | copy-start | bytes 196
  28.3 4.9 %copy-start.2 = (f32[1,1,768,768]{3,2,1,0:T(8,128)S(1)}, f32[1,1,768,768]{3,2,1,0:T(8,128)}, u32[]{:S(2)}) copy-start(f32[1,1,768,768]{3,2,1,0:T(8,128)} %param.8) | copy-start | bytes 7077892
  39.9 61.5 %collective-permute-start.23 = (f32[768,768]{1,0:T(8,128)S(1)}, f32[768,768]{1,0:T(8,128)S(1)}, u32[]{:S(2)}, u32[]{:S(2)}) collective-permute-start(f32[768,768]{1,0:T(8,128)S(1)} %fusion.4), channel_id=1, source_target_pairs={{0,8},{8,16},{16,24},{1,9},{9,17},{17,25},{2,10},{10,18},{18,26},{... | collective-permute-start | bytes 7077896 | tf_op jit(solution)/shard_map/ppermute | solution.py:336
  41.6 7.6 %collective-permute-start.4 = (f32[192,256]{1,0:T(8,128)S(1)}, f32[192,256]{1,0:T(8,128)S(1)}, u32[]{:S(2)}, u32[]{:S(2)}) collective-permute-start(f32[192,256]{1,0:T(8,128)S(1)} %get-tuple-element.50), channel_id=1, source_target_pairs={{0,3},{1,2},{2,1},{3,0},{4,7},{5,6},{6,5},{7,4},{8,11},{9,10},{10,... | collective-permute-start | bytes 589832 | tf_op jit(solution)/shard_map/ppermute | solution.py:349
  43.3 10.2 %collective-permute-start.5 = (f32[192,256]{1,0:T(8,128)S(1)}, f32[192,256]{1,0:T(8,128)S(1)}, u32[]{:S(2)}, u32[]{:S(2)}) collective-permute-start(f32[192,256]{1,0:T(8,128)S(1)} %get-tuple-element.51), channel_id=1, source_target_pairs={{0,2},{1,3},{2,0},{3,1},{4,6},{5,7},{6,4},{7,5},{8,10},{9,11},{10,... | collective-permute-start | bytes 589832 | tf_op jit(solution)/shard_map/ppermute | solution.py:349
  44.6 9.8 %collective-permute-start.6 = (f32[192,256]{1,0:T(8,128)S(1)}, f32[192,256]{1,0:T(8,128)S(1)}, u32[]{:S(2)}, u32[]{:S(2)}) collective-permute-start(f32[192,256]{1,0:T(8,128)S(1)} %get-tuple-element.52), channel_id=1, source_target_pairs={{0,1},{1,0},{2,3},{3,2},{4,5},{5,4},{6,7},{7,6},{8,9},{9,8},{10,11... | collective-permute-start | bytes 589832 | tf_op jit(solution)/shard_map/ppermute | solution.py:349
  54.5 10.8 %collective-permute-start.7 = (f32[192,128]{1,0:T(8,128)S(1)}, f32[192,128]{1,0:T(8,128)S(1)}, u32[]{:S(2)}, u32[]{:S(2)}) collective-permute-start(f32[192,128]{1,0:T(8,128)S(1)} %get-tuple-element.53.refs_0_), channel_id=1, source_target_pairs={{0,4},{1,5},{2,6},{3,7},{4,0},{5,1},{6,2},{7,3},{8,12},{9,13},{10,... | collective-permute-start | bytes 294920 | tf_op jit(solution)/shard_map/ppermute | solution.py:349
  56.8 12.2 %collective-permute-start.11 = (f32[192,128]{1,0:T(8,128)S(1)}, f32[192,128]{1,0:T(8,128)S(1)}, u32[]{:S(2)}, u32[]{:S(2)}) collective-permute-start(f32[192,128]{1,0:T(8,128)S(1)} %get-tuple-element.54.refs_0_), channel_id=1, source_target_pairs={{0,4},{1,5},{2,6},{3,7},{4,0},{5,1},{6,2},{7,3},{8,12},{9,13},{10,... | collective-permute-start | bytes 294920 | tf_op jit(solution)/shard_map/ppermute | solution.py:349
  65.4 6.6 %collective-permute-start.8 = (f32[192,128]{1,0:T(8,128)S(1)}, f32[192,128]{1,0:T(8,128)S(1)}, u32[]{:S(2)}, u32[]{:S(2)}) collective-permute-start(f32[192,128]{1,0:T(8,128)S(1)} %shard_map.109.refs_0_), channel_id=1, source_target_pairs={{0,1},{1,0},{2,3},{3,2},{4,5},{5,4},{6,7},{7,6},{8,9},{9,8},{10,11... | collective-permute-start | bytes 294920 | tf_op jit(solution)/shard_map/ppermute | solution.py:349
  67.0 5.7 %collective-permute-start.9 = (f32[192,128]{1,0:T(8,128)S(1)}, f32[192,128]{1,0:T(8,128)S(1)}, u32[]{:S(2)}, u32[]{:S(2)}) collective-permute-start(f32[192,128]{1,0:T(8,128)S(1)} %shard_map.109.refs_0_), channel_id=1, source_target_pairs={{0,2},{1,3},{2,0},{3,1},{4,6},{5,7},{6,4},{7,5},{8,10},{9,11},{10,... | collective-permute-start | bytes 294920 | tf_op jit(solution)/shard_map/ppermute | solution.py:349
  67.0 7.8 %collective-permute-start.10 = (f32[192,128]{1,0:T(8,128)S(1)}, f32[192,128]{1,0:T(8,128)S(1)}, u32[]{:S(2)}, u32[]{:S(2)}) collective-permute-start(f32[192,128]{1,0:T(8,128)S(1)} %shard_map.109.refs_0_), channel_id=1, source_target_pairs={{0,3},{1,2},{2,1},{3,0},{4,7},{5,6},{6,5},{7,4},{8,11},{9,10},{10,... | collective-permute-start | bytes 294920 | tf_op jit(solution)/shard_map/ppermute | solution.py:349
  69.0 6.6 %collective-permute-start.12 = (f32[192,128]{1,0:T(8,128)S(1)}, f32[192,128]{1,0:T(8,128)S(1)}, u32[]{:S(2)}, u32[]{:S(2)}) collective-permute-start(f32[192,128]{1,0:T(8,128)S(1)} %shard_map.110.refs_4_), channel_id=1, source_target_pairs={{0,1},{1,0},{2,3},{3,2},{4,5},{5,4},{6,7},{7,6},{8,9},{9,8},{10,11... | collective-permute-start | bytes 294920 | tf_op jit(solution)/shard_map/ppermute | solution.py:349
  72.0 4.6 %collective-permute-start.13 = (f32[192,128]{1,0:T(8,128)S(1)}, f32[192,128]{1,0:T(8,128)S(1)}, u32[]{:S(2)}, u32[]{:S(2)}) collective-permute-start(f32[192,128]{1,0:T(8,128)S(1)} %shard_map.110.refs_4_), channel_id=1, source_target_pairs={{0,2},{1,3},{2,0},{3,1},{4,6},{5,7},{6,4},{7,5},{8,10},{9,11},{10,... | collective-permute-start | bytes 294920 | tf_op jit(solution)/shard_map/ppermute | solution.py:349
  72.7 5.8 %collective-permute-start.14 = (f32[192,128]{1,0:T(8,128)S(1)}, f32[192,128]{1,0:T(8,128)S(1)}, u32[]{:S(2)}, u32[]{:S(2)}) collective-permute-start(f32[192,128]{1,0:T(8,128)S(1)} %shard_map.110.refs_4_), channel_id=1, source_target_pairs={{0,3},{1,2},{2,1},{3,0},{4,7},{5,6},{6,5},{7,4},{8,11},{9,10},{10,... | collective-permute-start | bytes 294920 | tf_op jit(solution)/shard_map/ppermute | solution.py:349
  83.1 6.4 %collective-permute-start.15 = (f32[192,128]{1,0:T(8,128)S(1)}, f32[192,128]{1,0:T(8,128)S(1)}, u32[]{:S(2)}, u32[]{:S(2)}) collective-permute-start(f32[192,128]{1,0:T(8,128)S(1)} %get-tuple-element.62), channel_id=1, source_target_pairs={{0,3},{1,2},{2,1},{3,0},{4,7},{5,6},{6,5},{7,4},{8,11},{9,10},{10,... | collective-permute-start | bytes 294920 | tf_op jit(solution)/shard_map/ppermute | solution.py:349
  85.0 4.8 %collective-permute-start.16 = (f32[192,128]{1,0:T(8,128)S(1)}, f32[192,128]{1,0:T(8,128)S(1)}, u32[]{:S(2)}, u32[]{:S(2)}) collective-permute-start(f32[192,128]{1,0:T(8,128)S(1)} %get-tuple-element.63), channel_id=1, source_target_pairs={{0,2},{1,3},{2,0},{3,1},{4,6},{5,7},{6,4},{7,5},{8,10},{9,11},{10,... | collective-permute-start | bytes 294920 | tf_op jit(solution)/shard_map/ppermute | solution.py:349
  85.3 5.9 %collective-permute-start.17 = (f32[192,128]{1,0:T(8,128)S(1)}, f32[192,128]{1,0:T(8,128)S(1)}, u32[]{:S(2)}, u32[]{:S(2)}) collective-permute-start(f32[192,128]{1,0:T(8,128)S(1)} %get-tuple-element.64), channel_id=1, source_target_pairs={{0,1},{1,0},{2,3},{3,2},{4,5},{5,4},{6,7},{7,6},{8,9},{9,8},{10,11... | collective-permute-start | bytes 294920 | tf_op jit(solution)/shard_map/ppermute | solution.py:349
  86.7 6.5 %collective-permute-start.18 = (f32[192,128]{1,0:T(8,128)S(1)}, f32[192,128]{1,0:T(8,128)S(1)}, u32[]{:S(2)}, u32[]{:S(2)}) collective-permute-start(f32[192,128]{1,0:T(8,128)S(1)} %get-tuple-element.67), channel_id=1, source_target_pairs={{0,3},{1,2},{2,1},{3,0},{4,7},{5,6},{6,5},{7,4},{8,11},{9,10},{10,... | collective-permute-start | bytes 294920 | tf_op jit(solution)/shard_map/ppermute | solution.py:349
  89.5 4.6 %collective-permute-start.19 = (f32[192,128]{1,0:T(8,128)S(1)}, f32[192,128]{1,0:T(8,128)S(1)}, u32[]{:S(2)}, u32[]{:S(2)}) collective-permute-start(f32[192,128]{1,0:T(8,128)S(1)} %get-tuple-element.68), channel_id=1, source_target_pairs={{0,2},{1,3},{2,0},{3,1},{4,6},{5,7},{6,4},{7,5},{8,10},{9,11},{10,... | collective-permute-start | bytes 294920 | tf_op jit(solution)/shard_map/ppermute | solution.py:349
  89.9 4.6 %collective-permute-start.20 = (f32[192,128]{1,0:T(8,128)S(1)}, f32[192,128]{1,0:T(8,128)S(1)}, u32[]{:S(2)}, u32[]{:S(2)}) collective-permute-start(f32[192,128]{1,0:T(8,128)S(1)} %get-tuple-element.69), channel_id=1, source_target_pairs={{0,1},{1,0},{2,3},{3,2},{4,5},{5,4},{6,7},{7,6},{8,9},{9,8},{10,11... | collective-permute-start | bytes 294920 | tf_op jit(solution)/shard_map/ppermute | solution.py:349
  91.3 6.7 %collective-permute-start.21 = (f32[96,128]{1,0:T(8,128)S(1)}, f32[96,128]{1,0:T(8,128)S(1)}, u32[]{:S(2)}, u32[]{:S(2)}) collective-permute-start(f32[96,128]{1,0:T(8,128)S(1)} %get-tuple-element.71), channel_id=1, source_target_pairs={{0,4},{1,5},{2,6},{3,7},{4,0},{5,1},{6,2},{7,3},{8,12},{9,13},{10,... | collective-permute-start | bytes 147464 | tf_op jit(solution)/shard_map/ppermute | solution.py:349
  94.5 5.1 %collective-permute-start.22 = (f32[96,128]{1,0:T(8,128)S(1)}, f32[96,128]{1,0:T(8,128)S(1)}, u32[]{:S(2)}, u32[]{:S(2)}) collective-permute-start(f32[96,128]{1,0:T(8,128)S(1)} %get-tuple-element.72), channel_id=1, source_target_pairs={{0,4},{1,5},{2,6},{3,7},{4,0},{5,1},{6,2},{7,3},{8,12},{9,13},{10,... | collective-permute-start | bytes 147464 | tf_op jit(solution)/shard_map/ppermute | solution.py:349

commit v4 on v3

--- a/solution.py
+++ b/solution.py
@@ -181,16 +181,22 @@
     )(far(charge), left_half_high, left_half_low, left_onto, far(ops))
 
 
-def apply_blocks(packed, scale, left_high, left_low, right_high, right_low, half_high, half_low, total):
+def apply_blocks(packed, scale, left_high, left_low, right_high, right_low, halfs, total):
     block = packed.shape[1]
     for q in range(NQ):
         here = slice(q * block, (q + 1) * block)
         high, low = split(packed[here, :])
         value = mm3(left_high[:, here], left_low[:, here], high, low) * scale
-        half_high[:, here], half_low[:, here] = split(value)
+        high, low = split(value)
+        for o in range(NQ):
+            there = slice(o * block, (o + 1) * block)
+            halfs[2 * o * block : (2 * o + 1) * block, here] = high[there, :]
+            halfs[(2 * o + 1) * block : 2 * (o + 1) * block, here] = low[there, :]
     for q in range(NQ):
         here = slice(q * block, (q + 1) * block)
-        total[here, :] = mm3(half_high[here, :], half_low[here, :], right_high[:, here], right_low[:, here])
+        both = mm(halfs[2 * q * block : 2 * (q + 1) * block, :], right_high[:, here])
+        rest = mm(halfs[2 * q * block : (2 * q + 1) * block, :], right_low[:, here])
+        total[here, :] = both[:block, :] + (both[block:, :] + rest)
 
 
 def first_kernel(group, me_ref, term_ref, table_ref, onto_ref, *refs):
@@ -198,7 +204,7 @@
     left_high, left_low, right_high, right_low = refs[group : group + 4]
     initial_ref, initial_rows_ref = refs[group + 4 : group + 6]
     outs = refs[group + 6 : 2 * group + 6]
-    half_high, half_low, total = refs[2 * group + 6 :]
+    halfs, total = refs[2 * group + 6 :]
     half = lax.div(me_ref[0], group)
     own = lax.rem(me_ref[0], group)
     pair, block = parts[0].shape
@@ -215,7 +221,7 @@
     initial_rows_ref[...] = parts[0][:rows, :] / norm
     scale = table_ref[term_ref[0, 0]]
     apply_blocks(
-        initial_ref[...], scale, left_high, left_low, right_high, right_low, half_high, half_low, total
+        initial_ref[...], scale, left_high, left_low, right_high, right_low, halfs, total
     )
     each = block // group
     for s in range(group):
@@ -230,7 +236,7 @@
     initial_ref, left_high, left_low, right_high, right_low = refs[count : count + 5]
     energy_ref, spread_ref, step_rows_ref, spot_ref = refs[count + 5 : count + 9]
     outs = refs[count + 9 : 2 * count + 9]
-    half_high, half_low, total, step_ref = refs[2 * count + 9 :]
+    halfs, total, step_ref = refs[2 * count + 9 :]
     half = lax.div(me_ref[0], group)
     own = lax.rem(me_ref[0], group)
     pair, width = parts[0].shape
@@ -252,7 +258,7 @@
     spread_ref[...] = spread
     scale = table_ref[term_ref[0, 0]]
     apply_blocks(
-        step_ref[...], scale, left_high, left_low, right_high, right_low, half_high, half_low, total
+        step_ref[...], scale, left_high, left_low, right_high, right_low, halfs, total
     )
     high, low = split(total[...])
     total[...] = mm(back_ref[...], high) + mm(back_ref[...], low)
@@ -410,7 +416,7 @@
     left_half_high, left_half_low, onto, back, left_column = sort_columns(left_charge, own_left)
     left_high, left_low, right_high, right_low = sort_rest(right_charge, left_half_high, left_half_low, onto, own_right)
     pieces = (left_high, left_low, right_high, right_low)
-    halves = [pltpu.VMEM((size, size), BF16), pltpu.VMEM((size, size), BF16), pltpu.VMEM((size, block), F32)]
+    halves = [pltpu.VMEM((2 * size, size), BF16), pltpu.VMEM((size, block), F32)]
     pairs = [pltpu.VMEM((2 * rows, block), F32)] * group
 
     initial, initial_rows, *sent = call(

time: 106 us -> 105 us (level)
  no operation moved by 1% of the time
where the time goes in v4:
time: 105 us
  starting transfers between devices  34.6 us (33%)
  waiting for transfers between devices  31.8 us (30%)
  Pallas kernels  29.4 us (28%)
  matrix products  6.64 us (6%)
  between operations  2.64 us (3%)
    ppermute x23, starting transfers between devices, swapped(): lax.ppermute(value, axis, [(source, source ^ mask) for source in range(co...  32.9 us
    ppermute x23, waiting for transfers between devices, swapped(): lax.ppermute(value, axis, [(source, source ^ mask) for source in range(co...  31.8 us
    pallas_call x11, Pallas kernels, call(): pl.pallas_call(kernel, in_specs=ins, out_specs=[VMEM] * len(outs), out_sh...  14.3 us
    pallas_call x1, Pallas kernels, sort_rest(): pl.pallas_call(sort_kernel, grid=(NQ,), in_specs=[VMEM] * 4 + [pl.BlockSp...  8.04 us
    pallas_call x1, Pallas kernels, sort_columns(): pl.pallas_call(columns_kernel, grid=(NQ,), in_specs=[VMEM, pl.BlockSpec((...  4.45 us
    dot_general x1, matrix products, all_steps(): lax.dot_general(basis_rotation[0], half_turn, (((0,), (0,)), ((), ())), p...  3.55 us
    dot_general x1, matrix products, all_steps(): jnp.dot(turned_left, basis_rotation[0], precision=lax.Precision.HIGH)  3.1 us
    pallas_call x1, Pallas kernels, all_steps(): pl.pallas_call(choose_kernel, in_specs=[SMEM, HBM, VMEM], out_specs=HBM,...  2.62 us
  transfers between devices with their start and end apart: 24, of which 14 were waited for; matrix products, arithmetic and copies ran while one was open for 0% of the time, Pallas kernels for 19%

profile of v4, /device:TPU:0, one launch (start us, length us, event | category | flops | bytes accessed | tf_op | source)
XLA Modules:
  0.0 105.1 jit_solution(13875392406490500392)
XLA Ops:
  0.6 0.0 copy-start
  0.7 1.8 %shard_map.104.first_ref = f32[96,256]{1,0:T(8,128)S(1)} custom-call(s32[1]{0:T(128)} %bitcast.me_ref, s32[1,768]{1,0:T(1,128)} %left_hbm.1, s32[1,768]{1,0:T(1,128)} %charge_ref.5, f32[96,768]{1,0:T(8,128)} %bitcast.25), custom_call_target="tpu_custom_call" | custom-call | tf_op jit(solution)/shard_map/pallas_call | solution.py:359
  2.5 4.1 %collective-permute-start = (f32[96,256]{1,0:T(8,128)S(1)}, f32[96,256]{1,0:T(8,128)S(1)}, u32[]{:S(2)}, u32[]{:S(2)}) collective-permute-start(f32[96,256]{1,0:T(8,128)S(1)} %shard_map.104.first_ref), channel_id=1, source_target_pairs={{0,4},{1,5},{2,6},{3,7},{4,0},{5,1},{6,2},{7,3},{8,12},{9,13},{10,... | collective-permute-start | bytes 294920 | tf_op jit(solution)/shard_map/ppermute | solution.py:355
  6.6 4.9 %collective-permute-done.second_ref = f32[96,256]{1,0:T(8,128)S(1)} collective-permute-done((f32[96,256]{1,0:T(8,128)S(1)}, f32[96,256]{1,0:T(8,128)S(1)}, u32[]{:S(2)}, u32[]{:S(2)}) %collective-permute-start) | collective-permute-done | bytes 98336 | tf_op jit(solution)/shard_map/ppermute | solution.py:355
  11.5 1.6 %collective-permute-start.1 = (f32[192,256]{1,0:T(8,128)S(1)}, f32[192,256]{1,0:T(8,128)S(1)}, u32[]{:S(2)}, u32[]{:S(2)}) collective-permute-start(f32[192,256]{1,0:T(8,128)S(1)} %shard_map.105.refs_0_), channel_id=1, source_target_pairs={{0,1},{1,0},{2,3},{3,2},{4,5},{5,4},{6,7},{7,6},{8,9},{9,8},{10,11... | collective-permute-start | bytes 589832 | tf_op jit(solution)/shard_map/ppermute | solution.py:355
  13.2 0.7 collective-permute-start.2
  13.8 1.3 %collective-permute-start.3 = (f32[192,256]{1,0:T(8,128)S(1)}, f32[192,256]{1,0:T(8,128)S(1)}, u32[]{:S(2)}, u32[]{:S(2)}) collective-permute-start(f32[192,256]{1,0:T(8,128)S(1)} %shard_map.105.refs_0_), channel_id=1, source_target_pairs={{0,3},{1,2},{2,1},{3,0},{4,7},{5,6},{6,5},{7,4},{8,11},{9,10},{10,... | collective-permute-start | bytes 589832 | tf_op jit(solution)/shard_map/ppermute | solution.py:355
  15.8 4.5 %shard_map.103 = (bf16[768,768]{1,0:T(8,128)(2,1)S(1)}, bf16[768,768]{1,0:T(8,128)(2,1)S(1)}, bf16[768,768]{1,0:T(8,128)(2,1)S(1)}, bf16[768,768]{1,0:T(8,128)(2,1)S(1)}, f32[768,128]{1,0:T(8,128)S(1)}) custom-call(s32[1,768]{1,0:T(1,128)} %left_hbm.1, f32[768,768]{1,0:T(8,128)} %bitcast.19), custom_call_target="tpu_custom_call" | custom-call | tf_op jit(solution)/shard_map/pallas_call | solution.py:160
  20.2 8.0 %shard_map.106 = (bf16[768,768]{1,0:T(8,128)(2,1)S(1)}, bf16[768,768]{1,0:T(8,128)(2,1)S(1)}, bf16[768,768]{1,0:T(8,128)(2,1)S(1)}, bf16[768,768]{1,0:T(8,128)(2,1)S(1)}) custom-call(s32[1,768]{1,0:T(1,128)} %charge_ref.5, bf16[768,768]{1,0:T(8,128)(2,1)S(1)} %get-tuple-element.43.left_half_high, bf16[768,768]{1,0:T(8,128)(2,1)S(1)} %get-tuple-element.44.left_half_low, ...), custom_call_target="tpu_custom_call" | custom-call | tf_op jit(solution)/shard_map/pallas_call | solution.py:173
  28.3 4.9 %shard_map.107 = (f32[768,256]{1,0:T(8,128)S(1)}, f32[96,256]{1,0:T(8,128)S(1)}, f32[192,256]{1,0:T(8,128)S(1)}, f32[192,256]{1,0:T(8,128)S(1)}, f32[192,256]{1,0:T(8,128)S(1)}, /*index=5*/f32[192,256]{1,0:T(8,128)S(1)}) custom-call(s32[1]{0:T(128)} %bitcast.me_ref, s32[1,1]{1,0:T(1,128)S(6)} %copy.14.term_ref, f32[16]{0:T(128)S(1)} %copy-done.1, ...), custom_call_target="tpu_custom_call" | custom-call | tf_op jit(solution)/shard_map/pallas_call | solution.py:359
  33.2 3.1 %fusion.2 = f32[768,768]{1,0:T(8,128)S(1)} fusion(f32[768,768]{1,0:T(8,128)S(1)} %bitcast.21, f32[1,768,768]{2,1,0:T(8,128)S(1)} %copy-done), kind=kOutput, calls=%fused_computation.2 | convolution fusion | flops 2717908992 | bytes 7077888 | tf_op jit(solution)/shard_map/dot_general | solution.py:490
  36.4 3.5 %fusion.4 = f32[768,768]{1,0:T(8,128)S(1)} fusion(f32[768,768]{1,0:T(8,128)S(1)} %fusion.2, f32[1,768,768]{2,1,0:T(8,128)S(1)} %copy-done), kind=kOutput, calls=%fused_computation.4 | convolution fusion | flops 2717908992 | bytes 7077888 | tf_op jit(solution)/shard_map/dot_general | solution.py:491
  39.9 1.7 %collective-permute-start.23 = (f32[768,768]{1,0:T(8,128)S(1)}, f32[768,768]{1,0:T(8,128)S(1)}, u32[]{:S(2)}, u32[]{:S(2)}) collective-permute-start(f32[768,768]{1,0:T(8,128)S(1)} %fusion.4), channel_id=1, source_target_pairs={{0,8},{8,16},{16,24},{1,9},{9,17},{17,25},{2,10},{10,18},{18,26},{... | collective-permute-start | bytes 7077896 | tf_op jit(solution)/shard_map/ppermute | solution.py:342
  41.6 1.7 %collective-permute-start.4 = (f32[192,256]{1,0:T(8,128)S(1)}, f32[192,256]{1,0:T(8,128)S(1)}, u32[]{:S(2)}, u32[]{:S(2)}) collective-permute-start(f32[192,256]{1,0:T(8,128)S(1)} %get-tuple-element.50), channel_id=1, source_target_pairs={{0,3},{1,2},{2,1},{3,0},{4,7},{5,6},{6,5},{7,4},{8,11},{9,10},{10,... | collective-permute-start | bytes 589832 | tf_op jit(solution)/shard_map/ppermute | solution.py:355
  43.3 1.3 %collective-permute-start.5 = (f32[192,256]{1,0:T(8,128)S(1)}, f32[192,256]{1,0:T(8,128)S(1)}, u32[]{:S(2)}, u32[]{:S(2)}) collective-permute-start(f32[192,256]{1,0:T(8,128)S(1)} %get-tuple-element.51), channel_id=1, source_target_pairs={{0,2},{1,3},{2,0},{3,1},{4,6},{5,7},{6,4},{7,5},{8,10},{9,11},{10,... | collective-permute-start | bytes 589832 | tf_op jit(solution)/shard_map/ppermute | solution.py:355
  44.6 0.5 collective-permute-start.6
  45.1 4.1 %collective-permute-done.4.refs_1_ = f32[192,256]{1,0:T(8,128)S(1)} collective-permute-done((f32[192,256]{1,0:T(8,128)S(1)}, f32[192,256]{1,0:T(8,128)S(1)}, u32[]{:S(2)}, u32[]{:S(2)}) %collective-permute-start.4) | collective-permute-done | bytes 196640 | tf_op jit(solution)/shard_map/ppermute | solution.py:355
  49.2 4.3 %collective-permute-done.5.refs_2_ = f32[192,256]{1,0:T(8,128)S(1)} collective-permute-done((f32[192,256]{1,0:T(8,128)S(1)}, f32[192,256]{1,0:T(8,128)S(1)}, u32[]{:S(2)}, u32[]{:S(2)}) %collective-permute-start.5) | collective-permute-done | bytes 196640 | tf_op jit(solution)/shard_map/ppermute | solution.py:355
  53.5 1.0 collective-permute-done.6.refs_3_
  54.5 0.1 shard_map.108
  54.5 2.2 %collective-permute-start.7 = (f32[192,128]{1,0:T(8,128)S(1)}, f32[192,128]{1,0:T(8,128)S(1)}, u32[]{:S(2)}, u32[]{:S(2)}) collective-permute-start(f32[192,128]{1,0:T(8,128)S(1)} %get-tuple-element.53.refs_0_), channel_id=1, source_target_pairs={{0,4},{1,5},{2,6},{3,7},{4,0},{5,1},{6,2},{7,3},{8,12},{9,13},{10,... | collective-permute-start | bytes 294920 | tf_op jit(solution)/shard_map/ppermute | solution.py:355
  56.8 0.8 collective-permute-start.11
  57.5 7.9 %collective-permute-done.7.refs_1_ = f32[192,128]{1,0:T(8,128)S(1)} collective-permute-done((f32[192,128]{1,0:T(8,128)S(1)}, f32[192,128]{1,0:T(8,128)S(1)}, u32[]{:S(2)}, u32[]{:S(2)}) %collective-permute-start.7) | collective-permute-done | bytes 98336 | tf_op jit(solution)/shard_map/ppermute | solution.py:355
  65.4 1.6 %collective-permute-start.8 = (f32[192,128]{1,0:T(8,128)S(1)}, f32[192,128]{1,0:T(8,128)S(1)}, u32[]{:S(2)}, u32[]{:S(2)}) collective-permute-start(f32[192,128]{1,0:T(8,128)S(1)} %shard_map.109.refs_0_), channel_id=1, source_target_pairs={{0,1},{1,0},{2,3},{3,2},{4,5},{5,4},{6,7},{7,6},{8,9},{9,8},{10,11... | collective-permute-start | bytes 294920 | tf_op jit(solution)/shard_map/ppermute | solution.py:355
  67.0 2.0 %collective-permute-start.10 = (f32[192,128]{1,0:T(8,128)S(1)}, f32[192,128]{1,0:T(8,128)S(1)}, u32[]{:S(2)}, u32[]{:S(2)}) collective-permute-start(f32[192,128]{1,0:T(8,128)S(1)} %shard_map.109.refs_0_), channel_id=1, source_target_pairs={{0,3},{1,2},{2,1},{3,0},{4,7},{5,6},{6,5},{7,4},{8,11},{9,10},{10,... | collective-permute-start | bytes 294920 | tf_op jit(solution)/shard_map/ppermute | solution.py:355
  69.0 1.6 %collective-permute-start.12 = (f32[192,128]{1,0:T(8,128)S(1)}, f32[192,128]{1,0:T(8,128)S(1)}, u32[]{:S(2)}, u32[]{:S(2)}) collective-permute-start(f32[192,128]{1,0:T(8,128)S(1)} %shard_map.110.refs_4_), channel_id=1, source_target_pairs={{0,1},{1,0},{2,3},{3,2},{4,5},{5,4},{6,7},{7,6},{8,9},{9,8},{10,11... | collective-permute-start | bytes 294920 | tf_op jit(solution)/shard_map/ppermute | solution.py:355
  70.6 1.4 %collective-permute-done.8.refs_1_ = f32[192,128]{1,0:T(8,128)S(1)} collective-permute-done((f32[192,128]{1,0:T(8,128)S(1)}, f32[192,128]{1,0:T(8,128)S(1)}, u32[]{:S(2)}, u32[]{:S(2)}) %collective-permute-start.8) | collective-permute-done | bytes 98336 | tf_op jit(solution)/shard_map/ppermute | solution.py:355
  72.0 0.6 collective-permute-done.9.refs_2_
  72.6 2.2 %collective-permute-start.14 = (f32[192,128]{1,0:T(8,128)S(1)}, f32[192,128]{1,0:T(8,128)S(1)}, u32[]{:S(2)}, u32[]{:S(2)}) collective-permute-start(f32[192,128]{1,0:T(8,128)S(1)} %shard_map.110.refs_4_), channel_id=1, source_target_pairs={{0,3},{1,2},{2,1},{3,0},{4,7},{5,6},{6,5},{7,4},{8,11},{9,10},{10,... | collective-permute-start | bytes 294920 | tf_op jit(solution)/shard_map/ppermute | solution.py:355
  74.8 0.7 collective-permute-done.12.refs_5_
  75.5 1.1 %collective-permute-done.13.refs_6_ = f32[192,128]{1,0:T(8,128)S(1)} collective-permute-done((f32[192,128]{1,0:T(8,128)S(1)}, f32[192,128]{1,0:T(8,128)S(1)}, u32[]{:S(2)}, u32[]{:S(2)}) %collective-permute-start.13) | collective-permute-done | bytes 98336 | tf_op jit(solution)/shard_map/ppermute | solution.py:355
  76.6 1.9 %collective-permute-done.14.refs_7_ = f32[192,128]{1,0:T(8,128)S(1)} collective-permute-done((f32[192,128]{1,0:T(8,128)S(1)}, f32[192,128]{1,0:T(8,128)S(1)}, u32[]{:S(2)}, u32[]{:S(2)}) %collective-permute-start.14) | collective-permute-done | bytes 98336 | tf_op jit(solution)/shard_map/ppermute | solution.py:355
  78.5 4.6 %shard_map.111 = (f32[1,1]{1,0:T(1,128)S(1)}, f32[1,1]{1,0:T(1,128)}, f32[96,256]{1,0:T(8,128)S(1)}, f32[96,128]{1,0:T(8,128)S(1)}, f32[192,128]{1,0:T(8,128)S(1...) custom-call(s32[1]{0:T(128)} %bitcast.me_ref, ...), custom_call_target="tpu_custom_call" | custom-call | tf_op jit(solution)/shard_map/pallas_call | solution.py:359
  83.1 1.9 %collective-permute-start.15 = (f32[192,128]{1,0:T(8,128)S(1)}, f32[192,128]{1,0:T(8,128)S(1)}, u32[]{:S(2)}, u32[]{:S(2)}) collective-permute-start(f32[192,128]{1,0:T(8,128)S(1)} %get-tuple-element.62), channel_id=1, source_target_pairs={{0,3},{1,2},{2,1},{3,0},{4,7},{5,6},{6,5},{7,4},{8,11},{9,10},{10,... | collective-permute-start | bytes 294920 | tf_op jit(solution)/shard_map/ppermute | solution.py:355
  85.0 0.3 collective-permute-start.16
  85.3 1.4 %collective-permute-start.17 = (f32[192,128]{1,0:T(8,128)S(1)}, f32[192,128]{1,0:T(8,128)S(1)}, u32[]{:S(2)}, u32[]{:S(2)}) collective-permute-start(f32[192,128]{1,0:T(8,128)S(1)} %get-tuple-element.64), channel_id=1, source_target_pairs={{0,1},{1,0},{2,3},{3,2},{4,5},{5,4},{6,7},{7,6},{8,9},{9,8},{10,11... | collective-permute-start | bytes 294920 | tf_op jit(solution)/shard_map/ppermute | solution.py:355
  86.6 1.9 %collective-permute-start.18 = (f32[192,128]{1,0:T(8,128)S(1)}, f32[192,128]{1,0:T(8,128)S(1)}, u32[]{:S(2)}, u32[]{:S(2)}) collective-permute-start(f32[192,128]{1,0:T(8,128)S(1)} %get-tuple-element.67), channel_id=1, source_target_pairs={{0,3},{1,2},{2,1},{3,0},{4,7},{5,6},{6,5},{7,4},{8,11},{9,10},{10,... | collective-permute-start | bytes 294920 | tf_op jit(solution)/shard_map/ppermute | solution.py:355
  88.5 1.0 collective-permute-done.15.refs_1_
  89.5 0.3 collective-permute-start.19
  89.8 1.4 %collective-permute-start.20 = (f32[192,128]{1,0:T(8,128)S(1)}, f32[192,128]{1,0:T(8,128)S(1)}, u32[]{:S(2)}, u32[]{:S(2)}) collective-permute-start(f32[192,128]{1,0:T(8,128)S(1)} %get-tuple-element.69), channel_id=1, source_target_pairs={{0,1},{1,0},{2,3},{3,2},{4,5},{5,4},{6,7},{7,6},{8,9},{9,8},{10,11... | collective-permute-start | bytes 294920 | tf_op jit(solution)/shard_map/ppermute | solution.py:355
  91.2 1.8 %collective-permute-start.21 = (f32[96,128]{1,0:T(8,128)S(1)}, f32[96,128]{1,0:T(8,128)S(1)}, u32[]{:S(2)}, u32[]{:S(2)}) collective-permute-start(f32[96,128]{1,0:T(8,128)S(1)} %get-tuple-element.71), channel_id=1, source_target_pairs={{0,4},{1,5},{2,6},{3,7},{4,0},{5,1},{6,2},{7,3},{8,12},{9,13},{10,... | collective-permute-start | bytes 147464 | tf_op jit(solution)/shard_map/ppermute | solution.py:355
  93.1 1.0 collective-permute-done.19.refs_2_
  94.1 0.3 collective-permute-done.20.refs_3_
  94.5 2.4 %collective-permute-start.22 = (f32[96,128]{1,0:T(8,128)S(1)}, f32[96,128]{1,0:T(8,128)S(1)}, u32[]{:S(2)}, u32[]{:S(2)}) collective-permute-start(f32[96,128]{1,0:T(8,128)S(1)} %get-tuple-element.72), channel_id=1, source_target_pairs={{0,4},{1,5},{2,6},{3,7},{4,0},{5,1},{6,2},{7,3},{8,12},{9,13},{10,... | collective-permute-start | bytes 147464 | tf_op jit(solution)/shard_map/ppermute | solution.py:355
  96.9 1.0 shard_map.112.onto_ref
  97.9 1.6 %collective-permute-done.22.refs_3_ = f32[96,128]{1,0:T(8,128)S(1)} collective-permute-done((f32[96,128]{1,0:T(8,128)S(1)}, f32[96,128]{1,0:T(8,128)S(1)}, u32[]{:S(2)}, u32[]{:S(2)}) %collective-permute-start.22) | collective-permute-done | bytes 49184 | tf_op jit(solution)/shard_map/ppermute | solution.py:355
  99.5 1.9 %shard_map.115 = f32[96,768]{1,0:T(8,128)} custom-call(f32[96,128]{1,0:T(8,128)S(1)} %get-tuple-element.56.spot_ref, bf16[768,768]{1,0:T(8,128)(2,1)S(1)} %shard_map.112.onto_ref, f32[1,1]{1,0:T(1,128)S(1)} %get-tuple-element.57.energy_ref, f32[1,1]{1,0:T(1,128)} %get-tuple-element.58.spread_ref, f32[96,256]{1,0:T(8,128)S(1)} %get-tuple-element.59.initial_ref, ...), custom_call_target="tpu_custom_call" | custom-call | tf_op jit(solution)/shard_map/pallas_call | solution.py:359
  101.4 2.6 %shard_map.116 = f32[768,768]{1,0:T(8,128)} custom-call(s32[1]{0:T(128)} %bitcast.1.segment_ref, f32[768,768]{1,0:T(8,128)} %bitcast.20, f32[768,768]{1,0:T(8,128)S(1)} %collective-permute-done.23.shifted_ref), custom_call_target="tpu_custom_call" | custom-call | tf_op jit(solution)/shard_map/pallas_call | solution.py:495
  (22 shorter events, 0.1 us)
Async XLA Ops:
  0.6 32.6 %copy-start = (f32[1,768,768]{2,1,0:T(8,128)S(1)}, f32[1,768,768]{2,1,0:T(8,128)}, u32[]{:S(2)}) copy-start(f32[1,768,768]{2,1,0:T(8,128)} %param.11) | copy-start | bytes 7077892
  2.5 9.0 %collective-permute-start = (f32[96,256]{1,0:T(8,128)S(1)}, f32[96,256]{1,0:T(8,128)S(1)}, u32[]{:S(2)}, u32[]{:S(2)}) collective-permute-start(f32[96,256]{1,0:T(8,128)S(1)} %shard_map.104.first_ref), channel_id=1, source_target_pairs={{0,4},{1,5},{2,6},{3,7},{4,0},{5,1},{6,2},{7,3},{8,12},{9,13},{10,... | collective-permute-start | bytes 294920 | tf_op jit(solution)/shard_map/ppermute | solution.py:355
  11.5 16.7 %collective-permute-start.1 = (f32[192,256]{1,0:T(8,128)S(1)}, f32[192,256]{1,0:T(8,128)S(1)}, u32[]{:S(2)}, u32[]{:S(2)}) collective-permute-start(f32[192,256]{1,0:T(8,128)S(1)} %shard_map.105.refs_0_), channel_id=1, source_target_pairs={{0,1},{1,0},{2,3},{3,2},{4,5},{5,4},{6,7},{7,6},{8,9},{9,8},{10,11... | collective-permute-start | bytes 589832 | tf_op jit(solution)/shard_map/ppermute | solution.py:355
  13.2 15.1 %collective-permute-start.2 = (f32[192,256]{1,0:T(8,128)S(1)}, f32[192,256]{1,0:T(8,128)S(1)}, u32[]{:S(2)}, u32[]{:S(2)}) collective-permute-start(f32[192,256]{1,0:T(8,128)S(1)} %shard_map.105.refs_0_), channel_id=1, source_target_pairs={{0,2},{1,3},{2,0},{3,1},{4,6},{5,7},{6,4},{7,5},{8,10},{9,11},{10,... | collective-permute-start | bytes 589832 | tf_op jit(solution)/shard_map/ppermute | solution.py:355
  13.8 14.5 %collective-permute-start.3 = (f32[192,256]{1,0:T(8,128)S(1)}, f32[192,256]{1,0:T(8,128)S(1)}, u32[]{:S(2)}, u32[]{:S(2)}) collective-permute-start(f32[192,256]{1,0:T(8,128)S(1)} %shard_map.105.refs_0_), channel_id=1, source_target_pairs={{0,3},{1,2},{2,1},{3,0},{4,7},{5,6},{6,5},{7,4},{8,11},{9,10},{10,... | collective-permute-start | bytes 589832 | tf_op jit(solution)/shard_map/ppermute | solution.py:355
  20.2 8.1 %copy-start.1 = (f32[16]{0:T(128)S(1)}, f32[16]{0:T(128)}, u32[]{:S(2)}) copy-start(f32[16]{0:T(128)} %table_ref.3) | copy-start | bytes 196
  28.3 4.9 %copy-start.2 = (f32[1,1,768,768]{3,2,1,0:T(8,128)S(1)}, f32[1,1,768,768]{3,2,1,0:T(8,128)}, u32[]{:S(2)}) copy-start(f32[1,1,768,768]{3,2,1,0:T(8,128)} %param.8) | copy-start | bytes 7077892
  39.9 61.5 %collective-permute-start.23 = (f32[768,768]{1,0:T(8,128)S(1)}, f32[768,768]{1,0:T(8,128)S(1)}, u32[]{:S(2)}, u32[]{:S(2)}) collective-permute-start(f32[768,768]{1,0:T(8,128)S(1)} %fusion.4), channel_id=1, source_target_pairs={{0,8},{8,16},{16,24},{1,9},{9,17},{17,25},{2,10},{10,18},{18,26},{... | collective-permute-start | bytes 7077896 | tf_op jit(solution)/shard_map/ppermute | solution.py:342
  41.6 7.7 %collective-permute-start.4 = (f32[192,256]{1,0:T(8,128)S(1)}, f32[192,256]{1,0:T(8,128)S(1)}, u32[]{:S(2)}, u32[]{:S(2)}) collective-permute-start(f32[192,256]{1,0:T(8,128)S(1)} %get-tuple-element.50), channel_id=1, source_target_pairs={{0,3},{1,2},{2,1},{3,0},{4,7},{5,6},{6,5},{7,4},{8,11},{9,10},{10,... | collective-permute-start | bytes 589832 | tf_op jit(solution)/shard_map/ppermute | solution.py:355
  43.3 10.2 %collective-permute-start.5 = (f32[192,256]{1,0:T(8,128)S(1)}, f32[192,256]{1,0:T(8,128)S(1)}, u32[]{:S(2)}, u32[]{:S(2)}) collective-permute-start(f32[192,256]{1,0:T(8,128)S(1)} %get-tuple-element.51), channel_id=1, source_target_pairs={{0,2},{1,3},{2,0},{3,1},{4,6},{5,7},{6,4},{7,5},{8,10},{9,11},{10,... | collective-permute-start | bytes 589832 | tf_op jit(solution)/shard_map/ppermute | solution.py:355
  44.6 9.8 %collective-permute-start.6 = (f32[192,256]{1,0:T(8,128)S(1)}, f32[192,256]{1,0:T(8,128)S(1)}, u32[]{:S(2)}, u32[]{:S(2)}) collective-permute-start(f32[192,256]{1,0:T(8,128)S(1)} %get-tuple-element.52), channel_id=1, source_target_pairs={{0,1},{1,0},{2,3},{3,2},{4,5},{5,4},{6,7},{7,6},{8,9},{9,8},{10,11... | collective-permute-start | bytes 589832 | tf_op jit(solution)/shard_map/ppermute | solution.py:355
  54.5 10.8 %collective-permute-start.7 = (f32[192,128]{1,0:T(8,128)S(1)}, f32[192,128]{1,0:T(8,128)S(1)}, u32[]{:S(2)}, u32[]{:S(2)}) collective-permute-start(f32[192,128]{1,0:T(8,128)S(1)} %get-tuple-element.53.refs_0_), channel_id=1, source_target_pairs={{0,4},{1,5},{2,6},{3,7},{4,0},{5,1},{6,2},{7,3},{8,12},{9,13},{10,... | collective-permute-start | bytes 294920 | tf_op jit(solution)/shard_map/ppermute | solution.py:355
  56.8 12.2 %collective-permute-start.11 = (f32[192,128]{1,0:T(8,128)S(1)}, f32[192,128]{1,0:T(8,128)S(1)}, u32[]{:S(2)}, u32[]{:S(2)}) collective-permute-start(f32[192,128]{1,0:T(8,128)S(1)} %get-tuple-element.54.refs_0_), channel_id=1, source_target_pairs={{0,4},{1,5},{2,6},{3,7},{4,0},{5,1},{6,2},{7,3},{8,12},{9,13},{10,... | collective-permute-start | bytes 294920 | tf_op jit(solution)/shard_map/ppermute | solution.py:355
  65.4 6.6 %collective-permute-start.8 = (f32[192,128]{1,0:T(8,128)S(1)}, f32[192,128]{1,0:T(8,128)S(1)}, u32[]{:S(2)}, u32[]{:S(2)}) collective-permute-start(f32[192,128]{1,0:T(8,128)S(1)} %shard_map.109.refs_0_), channel_id=1, source_target_pairs={{0,1},{1,0},{2,3},{3,2},{4,5},{5,4},{6,7},{7,6},{8,9},{9,8},{10,11... | collective-permute-start | bytes 294920 | tf_op jit(solution)/shard_map/ppermute | solution.py:355
  67.0 5.7 %collective-permute-start.9 = (f32[192,128]{1,0:T(8,128)S(1)}, f32[192,128]{1,0:T(8,128)S(1)}, u32[]{:S(2)}, u32[]{:S(2)}) collective-permute-start(f32[192,128]{1,0:T(8,128)S(1)} %shard_map.109.refs_0_), channel_id=1, source_target_pairs={{0,2},{1,3},{2,0},{3,1},{4,6},{5,7},{6,4},{7,5},{8,10},{9,11},{10,... | collective-permute-start | bytes 294920 | tf_op jit(solution)/shard_map/ppermute | solution.py:355
  67.0 7.8 %collective-permute-start.10 = (f32[192,128]{1,0:T(8,128)S(1)}, f32[192,128]{1,0:T(8,128)S(1)}, u32[]{:S(2)}, u32[]{:S(2)}) collective-permute-start(f32[192,128]{1,0:T(8,128)S(1)} %shard_map.109.refs_0_), channel_id=1, source_target_pairs={{0,3},{1,2},{2,1},{3,0},{4,7},{5,6},{6,5},{7,4},{8,11},{9,10},{10,... | collective-permute-start | bytes 294920 | tf_op jit(solution)/shard_map/ppermute | solution.py:355
  69.0 6.6 %collective-permute-start.12 = (f32[192,128]{1,0:T(8,128)S(1)}, f32[192,128]{1,0:T(8,128)S(1)}, u32[]{:S(2)}, u32[]{:S(2)}) collective-permute-start(f32[192,128]{1,0:T(8,128)S(1)} %shard_map.110.refs_4_), channel_id=1, source_target_pairs={{0,1},{1,0},{2,3},{3,2},{4,5},{5,4},{6,7},{7,6},{8,9},{9,8},{10,11... | collective-permute-start | bytes 294920 | tf_op jit(solution)/shard_map/ppermute | solution.py:355
  72.0 4.6 %collective-permute-start.13 = (f32[192,128]{1,0:T(8,128)S(1)}, f32[192,128]{1,0:T(8,128)S(1)}, u32[]{:S(2)}, u32[]{:S(2)}) collective-permute-start(f32[192,128]{1,0:T(8,128)S(1)} %shard_map.110.refs_4_), channel_id=1, source_target_pairs={{0,2},{1,3},{2,0},{3,1},{4,6},{5,7},{6,4},{7,5},{8,10},{9,11},{10,... | collective-permute-start | bytes 294920 | tf_op jit(solution)/shard_map/ppermute | solution.py:355
  72.6 5.8 %collective-permute-start.14 = (f32[192,128]{1,0:T(8,128)S(1)}, f32[192,128]{1,0:T(8,128)S(1)}, u32[]{:S(2)}, u32[]{:S(2)}) collective-permute-start(f32[192,128]{1,0:T(8,128)S(1)} %shard_map.110.refs_4_), channel_id=1, source_target_pairs={{0,3},{1,2},{2,1},{3,0},{4,7},{5,6},{6,5},{7,4},{8,11},{9,10},{10,... | collective-permute-start | bytes 294920 | tf_op jit(solution)/shard_map/ppermute | solution.py:355
  83.1 6.4 %collective-permute-start.15 = (f32[192,128]{1,0:T(8,128)S(1)}, f32[192,128]{1,0:T(8,128)S(1)}, u32[]{:S(2)}, u32[]{:S(2)}) collective-permute-start(f32[192,128]{1,0:T(8,128)S(1)} %get-tuple-element.62), channel_id=1, source_target_pairs={{0,3},{1,2},{2,1},{3,0},{4,7},{5,6},{6,5},{7,4},{8,11},{9,10},{10,... | collective-permute-start | bytes 294920 | tf_op jit(solution)/shard_map/ppermute | solution.py:355
  85.0 4.8 %collective-permute-start.16 = (f32[192,128]{1,0:T(8,128)S(1)}, f32[192,128]{1,0:T(8,128)S(1)}, u32[]{:S(2)}, u32[]{:S(2)}) collective-permute-start(f32[192,128]{1,0:T(8,128)S(1)} %get-tuple-element.63), channel_id=1, source_target_pairs={{0,2},{1,3},{2,0},{3,1},{4,6},{5,7},{6,4},{7,5},{8,10},{9,11},{10,... | collective-permute-start | bytes 294920 | tf_op jit(solution)/shard_map/ppermute | solution.py:355
  85.3 5.9 %collective-permute-start.17 = (f32[192,128]{1,0:T(8,128)S(1)}, f32[192,128]{1,0:T(8,128)S(1)}, u32[]{:S(2)}, u32[]{:S(2)}) collective-permute-start(f32[192,128]{1,0:T(8,128)S(1)} %get-tuple-element.64), channel_id=1, source_target_pairs={{0,1},{1,0},{2,3},{3,2},{4,5},{5,4},{6,7},{7,6},{8,9},{9,8},{10,11... | collective-permute-start | bytes 294920 | tf_op jit(solution)/shard_map/ppermute | solution.py:355
  86.6 6.4 %collective-permute-start.18 = (f32[192,128]{1,0:T(8,128)S(1)}, f32[192,128]{1,0:T(8,128)S(1)}, u32[]{:S(2)}, u32[]{:S(2)}) collective-permute-start(f32[192,128]{1,0:T(8,128)S(1)} %get-tuple-element.67), channel_id=1, source_target_pairs={{0,3},{1,2},{2,1},{3,0},{4,7},{5,6},{6,5},{7,4},{8,11},{9,10},{10,... | collective-permute-start | bytes 294920 | tf_op jit(solution)/shard_map/ppermute | solution.py:355
  89.5 4.6 %collective-permute-start.19 = (f32[192,128]{1,0:T(8,128)S(1)}, f32[192,128]{1,0:T(8,128)S(1)}, u32[]{:S(2)}, u32[]{:S(2)}) collective-permute-start(f32[192,128]{1,0:T(8,128)S(1)} %get-tuple-element.68), channel_id=1, source_target_pairs={{0,2},{1,3},{2,0},{3,1},{4,6},{5,7},{6,4},{7,5},{8,10},{9,11},{10,... | collective-permute-start | bytes 294920 | tf_op jit(solution)/shard_map/ppermute | solution.py:355
  89.8 4.6 %collective-permute-start.20 = (f32[192,128]{1,0:T(8,128)S(1)}, f32[192,128]{1,0:T(8,128)S(1)}, u32[]{:S(2)}, u32[]{:S(2)}) collective-permute-start(f32[192,128]{1,0:T(8,128)S(1)} %get-tuple-element.69), channel_id=1, source_target_pairs={{0,1},{1,0},{2,3},{3,2},{4,5},{5,4},{6,7},{7,6},{8,9},{9,8},{10,11... | collective-permute-start | bytes 294920 | tf_op jit(solution)/shard_map/ppermute | solution.py:355
  91.2 6.7 %collective-permute-start.21 = (f32[96,128]{1,0:T(8,128)S(1)}, f32[96,128]{1,0:T(8,128)S(1)}, u32[]{:S(2)}, u32[]{:S(2)}) collective-permute-start(f32[96,128]{1,0:T(8,128)S(1)} %get-tuple-element.71), channel_id=1, source_target_pairs={{0,4},{1,5},{2,6},{3,7},{4,0},{5,1},{6,2},{7,3},{8,12},{9,13},{10,... | collective-permute-start | bytes 147464 | tf_op jit(solution)/shard_map/ppermute | solution.py:355
  94.5 5.1 %collective-permute-start.22 = (f32[96,128]{1,0:T(8,128)S(1)}, f32[96,128]{1,0:T(8,128)S(1)}, u32[]{:S(2)}, u32[]{:S(2)}) collective-permute-start(f32[96,128]{1,0:T(8,128)S(1)} %get-tuple-element.72), channel_id=1, source_target_pairs={{0,4},{1,5},{2,6},{3,7},{4,0},{5,1},{6,2},{7,3},{8,12},{9,13},{10,... | collective-permute-start | bytes 147464 | tf_op jit(solution)/shard_map/ppermute | solution.py:355
